TPU v7x, 256 devices: a whole 4x4x8 slice. The times are simulated.
256 devices in a mesh: ctx: 128 (over x, y, z), kv: 2 (over core).
Axes of the slice: x: 4, y: 4, z: 8, core: 2. Of those that a mesh axis runs over, the one named last changes fastest.
Arguments:
- query_raw: bfloat16 [16384, 32, 128], P('ctx', 'kv')
- key_raw: bfloat16 [16384, 16, 128], P('ctx', 'kv')
- value_matrix: bfloat16 [16384, 16, 128], P('ctx', 'kv'), may hold values from -6 to 6
- query_gain: float32 [128], replicated, may hold values from 0.5 to 6
- key_gain: float32 [128], replicated, may hold values from 0.5 to 6
- doc_ids: int32 [16384], replicated, may hold values from 0 to 63, never falling along the last dimension, each value on 1 to 2048 neighbouring positions
- output_gradient: bfloat16 [16384, 32, 128], P('ctx', 'kv')
Outputs:
- query_grad: bfloat16 [16384, 32, 128], P('ctx', 'kv')
- key_grad: bfloat16 [16384, 16, 128], P('ctx', 'kv')
- value_grad: bfloat16 [16384, 16, 128], P('ctx', 'kv')
- query_gain_grad: float32 [128], replicated
- key_gain_grad: float32 [128], replicated
Inputs may be any that keep to these rules, and one draw needn't show every extreme that they name: `doc_ids`: file numbers never fall along the sequence; every file has 1 to 2048 tokens and one has exactly 2048.
All inputs are finite; a program needn't handle non-finite values.
Results may differ from a plain program's by a relative error of at most 0.035.
The roundings to bfloat16 on the way count: a program that leaves them out, or rounds other values in their place, can miss the bound.
Values may be sent and summed in bfloat16 or wider, within the bound.
No kernel may reach another device: no remote copies, remote signals or barrier semaphores. Data moves between devices by JAX's collectives and lax.ppermute only.
A program may use at most 128 MiB of HBM per device.

v0:
```python
import jax
import jax.numpy as jnp
from jax import lax
from jax.sharding import PartitionSpec as P

LOOKBACK_SPAN = 1024


epsilon = 1e-06
score_scale = 168.0 ** (-0.5)
masked_score = -1e30


def passed_along(value, axis, steps):
    count = lax.axis_size(axis)
    first, last = (max(0, -steps), min(count, count - steps))
    return lax.ppermute(value, axis, [(source, source + steps) for source in range(first, last)])


def normalize(raw_rows, gain_values):
    widened = raw_rows.astype(jnp.float32)
    inverse = lax.rsqrt(jnp.mean(widened * widened, axis=-1, keepdims=True) + epsilon)
    unit_rows = widened * inverse
    return ((unit_rows * gain_values).astype(jnp.bfloat16), unit_rows, inverse)


def normalize_back(normed_grad, unit_rows, inverse, gain_values):
    scaled = normed_grad * gain_values
    return inverse * (scaled - unit_rows * jnp.mean(scaled * unit_rows, axis=-1, keepdims=True))


def tile_mask(doc_padded, first_row_index, key_start, block_rows):
    query_pos = first_row_index + jnp.arange(block_rows, dtype=jnp.int32)
    key_pos = key_start + jnp.arange(block_rows, dtype=jnp.int32)
    query_doc = lax.dynamic_slice_in_dim(doc_padded, first_row_index + LOOKBACK_SPAN, block_rows, 0)
    key_doc = lax.dynamic_slice_in_dim(doc_padded, key_start + LOOKBACK_SPAN, block_rows, 0)
    before = query_pos[:, None] - key_pos[None, :]
    return (
        (before >= 0)
        & (before < LOOKBACK_SPAN)
        & (key_pos[None, :] >= 0)
        & (query_doc[:, None] == key_doc[None, :])
    )


def tile_scores(query_four, key_tile, allowed):
    scores = (
        jnp.einsum("tgjd,sgd->gjts", query_four, key_tile, preferred_element_type=jnp.float32)
        * score_scale
    )
    return jnp.where(allowed, scores, masked_score)


def per_device(query_raw, key_raw, value_matrix, query_gain, key_gain, doc_ids, output_gradient):
    block_rows = query_raw.shape[0]
    kv_heads = key_raw.shape[1]
    query_group_width = query_raw.shape[1] // kv_heads
    head_width = query_raw.shape[2]
    reach_blocks = LOOKBACK_SPAN // block_rows
    first_row_index = lax.axis_index("ctx") * block_rows
    doc_padded = jnp.concatenate([jnp.full((LOOKBACK_SPAN,), -1, jnp.int32), doc_ids])
    query_matrix, query_unit, query_inv = normalize(query_raw, query_gain)
    key_matrix, key_unit, key_inv = normalize(key_raw, key_gain)
    query_four = query_matrix.reshape(block_rows, kv_heads, query_group_width, head_width)
    grad_four = output_gradient.reshape(block_rows, kv_heads, query_group_width, head_width)
    key_tiles = [key_matrix]
    value_tiles = [value_matrix]
    for offset in range(1, reach_blocks + 1):
        got_keys, got_values = passed_along((key_matrix, value_matrix), "ctx", offset)
        key_tiles.append(got_keys)
        value_tiles.append(got_values)
    tile_masks = [
        tile_mask(doc_padded, first_row_index, first_row_index - offset * block_rows, block_rows)
        for offset in range(reach_blocks + 1)
    ]
    stat_shape = (kv_heads, query_group_width, block_rows, 1)
    score_tiles = []
    for offset in range(reach_blocks + 1):
        score_tiles.append(tile_scores(query_four, key_tiles[offset], tile_masks[offset]))
    peak_score = jnp.full(stat_shape, masked_score, jnp.float32)
    exp_total = jnp.zeros(stat_shape, jnp.float32)
    for offset in range(reach_blocks + 1):
        scores = score_tiles[offset]
        new_peak = jnp.maximum(peak_score, jnp.max(scores, axis=-1, keepdims=True))
        rescaled = exp_total * jnp.exp(peak_score - new_peak)
        peak_score = new_peak
        exp_total = rescaled + jnp.sum(jnp.exp(scores - new_peak), axis=-1, keepdims=True)
    log_total = peak_score + jnp.log(exp_total)
    out_total = jnp.zeros((kv_heads, query_group_width, block_rows, head_width), jnp.float32)
    attend_tiles = []
    for offset in range(reach_blocks + 1):
        attend = jnp.exp(score_tiles[offset] - log_total).astype(jnp.bfloat16)
        attend, out_total = (
            attend,
            out_total
            + jnp.einsum(
                "gjts,sgd->gjtd", attend, value_tiles[offset], preferred_element_type=jnp.float32
            ),
        )
        attend_tiles.append(attend)
    out_rows = out_total.astype(jnp.bfloat16)
    row_dots = jnp.einsum("tgjd,gjtd->gjt", grad_four, out_rows, preferred_element_type=jnp.float32)
    query_total = jnp.zeros((block_rows, kv_heads, query_group_width, head_width), jnp.float32)
    key_parts = []
    value_parts = []
    for offset in range(reach_blocks + 1):
        tile_attend = attend_tiles[offset]
        prob_grad = jnp.einsum(
            "tgjd,sgd->gjts", grad_four, value_tiles[offset], preferred_element_type=jnp.float32
        )
        score_grad = (tile_attend.astype(jnp.float32) * (prob_grad - row_dots[..., None])).astype(
            jnp.bfloat16
        )
        query_term = jnp.einsum(
            "gjts,sgd->tgjd", score_grad, key_tiles[offset], preferred_element_type=jnp.float32
        )
        key_term = (
            jnp.einsum("gjts,tgjd->sgd", score_grad, query_four, preferred_element_type=jnp.float32)
            * score_scale
        )
        value_term = jnp.einsum(
            "gjts,tgjd->sgd", tile_attend, grad_four, preferred_element_type=jnp.float32
        )
        query_term, key_term, value_term = (query_term, key_term, value_term)
        query_total = query_total + query_term
        key_parts.append(key_term)
        value_parts.append(value_term)
    key_normed_grad = key_parts[0]
    value_total = value_parts[0]
    for offset in range(1, reach_blocks + 1):
        got_keys, got_values = (
            passed_along(key_parts[offset].astype(jnp.bfloat16), "ctx", -offset).astype(
                jnp.float32
            ),
            passed_along(value_parts[offset].astype(jnp.bfloat16), "ctx", -offset).astype(
                jnp.float32
            ),
        )
        key_normed_grad = key_normed_grad + got_keys
        value_total = value_total + got_values
    query_normed_grad = (
        query_total.reshape(block_rows, kv_heads * query_group_width, head_width) * score_scale
    )
    query_term_sum = jnp.sum(query_normed_grad * query_unit, axis=(0, 1))
    key_term_sum = jnp.sum(key_normed_grad * key_unit, axis=(0, 1))
    query_sum, key_sum = lax.psum((query_term_sum, key_term_sum), ("ctx", "kv"))
    seq_length = doc_ids.shape[0]
    query_grad = normalize_back(query_normed_grad, query_unit, query_inv, query_gain).astype(
        jnp.bfloat16
    )
    key_grad = normalize_back(key_normed_grad, key_unit, key_inv, key_gain).astype(jnp.bfloat16)
    return (
        query_grad,
        key_grad,
        value_total.astype(jnp.bfloat16),
        query_sum / seq_length,
        key_sum / seq_length,
    )


def solution(mesh):
    return jax.shard_map(
        per_device,
        mesh=mesh,
        in_specs=(
            P("ctx", "kv", None),
            P("ctx", "kv", None),
            P("ctx", "kv", None),
            P(),
            P(),
            P(),
            P("ctx", "kv", None),
        ),
        out_specs=(P("ctx", "kv", None), P("ctx", "kv", None), P("ctx", "kv", None), P(), P()),
        check_vma=False,
    )
```

profile of v0, /device:TPU:2, one launch (start us, length us, event | category | flops | bytes accessed | tf_op | source)
XLA Modules:
  0.0 344.8 jit_solution(15465120343574554280)
XLA Ops:
  0.7 1.2 fusion.122
  2.8 8.2 %collective-permute-start.5 = (bf16[128,8,128]{2,0,1:T(8,128)(2,1)S(1)}, bf16[128,8,128]{2,0,1:T(8,128)(2,1)S(1)}, u32[]{:S(2)}, u32[]{:S(2)}) collective-permute-start(bf16[128,8,128]{2,0,1:T(8,128)(2,1)S(1)} %fusion.116), channel_id=1, source_target_pairs={{0,12},{2,14},{4,16},{6,18},{8,20},{10,22},{12,24},{14,26},{16,28}... | collective-permute-start | bytes 786440 | tf_op jit(solution)/shard_map/ppermute | solution.py:17
  11.0 3.9 %collective-permute-start.4 = (bf16[128,8,128]{2,0,1:T(8,128)(2,1)S(1)}, bf16[128,8,128]{2,0,1:T(8,128)(2,1)S(1)}, u32[]{:S(2)}, u32[]{:S(2)}) collective-permute-start(bf16[128,8,128]{2,0,1:T(8,128)(2,1)S(1)} %fusion.116), channel_id=1, source_target_pairs={{0,10},{2,12},{4,14},{6,16},{8,18},{10,20},{12,22},{14,24},{16,26}... | collective-permute-start | bytes 786440 | tf_op jit(solution)/shard_map/ppermute | solution.py:17
  14.9 6.4 %collective-permute-start.3 = (bf16[128,8,128]{2,0,1:T(8,128)(2,1)S(1)}, bf16[128,8,128]{2,0,1:T(8,128)(2,1)S(1)}, u32[]{:S(2)}, u32[]{:S(2)}) collective-permute-start(bf16[128,8,128]{2,0,1:T(8,128)(2,1)S(1)} %fusion.116), channel_id=1, source_target_pairs={{0,8},{2,10},{4,12},{6,14},{8,16},{10,18},{12,20},{14,22},{16,24},... | collective-permute-start | bytes 786440 | tf_op jit(solution)/shard_map/ppermute | solution.py:17
  21.3 1.9 collective-permute-start.2
  23.2 3.5 %collective-permute-start.7 = (bf16[128,8,128]{2,0,1:T(8,128)(2,1)S(1)}, bf16[128,8,128]{2,0,1:T(8,128)(2,1)S(1)}, u32[]{:S(2)}, u32[]{:S(2)}) collective-permute-start(bf16[128,8,128]{2,0,1:T(8,128)(2,1)S(1)} %fusion.116), channel_id=1, source_target_pairs={{0,16},{2,18},{4,20},{6,22},{8,24},{10,26},{12,28},{14,30},{16,32}... | collective-permute-start | bytes 786440 | tf_op jit(solution)/shard_map/ppermute | solution.py:17
  31.1 3.6 %collective-permute-start.6 = (bf16[128,8,128]{2,0,1:T(8,128)(2,1)S(1)}, bf16[128,8,128]{2,0,1:T(8,128)(2,1)S(1)}, u32[]{:S(2)}, u32[]{:S(2)}) collective-permute-start(bf16[128,8,128]{2,0,1:T(8,128)(2,1)S(1)} %fusion.116), channel_id=1, source_target_pairs={{0,14},{2,16},{4,18},{6,20},{8,22},{10,24},{12,26},{14,28},{16,30}... | collective-permute-start | bytes 786440 | tf_op jit(solution)/shard_map/ppermute | solution.py:17
  35.1 15.6 %collective-permute-done.4 = bf16[128,8,128]{2,0,1:T(8,128)(2,1)S(1)} collective-permute-done((bf16[128,8,128]{2,0,1:T(8,128)(2,1)S(1)}, bf16[128,8,128]{2,0,1:T(8,128)(2,1)S(1)}, u32[]{:S(2)}, u32[]{:S(2)}) %collective-permute-start.4) | collective-permute-done | bytes 262176 | tf_op jit(solution)/shard_map/ppermute | solution.py:17
  50.7 1.9 collective-permute-start
  52.9 2.8 collective-permute-start.1
  56.1 8.7 %collective-permute-start.8 = (bf16[128,8,128]{2,0,1:T(8,128)(2,1)}, bf16[128,8,128]{2,0,1:T(8,128)(2,1)S(1)}, u32[]{:S(2)}, u32[]{:S(2)}) collective-permute-start(bf16[128,8,128]{2,0,1:T(8,128)(2,1)} %copy.236), channel_id=1, source_target_pairs={{0,2},{2,4},{4,6},{6,8},{8,10},{10,12},{12,14},{14,16},{16,18},{18... | collective-permute-start | bytes 786440 | tf_op jit(solution)/shard_map/ppermute | solution.py:17
  65.2 1.9 collective-permute-start.15
  67.4 4.8 %collective-permute-start.14 = (bf16[128,8,128]{2,0,1:T(8,128)(2,1)}, bf16[128,8,128]{2,0,1:T(8,128)(2,1)S(1)}, u32[]{:S(2)}, u32[]{:S(2)}) collective-permute-start(bf16[128,8,128]{2,0,1:T(8,128)(2,1)} %copy.236), channel_id=1, source_target_pairs={{0,14},{2,16},{4,18},{6,20},{8,22},{10,24},{12,26},{14,28},{16,30}... | collective-permute-start | bytes 786440 | tf_op jit(solution)/shard_map/ppermute | solution.py:17
  72.6 3.4 collective-permute-start.13
  76.3 5.1 %collective-permute-start.12 = (bf16[128,8,128]{2,0,1:T(8,128)(2,1)}, bf16[128,8,128]{2,0,1:T(8,128)(2,1)S(1)}, u32[]{:S(2)}, u32[]{:S(2)}) collective-permute-start(bf16[128,8,128]{2,0,1:T(8,128)(2,1)} %copy.236), channel_id=1, source_target_pairs={{0,10},{2,12},{4,14},{6,16},{8,18},{10,20},{12,22},{14,24},{16,26}... | collective-permute-start | bytes 786440 | tf_op jit(solution)/shard_map/ppermute | solution.py:17
  83.5 1.4 exponential_convert_fusion.6
  85.3 7.5 %collective-permute-done.15 = bf16[128,8,128]{2,0,1:T(8,128)(2,1)S(1)} collective-permute-done((bf16[128,8,128]{2,0,1:T(8,128)(2,1)}, bf16[128,8,128]{2,0,1:T(8,128)(2,1)S(1)}, u32[]{:S(2)}, u32[]{:S(2)}) %collective-permute-start.15) | collective-permute-done | bytes 262176 | tf_op jit(solution)/shard_map/ppermute | solution.py:17
  92.8 1.9 collective-permute-start.11
  95.1 1.9 collective-permute-start.10
  97.4 3.3 collective-permute-done.13
  100.7 2.1 collective-permute-start.9
  103.2 8.3 %collective-permute-done.12 = bf16[128,8,128]{2,0,1:T(8,128)(2,1)S(1)} collective-permute-done((bf16[128,8,128]{2,0,1:T(8,128)(2,1)}, bf16[128,8,128]{2,0,1:T(8,128)(2,1)S(1)}, u32[]{:S(2)}, u32[]{:S(2)}) %collective-permute-start.12) | collective-permute-done | bytes 262176 | tf_op jit(solution)/shard_map/ppermute | solution.py:17
  112.2 9.5 %collective-permute-done.10 = bf16[128,8,128]{2,0,1:T(8,128)(2,1)S(1)} collective-permute-done((bf16[128,8,128]{2,0,1:T(8,128)(2,1)}, bf16[128,8,128]{2,0,1:T(8,128)(2,1)S(1)}, u32[]{:S(2)}, u32[]{:S(2)}) %collective-permute-start.10) | collective-permute-done | bytes 262176 | tf_op jit(solution)/shard_map/ppermute | solution.py:17
  124.5 1.0 fusion.94
  126.2 1.0 fusion.93
  127.3 1.0 fusion.95
  128.3 6.1 %collective-permute-done.9 = bf16[128,8,128]{2,0,1:T(8,128)(2,1)S(1)} collective-permute-done((bf16[128,8,128]{2,0,1:T(8,128)(2,1)}, bf16[128,8,128]{2,0,1:T(8,128)(2,1)S(1)}, u32[]{:S(2)}, u32[]{:S(2)}) %collective-permute-start.9) | collective-permute-done | bytes 262176 | tf_op jit(solution)/shard_map/ppermute | solution.py:17
  135.1 2.2 multiply_reduce_fusion
  137.3 1.2 copy.351
  138.5 1.5 fusion.52
  140.4 1.0 fusion.98
  141.5 5.3 %collective-permute-start.17 = (bf16[128,8,128]{2,0,1:T(8,128)(2,1)}, bf16[128,8,128]{2,0,1:T(8,128)(2,1)}, u32[]{:S(2)}, u32[]{:S(2)}) collective-permute-start(bf16[128,8,128]{2,0,1:T(8,128)(2,1)} %fusion.98), channel_id=1, source_target_pairs={{4,0},{6,2},{8,4},{10,6},{12,8},{14,10},{16,12},{18,14},{20,16},{2... | collective-permute-start | bytes 786440 | tf_op jit(solution)/shard_map/ppermute | solution.py:17
  147.2 1.0 fusion.97
  148.2 1.9 collective-permute-start.16
  151.4 3.7 %collective-permute-start.18 = (bf16[128,8,128]{2,0,1:T(8,128)(2,1)}, bf16[128,8,128]{2,0,1:T(8,128)(2,1)}, u32[]{:S(2)}, u32[]{:S(2)}) collective-permute-start(bf16[128,8,128]{2,0,1:T(8,128)(2,1)} %fusion.99), channel_id=1, source_target_pairs={{6,0},{8,2},{10,4},{12,6},{14,8},{16,10},{18,12},{20,14},{22,16},{... | collective-permute-start | bytes 786440 | tf_op jit(solution)/shard_map/ppermute | solution.py:17
  155.5 1.0 fusion.100
  156.9 1.0 fusion.101
  157.9 2.1 collective-permute-start.20
  160.4 1.0 fusion.102
  161.7 1.0 fusion.103
  163.1 1.0 fusion.104
  171.7 1.6 fusion.17
  173.3 1.7 copy.278
  175.0 1.7 fusion.110
  176.8 1.4 fusion.109
  179.2 5.8 %collective-permute-start.19 = (bf16[128,8,128]{2,0,1:T(8,128)(2,1)S(1)}, bf16[128,8,128]{2,0,1:T(8,128)(2,1)S(1)}, u32[]{:S(2)}, u32[]{:S(2)}) collective-permute-start(bf16[128,8,128]{2,0,1:T(8,128)(2,1)S(1)} %copy-done.62), channel_id=1, source_target_pairs={{8,0},{10,2},{12,4},{14,6},{16,8},{18,10},{20,12},{22,14},{24,16},... | collective-permute-start | bytes 786440 | tf_op jit(solution)/shard_map/ppermute | solution.py:17
  186.0 3.9 %collective-permute-start.21 = (bf16[128,8,128]{2,0,1:T(8,128)(2,1)S(1)}, bf16[128,8,128]{2,0,1:T(8,128)(2,1)S(1)}, u32[]{:S(2)}, u32[]{:S(2)}) collective-permute-start(bf16[128,8,128]{2,0,1:T(8,128)(2,1)S(1)} %copy-done.61), channel_id=1, source_target_pairs={{12,0},{14,2},{16,4},{18,6},{20,8},{22,10},{24,12},{26,14},{28,16}... | collective-permute-start | bytes 786440 | tf_op jit(solution)/shard_map/ppermute | solution.py:17
  189.9 4.6 %collective-permute-start.22 = (bf16[128,8,128]{2,0,1:T(8,128)(2,1)S(1)}, bf16[128,8,128]{2,0,1:T(8,128)(2,1)S(1)}, u32[]{:S(2)}, u32[]{:S(2)}) collective-permute-start(bf16[128,8,128]{2,0,1:T(8,128)(2,1)S(1)} %copy-done.60), channel_id=1, source_target_pairs={{14,0},{16,2},{18,4},{20,6},{22,8},{24,10},{26,12},{28,14},{30,16}... | collective-permute-start | bytes 786440 | tf_op jit(solution)/shard_map/ppermute | solution.py:17
  194.5 2.8 collective-permute-start.23
  197.3 1.0 fusion.90
  198.3 1.0 fusion.89
  199.3 4.7 %collective-permute-start.24 = (bf16[128,8,128]{2,0,1:T(8,128)(2,1)S(1)}, bf16[128,8,128]{2,0,1:T(8,128)(2,1)}, u32[]{:S(2)}, u32[]{:S(2)}) collective-permute-start(bf16[128,8,128]{2,0,1:T(8,128)(2,1)S(1)} %copy-done.57), channel_id=1, source_target_pairs={{2,0},{4,2},{6,4},{8,6},{10,8},{12,10},{14,12},{16,14},{18,16},{20... | collective-permute-start | bytes 786440 | tf_op jit(solution)/shard_map/ppermute | solution.py:17
  204.1 5.2 %collective-permute-start.25 = (bf16[128,8,128]{2,0,1:T(8,128)(2,1)S(1)}, bf16[128,8,128]{2,0,1:T(8,128)(2,1)}, u32[]{:S(2)}, u32[]{:S(2)}) collective-permute-start(bf16[128,8,128]{2,0,1:T(8,128)(2,1)S(1)} %copy-done.58), channel_id=1, source_target_pairs={{4,0},{6,2},{8,4},{10,6},{12,8},{14,10},{16,12},{18,14},{20,16},{2... | collective-permute-start | bytes 786440 | tf_op jit(solution)/shard_map/ppermute | solution.py:17
  209.2 4.9 %collective-permute-done.21 = bf16[128,8,128]{2,0,1:T(8,128)(2,1)S(1)} collective-permute-done((bf16[128,8,128]{2,0,1:T(8,128)(2,1)S(1)}, bf16[128,8,128]{2,0,1:T(8,128)(2,1)S(1)}, u32[]{:S(2)}, u32[]{:S(2)}) %collective-permute-start.21) | collective-permute-done | bytes 262176 | tf_op jit(solution)/shard_map/ppermute | solution.py:17
  214.1 1.9 collective-permute-start.26
  216.0 5.2 %collective-permute-start.27 = (bf16[128,8,128]{2,0,1:T(8,128)(2,1)S(1)}, bf16[128,8,128]{2,0,1:T(8,128)(2,1)}, u32[]{:S(2)}, u32[]{:S(2)}) collective-permute-start(bf16[128,8,128]{2,0,1:T(8,128)(2,1)S(1)} %copy-done.55), channel_id=1, source_target_pairs={{8,0},{10,2},{12,4},{14,6},{16,8},{18,10},{20,12},{22,14},{24,16},... | collective-permute-start | bytes 786440 | tf_op jit(solution)/shard_map/ppermute | solution.py:17
  221.3 23.8 %collective-permute-start.28 = (bf16[128,8,128]{2,0,1:T(8,128)(2,1)}, bf16[128,8,128]{2,0,1:T(8,128)(2,1)}, u32[]{:S(2)}, u32[]{:S(2)}) collective-permute-start(bf16[128,8,128]{2,0,1:T(8,128)(2,1)} %fusion.92), channel_id=1, source_target_pairs={{10,0},{12,2},{14,4},{16,6},{18,8},{20,10},{22,12},{24,14},{26,16}... | collective-permute-start | bytes 786440 | tf_op jit(solution)/shard_map/ppermute | solution.py:17
  245.1 1.9 fusion.121
  246.9 70.5 %all-reduce.1 = (f32[128]{0:T(128)S(1)}, f32[128]{0:T(128)S(1)}) all-reduce(f32[128]{0:T(128)S(1)} %get-tuple-element.20, f32[128]{0:T(128)S(1)} %get-tuple-element.22), channel_id=1, replica_groups=mesh['ctx'=128,'kv'=2] {'ctx','kv'}, use_global_device_ids=true, to_apply=%region_23.24 | all-reduce | flops 256 | bytes 2048 | tf_op jit(solution)/shard_map/psum | solution.py:146
  317.4 3.9 %collective-permute-start.29 = (bf16[128,8,128]{2,0,1:T(8,128)(2,1)}, bf16[128,8,128]{2,0,1:T(8,128)(2,1)S(1)}, u32[]{:S(2)}, u32[]{:S(2)}) collective-permute-start(bf16[128,8,128]{2,0,1:T(8,128)(2,1)} %fusion.91), channel_id=1, source_target_pairs={{12,0},{14,2},{16,4},{18,6},{20,8},{22,10},{24,12},{26,14},{28,16}... | collective-permute-start | bytes 786440 | tf_op jit(solution)/shard_map/ppermute | solution.py:17
  321.3 5.4 %collective-permute-start.30 = (bf16[128,8,128]{2,0,1:T(8,128)(2,1)}, bf16[128,8,128]{2,0,1:T(8,128)(2,1)S(1)}, u32[]{:S(2)}, u32[]{:S(2)}) collective-permute-start(bf16[128,8,128]{2,0,1:T(8,128)(2,1)} %fusion.90), channel_id=1, source_target_pairs={{14,0},{16,2},{18,4},{20,6},{22,8},{24,10},{26,12},{28,14},{30,16}... | collective-permute-start | bytes 786440 | tf_op jit(solution)/shard_map/ppermute | solution.py:17
  326.7 2.2 collective-permute-start.31
  330.0 11.0 %collective-permute-done.30 = bf16[128,8,128]{2,0,1:T(8,128)(2,1)S(1)} collective-permute-done((bf16[128,8,128]{2,0,1:T(8,128)(2,1)}, bf16[128,8,128]{2,0,1:T(8,128)(2,1)S(1)}, u32[]{:S(2)}, u32[]{:S(2)}) %collective-permute-start.30) | collective-permute-done | bytes 262176 | tf_op jit(solution)/shard_map/ppermute | solution.py:17
  341.0 1.7 add_convert_fusion
  (242 shorter events, 31.9 us)
Async XLA Ops:
  0.6 26.2 %copy-start.11 = (bf16[128,16,128]{2,1,0:T(8,128)(2,1)S(1)}, bf16[128,16,128]{2,1,0:T(8,128)(2,1)}, u32[]{:S(2)}) copy-start(bf16[128,16,128]{2,1,0:T(8,128)(2,1)} %param.7) | copy-start | bytes 1572868
  2.8 28.3 %collective-permute-start.5 = (bf16[128,8,128]{2,0,1:T(8,128)(2,1)S(1)}, bf16[128,8,128]{2,0,1:T(8,128)(2,1)S(1)}, u32[]{:S(2)}, u32[]{:S(2)}) collective-permute-start(bf16[128,8,128]{2,0,1:T(8,128)(2,1)S(1)} %fusion.116), channel_id=1, source_target_pairs={{0,12},{2,14},{4,16},{6,18},{8,20},{10,22},{12,24},{14,26},{16,28}... | collective-permute-start | bytes 786440 | tf_op jit(solution)/shard_map/ppermute | solution.py:17
  11.0 39.7 %collective-permute-start.4 = (bf16[128,8,128]{2,0,1:T(8,128)(2,1)S(1)}, bf16[128,8,128]{2,0,1:T(8,128)(2,1)S(1)}, u32[]{:S(2)}, u32[]{:S(2)}) collective-permute-start(bf16[128,8,128]{2,0,1:T(8,128)(2,1)S(1)} %fusion.116), channel_id=1, source_target_pairs={{0,10},{2,12},{4,14},{6,16},{8,18},{10,20},{12,22},{14,24},{16,26}... | collective-permute-start | bytes 786440 | tf_op jit(solution)/shard_map/ppermute | solution.py:17
  14.9 38.0 %collective-permute-start.3 = (bf16[128,8,128]{2,0,1:T(8,128)(2,1)S(1)}, bf16[128,8,128]{2,0,1:T(8,128)(2,1)S(1)}, u32[]{:S(2)}, u32[]{:S(2)}) collective-permute-start(bf16[128,8,128]{2,0,1:T(8,128)(2,1)S(1)} %fusion.116), channel_id=1, source_target_pairs={{0,8},{2,10},{4,12},{6,14},{8,16},{10,18},{12,20},{14,22},{16,24},... | collective-permute-start | bytes 786440 | tf_op jit(solution)/shard_map/ppermute | solution.py:17
  21.3 34.7 %collective-permute-start.2 = (bf16[128,8,128]{2,0,1:T(8,128)(2,1)S(1)}, bf16[128,8,128]{2,0,1:T(8,128)(2,1)S(1)}, u32[]{:S(2)}, u32[]{:S(2)}) collective-permute-start(bf16[128,8,128]{2,0,1:T(8,128)(2,1)S(1)} %fusion.116), channel_id=1, source_target_pairs={{0,6},{2,8},{4,10},{6,12},{8,14},{10,16},{12,18},{14,20},{16,22},{... | collective-permute-start | bytes 786440 | tf_op jit(solution)/shard_map/ppermute | solution.py:17
  23.2 41.9 %collective-permute-start.7 = (bf16[128,8,128]{2,0,1:T(8,128)(2,1)S(1)}, bf16[128,8,128]{2,0,1:T(8,128)(2,1)S(1)}, u32[]{:S(2)}, u32[]{:S(2)}) collective-permute-start(bf16[128,8,128]{2,0,1:T(8,128)(2,1)S(1)} %fusion.116), channel_id=1, source_target_pairs={{0,16},{2,18},{4,20},{6,22},{8,24},{10,26},{12,28},{14,30},{16,32}... | collective-permute-start | bytes 786440 | tf_op jit(solution)/shard_map/ppermute | solution.py:17
  31.1 4.0 %copy-start.23 = (bf16[128,8,128]{2,0,1:T(8,128)(2,1)}, bf16[128,8,128]{2,0,1:T(8,128)(2,1)S(1)}, u32[]{:S(2)}) copy-start(bf16[128,8,128]{2,0,1:T(8,128)(2,1)S(1)} %collective-permute-done.5) | copy-start | bytes 786436
  31.1 36.3 %collective-permute-start.6 = (bf16[128,8,128]{2,0,1:T(8,128)(2,1)S(1)}, bf16[128,8,128]{2,0,1:T(8,128)(2,1)S(1)}, u32[]{:S(2)}, u32[]{:S(2)}) collective-permute-start(bf16[128,8,128]{2,0,1:T(8,128)(2,1)S(1)} %fusion.116), channel_id=1, source_target_pairs={{0,14},{2,16},{4,18},{6,20},{8,22},{10,24},{12,26},{14,28},{16,30}... | collective-permute-start | bytes 786440 | tf_op jit(solution)/shard_map/ppermute | solution.py:17
  50.7 21.9 %collective-permute-start = (bf16[128,8,128]{2,0,1:T(8,128)(2,1)S(1)}, bf16[128,8,128]{2,0,1:T(8,128)(2,1)S(1)}, u32[]{:S(2)}, u32[]{:S(2)}) collective-permute-start(bf16[128,8,128]{2,0,1:T(8,128)(2,1)S(1)} %fusion.116), channel_id=1, source_target_pairs={{0,2},{2,4},{4,6},{6,8},{8,10},{10,12},{12,14},{14,16},{16,18},{18... | collective-permute-start | bytes 786440 | tf_op jit(solution)/shard_map/ppermute | solution.py:17
  52.9 3.1 copy-start.29
  52.9 23.4 %collective-permute-start.1 = (bf16[128,8,128]{2,0,1:T(8,128)(2,1)S(1)}, bf16[128,8,128]{2,0,1:T(8,128)(2,1)S(1)}, u32[]{:S(2)}, u32[]{:S(2)}) collective-permute-start(bf16[128,8,128]{2,0,1:T(8,128)(2,1)S(1)} %fusion.116), channel_id=1, source_target_pairs={{0,4},{2,6},{4,8},{6,10},{8,12},{10,14},{12,16},{14,18},{16,20},{1... | collective-permute-start | bytes 786440 | tf_op jit(solution)/shard_map/ppermute | solution.py:17
  56.0 9.1 %copy-start.31 = (bf16[128,8,128]{2,0,1:T(8,128)(2,1)}, bf16[128,8,128]{2,0,1:T(8,128)(2,1)S(1)}, u32[]{:S(2)}) copy-start(bf16[128,8,128]{2,0,1:T(8,128)(2,1)S(1)} %collective-permute-done.2) | copy-start | bytes 786436
  56.1 66.3 %collective-permute-start.8 = (bf16[128,8,128]{2,0,1:T(8,128)(2,1)}, bf16[128,8,128]{2,0,1:T(8,128)(2,1)S(1)}, u32[]{:S(2)}, u32[]{:S(2)}) collective-permute-start(bf16[128,8,128]{2,0,1:T(8,128)(2,1)} %copy.236), channel_id=1, source_target_pairs={{0,2},{2,4},{4,6},{6,8},{8,10},{10,12},{12,14},{14,16},{16,18},{18... | collective-permute-start | bytes 786440 | tf_op jit(solution)/shard_map/ppermute | solution.py:17
  65.2 27.6 %collective-permute-start.15 = (bf16[128,8,128]{2,0,1:T(8,128)(2,1)}, bf16[128,8,128]{2,0,1:T(8,128)(2,1)S(1)}, u32[]{:S(2)}, u32[]{:S(2)}) collective-permute-start(bf16[128,8,128]{2,0,1:T(8,128)(2,1)} %copy.236), channel_id=1, source_target_pairs={{0,16},{2,18},{4,20},{6,22},{8,24},{10,26},{12,28},{14,30},{16,32}... | collective-permute-start | bytes 786440 | tf_op jit(solution)/shard_map/ppermute | solution.py:17
  67.4 5.1 %copy-start.33 = (bf16[128,8,128]{2,0,1:T(8,128)(2,1)}, bf16[128,8,128]{2,0,1:T(8,128)(2,1)S(1)}, u32[]{:S(2)}) copy-start(bf16[128,8,128]{2,0,1:T(8,128)(2,1)S(1)} %collective-permute-done.6) | copy-start | bytes 786436
  67.4 27.7 %collective-permute-start.14 = (bf16[128,8,128]{2,0,1:T(8,128)(2,1)}, bf16[128,8,128]{2,0,1:T(8,128)(2,1)S(1)}, u32[]{:S(2)}, u32[]{:S(2)}) collective-permute-start(bf16[128,8,128]{2,0,1:T(8,128)(2,1)} %copy.236), channel_id=1, source_target_pairs={{0,14},{2,16},{4,18},{6,20},{8,22},{10,24},{12,26},{14,28},{16,30}... | collective-permute-start | bytes 786440 | tf_op jit(solution)/shard_map/ppermute | solution.py:17
  72.6 3.7 %copy-start.51 = (bf16[128,8,128]{2,0,1:T(8,128)(2,1)}, bf16[128,8,128]{2,0,1:T(8,128)(2,1)S(1)}, u32[]{:S(2)}) copy-start(bf16[128,8,128]{2,0,1:T(8,128)(2,1)S(1)} %collective-permute-done) | copy-start | bytes 786436
  72.6 28.1 %collective-permute-start.13 = (bf16[128,8,128]{2,0,1:T(8,128)(2,1)}, bf16[128,8,128]{2,0,1:T(8,128)(2,1)S(1)}, u32[]{:S(2)}, u32[]{:S(2)}) collective-permute-start(bf16[128,8,128]{2,0,1:T(8,128)(2,1)} %copy.236), channel_id=1, source_target_pairs={{0,12},{2,14},{4,16},{6,18},{8,20},{10,22},{12,24},{14,26},{16,28}... | collective-permute-start | bytes 786440 | tf_op jit(solution)/shard_map/ppermute | solution.py:17
  76.3 5.4 %copy-start.35 = (bf16[128,8,128]{2,0,1:T(8,128)(2,1)}, bf16[128,8,128]{2,0,1:T(8,128)(2,1)S(1)}, u32[]{:S(2)}) copy-start(bf16[128,8,128]{2,0,1:T(8,128)(2,1)S(1)} %collective-permute-done.1) | copy-start | bytes 786436
  76.3 35.2 %collective-permute-start.12 = (bf16[128,8,128]{2,0,1:T(8,128)(2,1)}, bf16[128,8,128]{2,0,1:T(8,128)(2,1)S(1)}, u32[]{:S(2)}, u32[]{:S(2)}) collective-permute-start(bf16[128,8,128]{2,0,1:T(8,128)(2,1)} %copy.236), channel_id=1, source_target_pairs={{0,10},{2,12},{4,14},{6,16},{8,18},{10,20},{12,22},{14,24},{16,26}... | collective-permute-start | bytes 786440 | tf_op jit(solution)/shard_map/ppermute | solution.py:17
  84.9 10.2 %copy-start.13 = (bf16[8,2,128,128]{2,3,1,0:T(8,128)(2,1)}, bf16[8,2,128,128]{2,3,1,0:T(8,128)(2,1)S(1)}, u32[]{:S(2)}) copy-start(bf16[8,2,128,128]{2,3,1,0:T(8,128)(2,1)S(1)} %get-tuple-element.51) | copy-start | bytes 1572868
  84.9 38.2 %copy-start.15 = (bf16[8,2,128,128]{2,3,1,0:T(8,128)(2,1)}, bf16[8,2,128,128]{2,3,1,0:T(8,128)(2,1)S(1)}, u32[]{:S(2)}) copy-start(bf16[8,2,128,128]{2,3,1,0:T(8,128)(2,1)S(1)} %get-tuple-element.44) | copy-start | bytes 1572868
  84.9 39.6 %copy-start.7 = (bf16[8,2,128,128]{2,3,1,0:T(8,128)(2,1)}, bf16[8,2,128,128]{2,3,1,0:T(8,128)(2,1)S(1)}, u32[]{:S(2)}) copy-start(bf16[8,2,128,128]{2,3,1,0:T(8,128)(2,1)S(1)} %get-tuple-element.45) | copy-start | bytes 1572868
  84.9 41.0 %copy-start.5 = (bf16[8,2,128,128]{2,3,1,0:T(8,128)(2,1)}, bf16[8,2,128,128]{2,3,1,0:T(8,128)(2,1)S(1)}, u32[]{:S(2)}) copy-start(bf16[8,2,128,128]{2,3,1,0:T(8,128)(2,1)S(1)} %get-tuple-element.46) | copy-start | bytes 1572868
  84.9 49.5 %copy-start.9 = (bf16[8,2,128,128]{2,3,1,0:T(8,128)(2,1)}, bf16[8,2,128,128]{2,3,1,0:T(8,128)(2,1)S(1)}, u32[]{:S(2)}) copy-start(bf16[8,2,128,128]{2,3,1,0:T(8,128)(2,1)S(1)} %get-tuple-element.43) | copy-start | bytes 1572868
  84.9 71.6 %copy-start.3 = (bf16[8,2,128,128]{2,3,1,0:T(8,128)(2,1)}, bf16[8,2,128,128]{2,3,1,0:T(8,128)(2,1)S(1)}, u32[]{:S(2)}) copy-start(bf16[8,2,128,128]{2,3,1,0:T(8,128)(2,1)S(1)} %get-tuple-element.47) | copy-start | bytes 1572868
  84.9 75.1 %copy-start.1 = (bf16[8,2,128,128]{2,3,1,0:T(8,128)(2,1)}, bf16[8,2,128,128]{2,3,1,0:T(8,128)(2,1)S(1)}, u32[]{:S(2)}) copy-start(bf16[8,2,128,128]{2,3,1,0:T(8,128)(2,1)S(1)} %get-tuple-element.48) | copy-start | bytes 1572868
  92.8 32.7 %collective-permute-start.11 = (bf16[128,8,128]{2,0,1:T(8,128)(2,1)}, bf16[128,8,128]{2,0,1:T(8,128)(2,1)S(1)}, u32[]{:S(2)}, u32[]{:S(2)}) collective-permute-start(bf16[128,8,128]{2,0,1:T(8,128)(2,1)} %copy.236), channel_id=1, source_target_pairs={{0,8},{2,10},{4,12},{6,14},{8,16},{10,18},{12,20},{14,22},{16,24},... | collective-permute-start | bytes 786440 | tf_op jit(solution)/shard_map/ppermute | solution.py:17
  95.1 26.5 %collective-permute-start.10 = (bf16[128,8,128]{2,0,1:T(8,128)(2,1)}, bf16[128,8,128]{2,0,1:T(8,128)(2,1)S(1)}, u32[]{:S(2)}, u32[]{:S(2)}) collective-permute-start(bf16[128,8,128]{2,0,1:T(8,128)(2,1)} %copy.236), channel_id=1, source_target_pairs={{0,6},{2,8},{4,10},{6,12},{8,14},{10,16},{12,18},{14,20},{16,22},{... | collective-permute-start | bytes 786440 | tf_op jit(solution)/shard_map/ppermute | solution.py:17
  100.7 33.7 %collective-permute-start.9 = (bf16[128,8,128]{2,0,1:T(8,128)(2,1)}, bf16[128,8,128]{2,0,1:T(8,128)(2,1)S(1)}, u32[]{:S(2)}, u32[]{:S(2)}) collective-permute-start(bf16[128,8,128]{2,0,1:T(8,128)(2,1)} %copy.236), channel_id=1, source_target_pairs={{0,4},{2,6},{4,8},{6,10},{8,12},{10,14},{12,16},{14,18},{16,20},{1... | collective-permute-start | bytes 786440 | tf_op jit(solution)/shard_map/ppermute | solution.py:17
  140.1 24.0 %copy-start.21 = (bf16[8,2,128,128]{2,3,1,0:T(8,128)(2,1)}, bf16[8,2,128,128]{2,3,1,0:T(8,128)(2,1)S(1)}, u32[]{:S(2)}) copy-start(bf16[8,2,128,128]{2,3,1,0:T(8,128)(2,1)S(1)} %fusion.52) | copy-start | bytes 1572868
  140.4 6.4 %copy-start.16 = (bf16[8,2,128,128]{2,3,1,0:T(8,128)(2,1)S(1)}, bf16[8,2,128,128]{2,3,1,0:T(8,128)(2,1)}, u32[]{:S(2)}) copy-start(bf16[8,2,128,128]{2,3,1,0:T(8,128)(2,1)} %copy-done.15) | copy-start | bytes 1572868
  140.4 6.4 %copy-start.54 = (bf16[128,8,128]{2,0,1:T(8,128)(2,1)S(1)}, bf16[128,8,128]{2,0,1:T(8,128)(2,1)}, u32[]{:S(2)}) copy-start(bf16[128,8,128]{2,0,1:T(8,128)(2,1)} %copy-done.53) | copy-start | bytes 786436
  141.5 44.6 %collective-permute-start.17 = (bf16[128,8,128]{2,0,1:T(8,128)(2,1)}, bf16[128,8,128]{2,0,1:T(8,128)(2,1)}, u32[]{:S(2)}, u32[]{:S(2)}) collective-permute-start(bf16[128,8,128]{2,0,1:T(8,128)(2,1)} %fusion.98), channel_id=1, source_target_pairs={{4,0},{6,2},{8,4},{10,6},{12,8},{14,10},{16,12},{18,14},{20,16},{2... | collective-permute-start | bytes 786440 | tf_op jit(solution)/shard_map/ppermute | solution.py:17
  147.1 2.9 copy-start.8
  148.2 41.7 %collective-permute-start.16 = (bf16[128,8,128]{2,0,1:T(8,128)(2,1)}, bf16[128,8,128]{2,0,1:T(8,128)(2,1)}, u32[]{:S(2)}, u32[]{:S(2)}) collective-permute-start(bf16[128,8,128]{2,0,1:T(8,128)(2,1)} %fusion.97), channel_id=1, source_target_pairs={{2,0},{4,2},{6,4},{8,6},{10,8},{12,10},{14,12},{16,14},{18,16},{20... | collective-permute-start | bytes 786440 | tf_op jit(solution)/shard_map/ppermute | solution.py:17
  150.4 4.7 %copy-start.6 = (bf16[8,2,128,128]{2,3,1,0:T(8,128)(2,1)S(1)}, bf16[8,2,128,128]{2,3,1,0:T(8,128)(2,1)}, u32[]{:S(2)}) copy-start(bf16[8,2,128,128]{2,3,1,0:T(8,128)(2,1)} %copy-done.5) | copy-start | bytes 1572868
  150.4 4.7 %copy-start.46 = (bf16[128,8,128]{2,0,1:T(8,128)(2,1)S(1)}, bf16[128,8,128]{2,0,1:T(8,128)(2,1)}, u32[]{:S(2)}) copy-start(bf16[128,8,128]{2,0,1:T(8,128)(2,1)} %copy-done.45) | copy-start | bytes 786436
  151.4 43.1 %collective-permute-start.18 = (bf16[128,8,128]{2,0,1:T(8,128)(2,1)}, bf16[128,8,128]{2,0,1:T(8,128)(2,1)}, u32[]{:S(2)}, u32[]{:S(2)}) collective-permute-start(bf16[128,8,128]{2,0,1:T(8,128)(2,1)} %fusion.99), channel_id=1, source_target_pairs={{6,0},{8,2},{10,4},{12,6},{14,8},{16,10},{18,12},{20,14},{22,16},{... | collective-permute-start | bytes 786440 | tf_op jit(solution)/shard_map/ppermute | solution.py:17
  156.9 3.2 copy-start.42
  157.9 46.2 %collective-permute-start.20 = (bf16[128,8,128]{2,0,1:T(8,128)(2,1)}, bf16[128,8,128]{2,0,1:T(8,128)(2,1)}, u32[]{:S(2)}, u32[]{:S(2)}) collective-permute-start(bf16[128,8,128]{2,0,1:T(8,128)(2,1)} %fusion.101), channel_id=1, source_target_pairs={{10,0},{12,2},{14,4},{16,6},{18,8},{20,10},{22,12},{24,14},{26,16}... | collective-permute-start | bytes 786440 | tf_op jit(solution)/shard_map/ppermute | solution.py:17
  178.2 6.8 %copy-start.2 = (bf16[8,2,128,128]{2,3,1,0:T(8,128)(2,1)S(1)}, bf16[8,2,128,128]{2,3,1,0:T(8,128)(2,1)}, u32[]{:S(2)}) copy-start(bf16[8,2,128,128]{2,3,1,0:T(8,128)(2,1)} %copy-done.1) | copy-start | bytes 1572868
  179.2 6.8 %copy-start.61 = (bf16[128,8,128]{2,0,1:T(8,128)(2,1)S(1)}, bf16[128,8,128]{2,0,1:T(8,128)(2,1)}, u32[]{:S(2)}) copy-start(bf16[128,8,128]{2,0,1:T(8,128)(2,1)} %fusion.102) | copy-start | bytes 786436
  179.2 10.7 %copy-start.60 = (bf16[128,8,128]{2,0,1:T(8,128)(2,1)S(1)}, bf16[128,8,128]{2,0,1:T(8,128)(2,1)}, u32[]{:S(2)}) copy-start(bf16[128,8,128]{2,0,1:T(8,128)(2,1)} %fusion.103) | copy-start | bytes 786436
  179.2 15.3 %copy-start.59 = (bf16[128,8,128]{2,0,1:T(8,128)(2,1)S(1)}, bf16[128,8,128]{2,0,1:T(8,128)(2,1)}, u32[]{:S(2)}) copy-start(bf16[128,8,128]{2,0,1:T(8,128)(2,1)} %fusion.104) | copy-start | bytes 786436
  179.2 20.1 %collective-permute-start.19 = (bf16[128,8,128]{2,0,1:T(8,128)(2,1)S(1)}, bf16[128,8,128]{2,0,1:T(8,128)(2,1)S(1)}, u32[]{:S(2)}, u32[]{:S(2)}) collective-permute-start(bf16[128,8,128]{2,0,1:T(8,128)(2,1)S(1)} %copy-done.62), channel_id=1, source_target_pairs={{8,0},{10,2},{12,4},{14,6},{16,8},{18,10},{20,12},{22,14},{24,16},... | collective-permute-start | bytes 786440 | tf_op jit(solution)/shard_map/ppermute | solution.py:17
  185.0 60.0 %copy-start.64 = (f32[128]{0:T(128)S(1)}, f32[128]{0:T(128)}, u32[]{:S(2)}) copy-start(f32[128]{0:T(128)} %param.11) | copy-start | bytes 1540
  186.0 28.1 %collective-permute-start.21 = (bf16[128,8,128]{2,0,1:T(8,128)(2,1)S(1)}, bf16[128,8,128]{2,0,1:T(8,128)(2,1)S(1)}, u32[]{:S(2)}, u32[]{:S(2)}) collective-permute-start(bf16[128,8,128]{2,0,1:T(8,128)(2,1)S(1)} %copy-done.61), channel_id=1, source_target_pairs={{12,0},{14,2},{16,4},{18,6},{20,8},{22,10},{24,12},{26,14},{28,16}... | collective-permute-start | bytes 786440 | tf_op jit(solution)/shard_map/ppermute | solution.py:17
  189.9 26.1 %collective-permute-start.22 = (bf16[128,8,128]{2,0,1:T(8,128)(2,1)S(1)}, bf16[128,8,128]{2,0,1:T(8,128)(2,1)S(1)}, u32[]{:S(2)}, u32[]{:S(2)}) collective-permute-start(bf16[128,8,128]{2,0,1:T(8,128)(2,1)S(1)} %copy-done.60), channel_id=1, source_target_pairs={{14,0},{16,2},{18,4},{20,6},{22,8},{24,10},{26,12},{28,14},{30,16}... | collective-permute-start | bytes 786440 | tf_op jit(solution)/shard_map/ppermute | solution.py:17
  194.5 26.7 %collective-permute-start.23 = (bf16[128,8,128]{2,0,1:T(8,128)(2,1)S(1)}, bf16[128,8,128]{2,0,1:T(8,128)(2,1)S(1)}, u32[]{:S(2)}, u32[]{:S(2)}) collective-permute-start(bf16[128,8,128]{2,0,1:T(8,128)(2,1)S(1)} %copy-done.59), channel_id=1, source_target_pairs={{16,0},{18,2},{20,4},{22,6},{24,8},{26,10},{28,12},{30,14},{32,16}... | collective-permute-start | bytes 786440 | tf_op jit(solution)/shard_map/ppermute | solution.py:17
  197.3 6.8 %copy-start.58 = (bf16[128,8,128]{2,0,1:T(8,128)(2,1)S(1)}, bf16[128,8,128]{2,0,1:T(8,128)(2,1)}, u32[]{:S(2)}) copy-start(bf16[128,8,128]{2,0,1:T(8,128)(2,1)} %fusion.95) | copy-start | bytes 786436
  198.3 15.8 %copy-start.56 = (bf16[128,8,128]{2,0,1:T(8,128)(2,1)S(1)}, bf16[128,8,128]{2,0,1:T(8,128)(2,1)}, u32[]{:S(2)}) copy-start(bf16[128,8,128]{2,0,1:T(8,128)(2,1)} %fusion.94) | copy-start | bytes 786436
  198.3 17.7 %copy-start.55 = (bf16[128,8,128]{2,0,1:T(8,128)(2,1)S(1)}, bf16[128,8,128]{2,0,1:T(8,128)(2,1)}, u32[]{:S(2)}) copy-start(bf16[128,8,128]{2,0,1:T(8,128)(2,1)} %fusion.93) | copy-start | bytes 786436
  198.3 46.7 %copy-start.20 = (bf16[128,8,128]{2,1,0:T(8,128)(2,1)S(1)}, bf16[128,8,128]{2,1,0:T(8,128)(2,1)}, u32[]{:S(2)}) copy-start(bf16[128,8,128]{2,1,0:T(8,128)(2,1)} %param.8) | copy-start | bytes 786436
  198.3 46.7 %copy-start.22 = (bf16[8,2,128,128]{2,3,1,0:T(8,128)(2,1)S(1)}, bf16[8,2,128,128]{2,3,1,0:T(8,128)(2,1)}, u32[]{:S(2)}) copy-start(bf16[8,2,128,128]{2,3,1,0:T(8,128)(2,1)} %copy-done.21) | copy-start | bytes 1572868
  199.3 141.6 %copy-start.14 = (bf16[8,2,128,128]{2,3,1,0:T(8,128)(2,1)S(1)}, bf16[8,2,128,128]{2,3,1,0:T(8,128)(2,1)}, u32[]{:S(2)}) copy-start(bf16[8,2,128,128]{2,3,1,0:T(8,128)(2,1)} %copy-done.13) | copy-start | bytes 1572868
  199.3 118.1 %collective-permute-start.24 = (bf16[128,8,128]{2,0,1:T(8,128)(2,1)S(1)}, bf16[128,8,128]{2,0,1:T(8,128)(2,1)}, u32[]{:S(2)}, u32[]{:S(2)}) collective-permute-start(bf16[128,8,128]{2,0,1:T(8,128)(2,1)S(1)} %copy-done.57), channel_id=1, source_target_pairs={{2,0},{4,2},{6,4},{8,6},{10,8},{12,10},{14,12},{16,14},{18,16},{20... | collective-permute-start | bytes 786440 | tf_op jit(solution)/shard_map/ppermute | solution.py:17
  204.1 117.2 %collective-permute-start.25 = (bf16[128,8,128]{2,0,1:T(8,128)(2,1)S(1)}, bf16[128,8,128]{2,0,1:T(8,128)(2,1)}, u32[]{:S(2)}, u32[]{:S(2)}) collective-permute-start(bf16[128,8,128]{2,0,1:T(8,128)(2,1)S(1)} %copy-done.58), channel_id=1, source_target_pairs={{4,0},{6,2},{8,4},{10,6},{12,8},{14,10},{16,12},{18,14},{20,16},{2... | collective-permute-start | bytes 786440 | tf_op jit(solution)/shard_map/ppermute | solution.py:17
  214.1 112.6 %collective-permute-start.26 = (bf16[128,8,128]{2,0,1:T(8,128)(2,1)S(1)}, bf16[128,8,128]{2,0,1:T(8,128)(2,1)}, u32[]{:S(2)}, u32[]{:S(2)}) collective-permute-start(bf16[128,8,128]{2,0,1:T(8,128)(2,1)S(1)} %copy-done.56), channel_id=1, source_target_pairs={{6,0},{8,2},{10,4},{12,6},{14,8},{16,10},{18,12},{20,14},{22,16},{... | collective-permute-start | bytes 786440 | tf_op jit(solution)/shard_map/ppermute | solution.py:17
  216.0 113.9 %collective-permute-start.27 = (bf16[128,8,128]{2,0,1:T(8,128)(2,1)S(1)}, bf16[128,8,128]{2,0,1:T(8,128)(2,1)}, u32[]{:S(2)}, u32[]{:S(2)}) collective-permute-start(bf16[128,8,128]{2,0,1:T(8,128)(2,1)S(1)} %copy-done.55), channel_id=1, source_target_pairs={{8,0},{10,2},{12,4},{14,6},{16,8},{18,10},{20,12},{22,14},{24,16},... | collective-permute-start | bytes 786440 | tf_op jit(solution)/shard_map/ppermute | solution.py:17
  221.3 108.7 %collective-permute-start.28 = (bf16[128,8,128]{2,0,1:T(8,128)(2,1)}, bf16[128,8,128]{2,0,1:T(8,128)(2,1)}, u32[]{:S(2)}, u32[]{:S(2)}) collective-permute-start(bf16[128,8,128]{2,0,1:T(8,128)(2,1)} %fusion.92), channel_id=1, source_target_pairs={{10,0},{12,2},{14,4},{16,6},{18,8},{20,10},{22,12},{24,14},{26,16}... | collective-permute-start | bytes 786440 | tf_op jit(solution)/shard_map/ppermute | solution.py:17
  317.4 12.5 %collective-permute-start.29 = (bf16[128,8,128]{2,0,1:T(8,128)(2,1)}, bf16[128,8,128]{2,0,1:T(8,128)(2,1)S(1)}, u32[]{:S(2)}, u32[]{:S(2)}) collective-permute-start(bf16[128,8,128]{2,0,1:T(8,128)(2,1)} %fusion.91), channel_id=1, source_target_pairs={{12,0},{14,2},{16,4},{18,6},{20,8},{22,10},{24,12},{26,14},{28,16}... | collective-permute-start | bytes 786440 | tf_op jit(solution)/shard_map/ppermute | solution.py:17
  321.3 19.6 %collective-permute-start.30 = (bf16[128,8,128]{2,0,1:T(8,128)(2,1)}, bf16[128,8,128]{2,0,1:T(8,128)(2,1)S(1)}, u32[]{:S(2)}, u32[]{:S(2)}) collective-permute-start(bf16[128,8,128]{2,0,1:T(8,128)(2,1)} %fusion.90), channel_id=1, source_target_pairs={{14,0},{16,2},{18,4},{20,6},{22,8},{24,10},{26,12},{28,14},{30,16}... | collective-permute-start | bytes 786440 | tf_op jit(solution)/shard_map/ppermute | solution.py:17
  326.7 14.3 %collective-permute-start.31 = (bf16[128,8,128]{2,0,1:T(8,128)(2,1)}, bf16[128,8,128]{2,0,1:T(8,128)(2,1)S(1)}, u32[]{:S(2)}, u32[]{:S(2)}) collective-permute-start(bf16[128,8,128]{2,0,1:T(8,128)(2,1)} %fusion.89), channel_id=1, source_target_pairs={{16,0},{18,2},{20,4},{22,6},{24,8},{26,10},{28,12},{30,14},{32,16}... | collective-permute-start | bytes 786440 | tf_op jit(solution)/shard_map/ppermute | solution.py:17
  (34 other events, 44.4 us)
where the time goes:
time: 350 us; the launch traced here: 345 us
  starting transfers between devices  144 us (41%)
  blocking collectives  70.5 us (20%)
  waiting for transfers between devices  66.2 us (19%)
  matrix products  34.2 us (10%)
  local copies, waits for them, and re-layouts  14.2 us (4%)
  other arithmetic  13.3 us (4%)
    ppermute x32, starting transfers between devices, passed_along(): lax.ppermute(value, axis, [(source, source + steps) for source in range(f...  144 us
    psum x1, blocking collectives, per_device(): query_sum, key_sum = lax.psum((query_term_sum, key_term_sum), ('ctx', 'kv'))  70.5 us
    ppermute x32, waiting for transfers between devices, passed_along(): lax.ppermute(value, axis, [(source, source + steps) for source in range(f...  66.2 us
    unnamed x135, local copies, waits for them, and re-layouts  10.6 us
    dot_general x9, matrix products, per_device(): jnp.einsum('gjts,tgjd->sgd', score_grad, query_four, preferred_element_ty...  9.95 us
    dot_general x9, matrix products, per_device(): jnp.einsum('gjts,tgjd->sgd', tile_attend, grad_four, preferred_element_ty...  9.74 us
  transfers between devices with their start and end apart: 32, of which 8 were waited for; matrix products, arithmetic and copies ran while one was open for 12% of the time, Pallas kernels for 0%

commit v1 on v0

v1 whole, which is shorter than its diff:
```python
import functools
import jax
import jax.numpy as jnp
from jax import lax
from jax.experimental import pallas as pl
from jax.experimental.pallas import tpu as pltpu
from jax.sharding import Mesh, PartitionSpec as P

LOOKBACK_SPAN = 1024
epsilon = 1e-06
score_scale = 168.0 ** (-0.5)
exponent_scale = score_scale * 1.4426950408889634
masked_score = -1e30
F32 = jnp.float32
BF16 = jnp.bfloat16
VMEM = pl.BlockSpec(memory_space=pltpu.VMEM)


def call(body, out_shape, scratch, flops, moved, exps, *args):
    return pl.pallas_call(
        body,
        out_shape=out_shape,
        in_specs=[VMEM] * len(args),
        out_specs=jax.tree.map(lambda _: VMEM, out_shape),
        scratch_shapes=scratch,
        compiler_params=pltpu.CompilerParams(vmem_limit_bytes=48 << 20),
        cost_estimate=pl.CostEstimate(flops=flops, bytes_accessed=moved, transcendentals=exps),
    )(*args)


def pack_body(per_owner, *refs):
    count = len(per_owner)
    sources, out_ref, wide = refs[:count], refs[count], refs[count + 1]
    slot = 0
    for source, heads in zip(sources, per_owner):
        total = source.shape[1]
        wide[:, :total, :] = source[...].astype(F32)
        for head in range(total):
            out_ref[head // heads, slot + head % heads] = wide[:, head, :].astype(BF16)
        slot += heads


def pack(owners, *sources):
    tokens, _, width = sources[0].shape
    per_owner = [source.shape[1] // owners for source in sources]
    widest = max(source.shape[1] for source in sources)
    size = sum(source.size for source in sources)
    return call(
        functools.partial(pack_body, per_owner),
        jax.ShapeDtypeStruct((owners, sum(per_owner), tokens, width), BF16),
        [pltpu.VMEM((tokens, widest, width), F32)],
        size,
        4 * size,
        0,
        *sources,
    )


def unpack_body(per_owner, in_ref, *refs):
    outs, wide = refs[:-1], refs[-1]
    owners = in_ref.shape[0]
    slot = 0
    for out_ref, heads in zip(outs, per_owner):
        total = out_ref.shape[1]
        for head in range(total):
            wide[:, head, :] = in_ref[head // heads, slot + head % heads].astype(F32)
        out_ref[...] = wide[:, :total, :].astype(BF16)
        slot += heads


def unpack(received, per_owner):
    owners, _, tokens, width = received.shape
    return call(
        functools.partial(unpack_body, per_owner),
        [jax.ShapeDtypeStruct((tokens, owners * heads, width), BF16) for heads in per_owner],
        [pltpu.VMEM((tokens, owners * max(per_owner), width), F32)],
        received.size,
        4 * received.size,
        0,
        received,
    )


def unit_and_inverse(raw):
    widened = raw.astype(F32)
    inverse = lax.rsqrt(jnp.mean(widened * widened, axis=-1, keepdims=True) + epsilon)
    return widened * inverse, inverse


def normalize_back(normed_grad, unit_rows, inverse, gain_values):
    scaled = normed_grad * gain_values
    return inverse * (scaled - unit_rows * jnp.mean(scaled * unit_rows, axis=-1, keepdims=True))


def contract_last(left, right):
    return lax.dot_general(left, right, (((1,), (1,)), ((), ())), preferred_element_type=F32)


def matmul(left, right):
    return lax.dot_general(left, right, (((1,), (0,)), ((), ())), preferred_element_type=F32)


def fold_rows(tile, combine):
    return combine(tile.reshape(tile.shape[0] // 8, 8, tile.shape[1]), axis=0)


def attend_body(
    qd_ref, own_ref, prev_ref, doc_ref, qgain_ref, kgain_ref,
    qgrad_ref, dk_own_ref, dv_own_ref, back_ref, gain_ref,
    key_rows, key_cols, value_cols, key_docs, score_buf, attend_buf, grad_buf, dk_acc, dv_acc, gain_acc,
):
    blocks, _, rows, width = qd_ref.shape
    tiles = blocks + 1
    window = tiles * rows
    query_gain = qgain_ref[...]
    key_gain = kgain_ref[...]
    for block in range(2 * blocks):
        source = prev_ref if block < blocks else own_ref
        span = slice(block * rows, (block + 1) * rows)
        unit, _ = unit_and_inverse(source[block % blocks, 0])
        normed = (unit * key_gain).astype(BF16)
        key_rows[span, :] = normed
        key_cols[:, span] = normed.T
        value_cols[:, span] = source[block % blocks, 1].T
        key_docs[span, :] = jnp.broadcast_to(doc_ref[:, span], (rows, rows)).T
    dk_acc[...] = jnp.zeros_like(dk_acc)
    dv_acc[...] = jnp.zeros_like(dv_acc)
    gain_acc[...] = jnp.zeros_like(gain_acc)

    key_index = lax.broadcasted_iota(jnp.int32, (rows, rows), 0)
    query_index = lax.broadcasted_iota(jnp.int32, (rows, rows), 1)

    def one_block(block, _):
        start = pl.multiple_of(block * rows, rows)
        own_start = pl.multiple_of((block + blocks) * rows, rows)
        query_unit, query_inverse = unit_and_inverse(qd_ref[block, 0:2].reshape(2 * rows, width))
        query = (query_unit * query_gain).astype(BF16)
        out_grad = qd_ref[block, 2:4].reshape(2 * rows, width)
        query_docs = doc_ref[:, pl.ds(own_start, rows)]
        peak = jnp.full((8, 2 * rows), masked_score, F32)
        for tile in range(tiles):
            span = pl.ds(pl.multiple_of(start + tile * rows, rows), rows)
            allowed = key_docs[span, :] == query_docs
            if tile == 0:
                allowed = allowed & (key_index > query_index)
            if tile == tiles - 1:
                allowed = allowed & (key_index <= query_index)
            scores = contract_last(key_rows[span, :], query)
            scores = jnp.concatenate(
                [
                    jnp.where(allowed, scores[:, :rows], masked_score),
                    jnp.where(allowed, scores[:, rows:], masked_score),
                ],
                axis=1,
            )
            score_buf[tile * rows:(tile + 1) * rows, :] = scores
            peak = jnp.maximum(peak, fold_rows(scores, jnp.max))
        peak = jnp.max(peak, axis=0, keepdims=True)
        total = jnp.zeros((8, 2 * rows), F32)
        for tile in range(tiles):
            local = slice(tile * rows, (tile + 1) * rows)
            powers = jnp.exp2((score_buf[local, :] - peak) * exponent_scale)
            score_buf[local, :] = powers
            total = total + fold_rows(powers, jnp.sum)
        inverse_total = 1.0 / jnp.sum(total, axis=0, keepdims=True)
        for tile in range(tiles):
            local = slice(tile * rows, (tile + 1) * rows)
            attend_buf[local, :] = (score_buf[local, :] * inverse_total).astype(BF16)
        out_cols = matmul(value_cols[:, pl.ds(start, window)], attend_buf[...])
        out_grad_cols = jnp.concatenate(
            [out_grad[:rows].T, out_grad[rows:].T], axis=1
        ).astype(F32)
        row_dots = jnp.sum(
            out_grad_cols * out_cols.astype(BF16).astype(F32), axis=0, keepdims=True
        )
        for tile in range(tiles):
            local = slice(tile * rows, (tile + 1) * rows)
            source_block = block + tile
            value_rows = value_cols[:, pl.ds(pl.multiple_of(start + tile * rows, rows), rows)]
            prob_grad = lax.dot_general(
                value_rows, out_grad_cols.astype(BF16), (((0,), (0,)), ((), ())),
                preferred_element_type=F32,
            )
            grad_buf[local, :] = (
                attend_buf[local, :].astype(F32) * (prob_grad - row_dots)
            ).astype(BF16)
        reach = pl.ds(start, window)
        dk_acc[reach, :] += matmul(grad_buf[...], query)
        dv_acc[reach, :] += matmul(attend_buf[...], out_grad)
        query_cols = matmul(key_cols[:, reach], grad_buf[...])
        normed_grad = (
            jnp.concatenate([query_cols[:, :rows].T, query_cols[:, rows:].T], axis=0) * score_scale
        )
        gain_acc[0:8, :] += fold_rows(normed_grad * query_unit, jnp.sum)
        query_grad = normalize_back(normed_grad, query_unit, query_inverse, query_gain)
        qgrad_ref[block] = query_grad.astype(BF16).reshape(2, rows, width)
        return 0

    lax.fori_loop(0, blocks, one_block, 0)

    for block in range(2 * blocks):
        source = prev_ref if block < blocks else own_ref
        span = slice(block * rows, (block + 1) * rows)
        unit, _ = unit_and_inverse(source[block % blocks, 0])
        key_part = dk_acc[span, :] * score_scale
        gain_acc[8:16, :] += fold_rows(key_part * unit, jnp.sum)
        if block < blocks:
            back_ref[block, 0] = key_part.astype(BF16)
            back_ref[block, 1] = dv_acc[span, :].astype(BF16)
        else:
            dk_own_ref[block - blocks] = key_part
            dv_own_ref[block - blocks] = dv_acc[span, :]
    gain_ref[0:1, :] = jnp.sum(gain_acc[0:8, :], axis=0, keepdims=True)
    gain_ref[1:2, :] = jnp.sum(gain_acc[8:16, :], axis=0, keepdims=True)


def attend(queries, own, prev, docs, query_gain, key_gain):
    blocks, _, rows, width = queries.shape
    window = (blocks + 1) * rows
    tile_flops = 2 * window * 2 * rows * width
    return call(
        attend_body,
        [
            jax.ShapeDtypeStruct((blocks, 2, rows, width), BF16),
            jax.ShapeDtypeStruct((blocks, rows, width), F32),
            jax.ShapeDtypeStruct((blocks, rows, width), F32),
            jax.ShapeDtypeStruct((blocks, 2, rows, width), BF16),
            jax.ShapeDtypeStruct((2, width), F32),
        ],
        [
            pltpu.VMEM((2 * blocks * rows, width), BF16),
            pltpu.VMEM((width, 2 * blocks * rows), BF16),
            pltpu.VMEM((width, 2 * blocks * rows), BF16),
            pltpu.VMEM((2 * blocks * rows, rows), jnp.int32),
            pltpu.VMEM((window, 2 * rows), F32),
            pltpu.VMEM((window, 2 * rows), BF16),
            pltpu.VMEM((window, 2 * rows), BF16),
            pltpu.VMEM((2 * blocks * rows, width), F32),
            pltpu.VMEM((2 * blocks * rows, width), F32),
            pltpu.VMEM((16, width), F32),
        ],
        6 * blocks * tile_flops,
        8 * queries.size,
        blocks * window * 2 * rows,
        queries, own, prev, docs, query_gain, key_gain,
    )


def finish_keys_body(own_ref, dk_ref, dv_ref, back_ref, kgain_ref, out_ref):
    key_gain = kgain_ref[...]
    for block in range(own_ref.shape[0]):
        unit, inverse = unit_and_inverse(own_ref[block, 0])
        key_total = dk_ref[block] + back_ref[block, 0].astype(F32)
        value_total = dv_ref[block] + back_ref[block, 1].astype(F32)
        out_ref[block, 0] = normalize_back(key_total, unit, inverse, key_gain).astype(BF16)
        out_ref[block, 1] = value_total.astype(BF16)


def finish_keys(own, dk_own, dv_own, back, key_gain):
    return call(
        finish_keys_body,
        jax.ShapeDtypeStruct(own.shape, BF16),
        [],
        10 * own.size,
        8 * own.size,
        0,
        own, dk_own, dv_own, back, key_gain,
    )


def per_device(ring_axes, query_raw, key_raw, value_matrix, query_gain, key_gain, doc_ids, output_gradient):
    ring_size = lax.axis_size("z")
    rings = lax.axis_size(ring_axes)
    rows = query_raw.shape[0]
    width = query_raw.shape[2]
    span = ring_size * rows
    forward = [(ring, ring + 1) for ring in range(rings - 1)]
    backward = [(ring + 1, ring) for ring in range(rings - 1)]
    query_gain = query_gain.reshape(1, width)
    key_gain = key_gain.reshape(1, width)

    def exchange(value):
        return lax.all_to_all(value, "z", 0, 0, tiled=True)

    own = exchange(pack(ring_size, key_raw, value_matrix))
    prev = lax.ppermute(own, ring_axes, forward)
    queries = exchange(pack(ring_size, query_raw, output_gradient))
    doc_padded = jnp.concatenate([jnp.full((span,), -1, jnp.int32), doc_ids])
    docs = lax.dynamic_slice_in_dim(
        doc_padded, lax.axis_index(ring_axes) * span, 2 * span, 0
    ).reshape(1, 2 * span)
    query_back, dk_own, dv_own, back, gain_part = attend(
        queries, own, prev, docs, query_gain, key_gain
    )
    got_back = lax.ppermute(back, ring_axes, backward)
    (query_grad,) = unpack(exchange(query_back), [2])
    sent = finish_keys(own, dk_own, dv_own, got_back, key_gain)
    key_grad, value_grad = unpack(exchange(sent), [1, 1])
    gain_sum = gain_part
    for axis in ("kv", "z", "y", "x"):
        gain_sum = lax.psum(gain_sum, axis)
    gain_sum = gain_sum / doc_ids.shape[0]
    return query_grad, key_grad, value_grad, gain_sum[0], gain_sum[1]


def solution(mesh):
    ring_size = LOOKBACK_SPAN // 128
    grid = Mesh(mesh.devices.reshape(4, 4, ring_size, 2), ("x", "y", "z", "kv"))
    split = P(("x", "y", "z"), "kv", None)
    return jax.shard_map(
        functools.partial(per_device, ("x", "y")),
        mesh=grid,
        in_specs=(split, split, split, P(), P(), P(), split),
        out_specs=(split, split, split, P(), P()),
        check_vma=False,
    )
```

time: 350 us -> 160 us (0.46); the launches traced: 345 us -> 159 us
  starting transfers between devices: 144 us -> 30.9 us
  matrix products: 34.2 us -> 0 us
  Pallas kernels: 0 us -> 27.3 us
  blocking collectives: 70.5 us -> 44.1 us
  waiting for transfers between devices: 66.2 us -> 50.2 us
  other arithmetic: 13.3 us -> 0.01 us
  local copies, waits for them, and re-layouts: 14.2 us -> 5.75 us
    ppermute x32 -> x2, starting transfers between devices: 144 us -> 8.38 us  [the longest x1 4.9 us: per_device(): got_back = lax.ppermute(back, ring_axes, backward)]
    ppermute x32 -> x2, waiting for transfers between devices: 66.2 us -> 25.7 us  [the longest x1 14.3 us: per_device(): prev = lax.ppermute(own, ring_axes, forward)]
    dot_general x54 -> x0, matrix products: 34.2 us -> none  [the longest x9 9.95 us: per_device(): jnp.einsum('gjts,tgjd->sgd', score_grad, query_four, preferred_element_ty...]
    pallas_call x0 -> x6, Pallas kernels: none -> 27.3 us  [call(): pl.pallas_call(body, out_shape=out_shape, in_specs=[VMEM] * len(args), ou...]
    psum x1 -> x4, blocking collectives: 70.5 us -> 44.1 us  [per_device(): gain_sum = lax.psum(gain_sum, axis)]
    all_to_all x0 -> x4, waiting for transfers between devices: none -> 24.6 us  [exchange(): return lax.all_to_all(value, 'z', 0, 0, tiled=True)]
    all_to_all x0 -> x4, starting transfers between devices: none -> 22.5 us  [exchange(): return lax.all_to_all(value, 'z', 0, 0, tiled=True)]
    unnamed x135 -> x22, local copies, waits for them, and re-layouts: 10.6 us -> 5.21 us
  transfers between devices with their start and end apart: 32 -> 6, of which waited for: 8 -> 5; matrix products, arithmetic and copies ran while one was open for 12% -> 0% of each run, Pallas kernels for 0% -> 4%
where the time goes in v1:
time: 160 us; the launch traced here: 159 us
  waiting for transfers between devices  50.2 us (31%)
  blocking collectives  44.1 us (28%)
  starting transfers between devices  30.9 us (19%)
  Pallas kernels  27.3 us (17%)
  local copies, waits for them, and re-layouts  5.75 us (4%)
    psum x4, blocking collectives, per_device(): gain_sum = lax.psum(gain_sum, axis)  44.1 us
    pallas_call x6, Pallas kernels, call(): pl.pallas_call(body, out_shape=out_shape, in_specs=[VMEM] * len(args), ou...  27.3 us
    all_to_all x4, waiting for transfers between devices, exchange(): return lax.all_to_all(value, 'z', 0, 0, tiled=True)  24.6 us
    all_to_all x4, starting transfers between devices, exchange(): return lax.all_to_all(value, 'z', 0, 0, tiled=True)  22.5 us
    ppermute x1, waiting for transfers between devices, per_device(): prev = lax.ppermute(own, ring_axes, forward)  14.3 us
    ppermute x1, waiting for transfers between devices, per_device(): got_back = lax.ppermute(back, ring_axes, backward)  11.3 us
    unnamed x22, local copies, waits for them, and re-layouts  5.21 us
    ppermute x1, starting transfers between devices, per_device(): got_back = lax.ppermute(back, ring_axes, backward)  4.9 us
  transfers between devices with their start and end apart: 6, of which 5 were waited for; matrix products, arithmetic and copies ran while one was open for 0% of the time, Pallas kernels for 4%

profile of v1, /device:TPU:2, one launch (start us, length us, event | category | flops | bytes accessed | tf_op | source)
XLA Modules:
  0.0 159.0 jit_solution(6235571308800547408)
XLA Ops:
  0.6 0.0 copy-start.2
  0.6 0.9 copy-done.2
  1.6 0.0 copy-start.3
  1.6 0.9 copy-done.3
  2.5 2.1 %shard_map.111 = bf16[8,2,128,128]{3,2,1,0:T(8,128)(2,1)} custom-call(bf16[128,8,128]{2,1,0:T(8,128)(2,1)S(1)} %copy-done.2, bf16[128,8,128]{2,1,0:T(8,128)(2,1)S(1)} %copy-done.3), custom_call_target="tpu_custom_call" | custom-call | flops 262144 | bytes 1048576 | tf_op jit(solution)/shard_map/pallas_call | solution.py:20
  4.7 0.0 copy-start
  4.7 0.0 copy-start.1
  4.7 8.6 %all-to-all-start.1 = ((bf16[8,2,128,128]{3,2,1,0:T(8,128)(2,1)}), bf16[8,2,128,128]{3,2,1,0:T(8,128)(2,1)S(1)}, u32[]{:S(2)}, u32[]{:S(2)}) async-start(bf16[8,2,128,128]{3,2,1,0:T(8,128)(2,1)} %shard_map.111), calls=%async_computation.1 | async-start | bytes 1048576 | tf_op jit(solution)/shard_map/all_to_all | solution.py:283
  13.3 0.0 copy-done
  13.3 0.0 copy-done.1
  13.3 3.7 %shard_map.110 = bf16[8,4,128,128]{3,2,1,0:T(8,128)(2,1)} custom-call(bf16[128,16,128]{2,1,0:T(8,128)(2,1)S(1)} %copy-done, bf16[128,16,128]{2,1,0:T(8,128)(2,1)S(1)} %copy-done.1), custom_call_target="tpu_custom_call" | custom-call | flops 524288 | bytes 2097152 | tf_op jit(solution)/shard_map/pallas_call | solution.py:20
  17.0 13.8 %all-to-all-done.1.own_ref = bf16[8,2,128,128]{3,2,1,0:T(8,128)(2,1)S(1)} async-done(((bf16[8,2,128,128]{3,2,1,0:T(8,128)(2,1)}), bf16[8,2,128,128]{3,2,1,0:T(8,128)(2,1)S(1)}, u32[]{:S(2)}, u32[]{:S(2)}) %all-to-all-start.1) | async-done | bytes 524320 | tf_op jit(solution)/shard_map/all_to_all | solution.py:283
  30.8 0.0 copy-start.10
  30.8 3.7 %all-to-all-start = ((bf16[8,4,128,128]{3,2,1,0:T(8,128)(2,1)}), bf16[8,4,128,128]{3,2,1,0:T(8,128)(2,1)S(1)}, u32[]{:S(2)}, u32[]{:S(2)}) async-start(bf16[8,4,128,128]{3,2,1,0:T(8,128)(2,1)} %shard_map.110), calls=%async_computation | async-start | bytes 2097152 | tf_op jit(solution)/shard_map/all_to_all | solution.py:283
  34.5 3.5 %collective-permute-start = (bf16[8,2,128,128]{3,2,1,0:T(8,128)(2,1)S(1)}, bf16[8,2,128,128]{3,2,1,0:T(8,128)(2,1)S(1)}, u32[]{:S(2)}, u32[]{:S(2)}) collective-permute-start(bf16[8,2,128,128]{3,2,1,0:T(8,128)(2,1)S(1)} %all-to-all-done.1.own_ref), channel_id=1, source_target_pairs={{0,16},{16,32},{32,48},{48,64},{64,80},{80,96},{96,112},{112,128},... | collective-permute-start | bytes 1572872 | tf_op jit(solution)/shard_map/ppermute | solution.py:286
  38.0 0.0 copy-done.10
  38.0 14.3 %collective-permute-done.prev_ref = bf16[8,2,128,128]{3,2,1,0:T(8,128)(2,1)S(1)} collective-permute-done((bf16[8,2,128,128]{3,2,1,0:T(8,128)(2,1)S(1)}, bf16[8,2,128,128]{3,2,1,0:T(8,128)(2,1)S(1)}, u32[]{:S(2)}, u32[]{:S(2)}) %collective-permute-start) | collective-permute-done | bytes 524320 | tf_op jit(solution)/shard_map/ppermute | solution.py:286
  52.3 0.0 copy-start.5
  52.3 0.8 copy-done.5
  53.1 10.5 %all-to-all-done.qd_ref = bf16[8,4,128,128]{3,2,1,0:T(8,128)(2,1)S(1)} async-done(((bf16[8,4,128,128]{3,2,1,0:T(8,128)(2,1)}), bf16[8,4,128,128]{3,2,1,0:T(8,128)(2,1)S(1)}, u32[]{:S(2)}, u32[]{:S(2)}) %all-to-all-start) | async-done | bytes 1048608 | tf_op jit(solution)/shard_map/all_to_all | solution.py:283
  63.6 0.0 copy-start.4
  63.6 0.0 copy-start.9
  63.6 0.7 copy-done.4
  64.3 0.0 copy-done.9
  64.3 0.0 copy-start.6
  64.3 1.0 copy-done.6
  65.3 17.3 %shard_map.112 = (bf16[8,2,128,128]{3,2,1,0:T(8,128)(2,1)}, f32[8,128,128]{2,1,0:T(8,128)S(1)}, f32[8,128,128]{2,1,0:T(8,128)S(1)}, bf16[8,2,128,128]{3,2,1,0:T(8,128)(2,1)S(1)}, f32[2,128]{1,0:T(2,128)S(1)}) custom-call(bf16[8,4,128,128]{3,2,1,0:T(8,128)(2,1)S(1)} %all-to-all-done.qd_ref, bf16[8,2,128,128]{3,2,1,0:T(8,128)(2,1)S(1)} %all-to-all-done.1.own_ref, ...), custom_call_target="tpu_custom_call" | custom-call | flops 3623878656 | bytes 4194304 | tf_op jit(solution)/shard_map/pallas_call | solution.py:20
  82.6 0.0 copy-start.7
  82.6 0.8 copy-done.7
  83.4 0.0 copy-start.8
  83.4 3.6 %all-to-all-start.2 = ((bf16[8,2,128,128]{3,2,1,0:T(8,128)(2,1)}), bf16[8,2,128,128]{3,2,1,0:T(8,128)(2,1)S(1)}, u32[]{:S(2)}, u32[]{:S(2)}) async-start(bf16[8,2,128,128]{3,2,1,0:T(8,128)(2,1)} %get-tuple-element.12), calls=%async_computation.2 | async-start | bytes 1048576 | tf_op jit(solution)/shard_map/all_to_all | solution.py:283
  87.1 0.0 copy-done.8
  87.1 4.9 %collective-permute-start.1 = (bf16[8,2,128,128]{3,2,1,0:T(8,128)(2,1)S(1)}, bf16[8,2,128,128]{3,2,1,0:T(8,128)(2,1)S(1)}, u32[]{:S(2)}, u32[]{:S(2)}) collective-permute-start(bf16[8,2,128,128]{3,2,1,0:T(8,128)(2,1)S(1)} %copy-done.8), channel_id=1, source_target_pairs={{16,0},{32,16},{48,32},{64,48},{80,64},{96,80},{112,96},{128,112},... | collective-permute-start | bytes 1572872 | tf_op jit(solution)/shard_map/ppermute | solution.py:295
  92.0 11.3 %collective-permute-done.1.back_ref = bf16[8,2,128,128]{3,2,1,0:T(8,128)(2,1)S(1)} collective-permute-done((bf16[8,2,128,128]{3,2,1,0:T(8,128)(2,1)S(1)}, bf16[8,2,128,128]{3,2,1,0:T(8,128)(2,1)S(1)}, u32[]{:S(2)}, u32[]{:S(2)}) %collective-permute-start.1) | collective-permute-done | bytes 524320 | tf_op jit(solution)/shard_map/ppermute | solution.py:295
  103.3 1.4 shard_map.114
  104.7 0.2 all-to-all-done.2.in_ref
  104.9 6.6 %all-to-all-start.3 = ((bf16[8,2,128,128]{3,2,1,0:T(8,128)(2,1)}), bf16[8,2,128,128]{3,2,1,0:T(8,128)(2,1)S(1)}, u32[]{:S(2)}, u32[]{:S(2)}) async-start(bf16[8,2,128,128]{3,2,1,0:T(8,128)(2,1)} %shard_map.114), calls=%async_computation.3 | async-start | bytes 1048576 | tf_op jit(solution)/shard_map/all_to_all | solution.py:283
  111.5 2.5 %psum.28 = f32[2,128]{1,0:T(2,128)S(1)} all-reduce(f32[2,128]{1,0:T(2,128)S(1)} %get-tuple-element.18), channel_id=1, replica_groups=mesh['x'=4,'y'=4,'z'=8,'kv'=2] {'kv'}, use_global_device_ids=true, to_apply=%region_0.0 | all-reduce | flops 256 | bytes 2048 | tf_op jit(solution)/shard_map/psum | solution.py:301
  114.0 20.7 %psum.29 = f32[2,128]{1,0:T(2,128)S(1)} all-reduce(f32[2,128]{1,0:T(2,128)S(1)} %psum.28), channel_id=1, replica_groups=mesh['x'=4,'y'=4,'z'=8,'kv'=2] {'z'}, use_global_device_ids=true, to_apply=%region_1.0 | all-reduce | flops 256 | bytes 2048 | tf_op jit(solution)/shard_map/psum | solution.py:301
  134.6 12.3 %psum.30 = f32[2,128]{1,0:T(2,128)S(1)} all-reduce(f32[2,128]{1,0:T(2,128)S(1)} %psum.29), channel_id=1, replica_groups=mesh['x'=4,'y'=4,'z'=8,'kv'=2] {'y'}, use_global_device_ids=true, to_apply=%region_2.0 | all-reduce | flops 256 | bytes 2048 | tf_op jit(solution)/shard_map/psum | solution.py:301
  147.0 8.6 %psum.31 = f32[2,128]{1,0:T(2,128)S(1)} all-reduce(f32[2,128]{1,0:T(2,128)S(1)} %psum.30), channel_id=1, replica_groups=mesh['x'=4,'y'=4,'z'=8,'kv'=2] {'x'}, use_global_device_ids=true, to_apply=%region_3.0 | all-reduce | flops 256 | bytes 2048 | tf_op jit(solution)/shard_map/psum | solution.py:301
  155.6 0.5 slice_bitcast_fusion
  156.1 1.5 shard_map.113
  157.7 0.0 all-to-all-done.3.in_ref
  157.7 1.3 shard_map.115
  (2 shorter events, 0.0 us)
Async XLA Ops:
  0.6 1.0 copy-start.2
  1.6 0.9 copy-start.3
  4.7 8.6 %copy-start = (bf16[128,16,128]{2,1,0:T(8,128)(2,1)S(1)}, bf16[128,16,128]{2,1,0:T(8,128)(2,1)}, u32[]{:S(2)}) copy-start(bf16[128,16,128]{2,1,0:T(8,128)(2,1)} %refs_0_.2) | copy-start | bytes 1572868
  4.7 8.6 %copy-start.1 = (bf16[128,16,128]{2,1,0:T(8,128)(2,1)S(1)}, bf16[128,16,128]{2,1,0:T(8,128)(2,1)}, u32[]{:S(2)}) copy-start(bf16[128,16,128]{2,1,0:T(8,128)(2,1)} %refs_1_.2) | copy-start | bytes 1572868
  4.7 26.1 %all-to-all-start.1 = ((bf16[8,2,128,128]{3,2,1,0:T(8,128)(2,1)}), bf16[8,2,128,128]{3,2,1,0:T(8,128)(2,1)S(1)}, u32[]{:S(2)}, u32[]{:S(2)}) async-start(bf16[8,2,128,128]{3,2,1,0:T(8,128)(2,1)} %shard_map.111), calls=%async_computation.1 | async-start | bytes 1048576 | tf_op jit(solution)/shard_map/all_to_all | solution.py:283
  30.8 7.2 %copy-start.10 = (s32[16384]{0:T(1024)S(1)}, s32[16384]{0:T(1024)}, u32[]{:S(2)}) copy-start(s32[16384]{0:T(1024)} %param.12) | copy-start | bytes 196612
  30.8 32.8 %all-to-all-start = ((bf16[8,4,128,128]{3,2,1,0:T(8,128)(2,1)}), bf16[8,4,128,128]{3,2,1,0:T(8,128)(2,1)S(1)}, u32[]{:S(2)}, u32[]{:S(2)}) async-start(bf16[8,4,128,128]{3,2,1,0:T(8,128)(2,1)} %shard_map.110), calls=%async_computation | async-start | bytes 2097152 | tf_op jit(solution)/shard_map/all_to_all | solution.py:283
  34.5 17.8 %collective-permute-start = (bf16[8,2,128,128]{3,2,1,0:T(8,128)(2,1)S(1)}, bf16[8,2,128,128]{3,2,1,0:T(8,128)(2,1)S(1)}, u32[]{:S(2)}, u32[]{:S(2)}) collective-permute-start(bf16[8,2,128,128]{3,2,1,0:T(8,128)(2,1)S(1)} %all-to-all-done.1.own_ref), channel_id=1, source_target_pairs={{0,16},{16,32},{32,48},{48,64},{64,80},{80,96},{96,112},{112,128},... | collective-permute-start | bytes 1572872 | tf_op jit(solution)/shard_map/ppermute | solution.py:286
  52.3 0.8 copy-start.5
  63.6 0.7 copy-start.4
  63.6 0.7 copy-start.9
  64.3 1.0 copy-start.6
  82.6 0.8 copy-start.7
  83.4 3.6 %copy-start.8 = (bf16[8,2,128,128]{3,2,1,0:T(8,128)(2,1)S(1)}, bf16[8,2,128,128]{3,2,1,0:T(8,128)(2,1)}, u32[]{:S(2)}) copy-start(bf16[8,2,128,128]{3,2,1,0:T(8,128)(2,1)} %copy-done.7) | copy-start | bytes 1572868
  83.4 21.5 %all-to-all-start.2 = ((bf16[8,2,128,128]{3,2,1,0:T(8,128)(2,1)}), bf16[8,2,128,128]{3,2,1,0:T(8,128)(2,1)S(1)}, u32[]{:S(2)}, u32[]{:S(2)}) async-start(bf16[8,2,128,128]{3,2,1,0:T(8,128)(2,1)} %get-tuple-element.12), calls=%async_computation.2 | async-start | bytes 1048576 | tf_op jit(solution)/shard_map/all_to_all | solution.py:283
  87.1 16.3 %collective-permute-start.1 = (bf16[8,2,128,128]{3,2,1,0:T(8,128)(2,1)S(1)}, bf16[8,2,128,128]{3,2,1,0:T(8,128)(2,1)S(1)}, u32[]{:S(2)}, u32[]{:S(2)}) collective-permute-start(bf16[8,2,128,128]{3,2,1,0:T(8,128)(2,1)S(1)} %copy-done.8), channel_id=1, source_target_pairs={{16,0},{32,16},{48,32},{64,48},{80,64},{96,80},{112,96},{128,112},... | collective-permute-start | bytes 1572872 | tf_op jit(solution)/shard_map/ppermute | solution.py:295
  104.9 52.7 %all-to-all-start.3 = ((bf16[8,2,128,128]{3,2,1,0:T(8,128)(2,1)}), bf16[8,2,128,128]{3,2,1,0:T(8,128)(2,1)S(1)}, u32[]{:S(2)}, u32[]{:S(2)}) async-start(bf16[8,2,128,128]{3,2,1,0:T(8,128)(2,1)} %shard_map.114), calls=%async_computation.3 | async-start | bytes 1048576 | tf_op jit(solution)/shard_map/all_to_all | solution.py:283

commit v2 on v1

v2 whole, which is shorter than its diff:
```python
import functools
import jax
import jax.numpy as jnp
from jax import lax
from jax.experimental import pallas as pl
from jax.experimental.pallas import tpu as pltpu
from jax.sharding import Mesh, PartitionSpec as P

LOOKBACK_SPAN = 1024
epsilon = 1e-06
score_scale = 168.0 ** (-0.5)
exponent_scale = score_scale * 1.4426950408889634
masked_score = -1e30
F32 = jnp.float32
BF16 = jnp.bfloat16
TAIL_ROWS = 16
VMEM_BYTES = 8 << 20
HBM = pl.BlockSpec(memory_space=pltpu.HBM)
VMEM = pl.BlockSpec(memory_space=pltpu.VMEM)


def call(body, out_shape, scratch, flops, moved, exps, *args, vmem_bytes=VMEM_BYTES):
    return pl.pallas_call(
        body,
        out_shape=out_shape,
        in_specs=[VMEM] * len(args),
        out_specs=jax.tree.map(
            lambda out: HBM if getattr(out, "memory_space", None) == pltpu.HBM else VMEM,
            out_shape,
        ),
        scratch_shapes=scratch,
        compiler_params=pltpu.CompilerParams(vmem_limit_bytes=vmem_bytes),
        cost_estimate=pl.CostEstimate(flops=flops, bytes_accessed=moved, transcendentals=exps),
    )(*args)


def pack_body(per_owner, passed, *refs):
    count = len(per_owner)
    sources, extras, refs = refs[:count], refs[count:count + passed], refs[count + passed:]
    out_ref, extra_outs = refs[0], refs[1:1 + passed]
    staged, wide, sems = refs[1 + passed:-2], refs[-2], refs[-1]
    copies = [
        pltpu.make_async_copy(source, stage, sems.at[index])
        for index, (source, stage) in enumerate(zip(sources, staged))
    ]
    for copy in copies:
        copy.start()
    for extra, extra_out in zip(extras, extra_outs):
        extra_out[...] = extra[...]
    slot = 0
    for copy, stage, heads in zip(copies, staged, per_owner):
        copy.wait()
        tokens, total, width = stage.shape
        wide[...] = stage[...].astype(F32).reshape(tokens * total, width)
        for head in range(total):
            out_ref[head // heads, slot + head % heads] = wide[
                pl.ds(head, tokens, stride=total), :
            ].astype(BF16)
        slot += heads


def pack(owners, sources, *extras):
    tokens, total, width = sources[0].shape
    per_owner = [source.shape[1] // owners for source in sources]
    size = sum(source.size for source in sources)
    return pl.pallas_call(
        functools.partial(pack_body, per_owner, len(extras)),
        out_shape=[
            jax.ShapeDtypeStruct((owners, sum(per_owner), tokens, width), BF16),
        ] + [jax.ShapeDtypeStruct(extra.shape, extra.dtype) for extra in extras],
        in_specs=[pl.BlockSpec(memory_space=pltpu.HBM)] * len(sources) + [VMEM] * len(extras),
        out_specs=[VMEM] * (1 + len(extras)),
        scratch_shapes=[pltpu.VMEM(source.shape, BF16) for source in sources] + [
            pltpu.VMEM((tokens * total, width), F32),
            pltpu.SemaphoreType.DMA((len(sources),)),
        ],
        compiler_params=pltpu.CompilerParams(vmem_limit_bytes=VMEM_BYTES),
        cost_estimate=pl.CostEstimate(flops=size, bytes_accessed=4 * size, transcendentals=0),
    )(*[pltpu.with_memory_space_constraint(source, pltpu.HBM) for source in sources], *extras)


def unpack_queries_body(in_ref, out_ref, wide):
    owners = in_ref.shape[0]
    tokens, total, width = out_ref.shape
    heads = total // owners
    for head in range(total):
        first = (head % heads) * tokens
        wide[pl.ds(head, tokens, stride=total), :] = (
            in_ref[head // heads, first:first + tokens, :].astype(F32)
        )
    out_ref[...] = wide[...].reshape(tokens, total, width).astype(BF16)


def unpack_queries(received, tokens):
    owners, rows, width = received.shape
    heads = owners * (rows // tokens)
    return call(
        unpack_queries_body,
        jax.ShapeDtypeStruct((tokens, heads, width), BF16),
        [pltpu.VMEM((tokens * heads, width), F32)],
        received.size, 4 * received.size, 0, received,
    )


def unpack_gains_body(in_ref, gain_ref):
    owners, rows, _ = in_ref.shape
    pieces = in_ref[0, rows - TAIL_ROWS:, :].astype(F32)
    for owner in range(1, owners):
        pieces = pieces + in_ref[owner, rows - TAIL_ROWS:, :].astype(F32)
    for row in range(2):
        gain_ref[row:row + 1, :] = jnp.sum(pieces[3 * row:3 * row + 3], axis=0, keepdims=True)


def unpack_gains(received):
    width = received.shape[-1]
    return call(
        unpack_gains_body,
        jax.ShapeDtypeStruct((2, width), F32),
        [], 64 * width, 64 * width, 0, received,
    )


def unpack_keys_body(in_ref, key_out, value_out, wide):
    tokens, owners, width = key_out.shape
    for slot, out_ref in enumerate((key_out, value_out)):
        for head in range(owners):
            wide[slot, pl.ds(head, tokens, stride=owners), :] = in_ref[head, slot].astype(F32)
        out_ref[...] = wide[slot].reshape(tokens, owners, width).astype(BF16)


def unpack_keys(received):
    owners, _, tokens, width = received.shape
    shape = (tokens, owners, width)
    return call(
        unpack_keys_body,
        [jax.ShapeDtypeStruct(shape, BF16)] * 2,
        [pltpu.VMEM((2, tokens * owners, width), F32)],
        received.size, 4 * received.size, 0, received,
    )


def unit_and_inverse(raw):
    widened = raw.astype(F32)
    inverse = lax.rsqrt(jnp.mean(widened * widened, axis=-1, keepdims=True) + epsilon)
    return widened * inverse, inverse


def normalize_back(normed_grad, unit_rows, inverse, gain_values):
    scaled = normed_grad * gain_values
    return inverse * (scaled - unit_rows * jnp.mean(scaled * unit_rows, axis=-1, keepdims=True))


def contract_last(left, right):
    return lax.dot_general(left, right, (((1,), (1,)), ((), ())), preferred_element_type=F32)


def matmul(left, right):
    return lax.dot_general(left, right, (((1,), (0,)), ((), ())), preferred_element_type=F32)


def fold_rows(tile, combine):
    return combine(tile.reshape(tile.shape[0] // 8, 8, tile.shape[1]), axis=0)


def three_pieces(value):
    high = value.astype(BF16)
    rest = value - high.astype(F32)
    middle = rest.astype(BF16)
    return [high, middle, (rest - middle.astype(F32)).astype(BF16)]


def attend_body(
    qd_ref, own_ref, prev_ref, doc_ref, both_gains_ref,
    qgrad_ref, dk_own_ref, dv_own_ref, back_ref,
    key_rows, value_rows, key_cols, value_cols, key_docs,
    score_buf, power_buf, grad_buf, dk_acc, dv_acc, gain_acc, back_buf, back_sem,
):
    blocks, _, rows, width = qd_ref.shape
    tiles = blocks + 1
    window = tiles * rows
    query_gain = both_gains_ref[0:1, :]
    key_gain = both_gains_ref[1:2, :]
    for block in range(2 * blocks):
        source = prev_ref if block < blocks else own_ref
        span = slice(block * rows, (block + 1) * rows)
        unit, _ = unit_and_inverse(source[block % blocks, 0])
        normed = (unit * key_gain).astype(BF16)
        values = source[block % blocks, 1]
        key_rows[span, :] = normed
        value_rows[span, :] = values
        key_cols[:, span] = normed.T
        value_cols[:, span] = values.T
        key_docs[span, :] = jnp.broadcast_to(doc_ref[:, span], (rows, rows)).T
    dk_acc[...] = jnp.zeros_like(dk_acc)
    dv_acc[...] = jnp.zeros_like(dv_acc)
    gain_acc[...] = jnp.zeros_like(gain_acc)

    back_copy = pltpu.make_async_copy(back_buf, back_ref, back_sem)
    key_index = lax.broadcasted_iota(jnp.int32, (rows, rows), 0)
    query_index = lax.broadcasted_iota(jnp.int32, (rows, rows), 1)
    CHUNK = 1

    def powers_of(block):
        slot = block % 2
        query_unit, query_inverse = unit_and_inverse(qd_ref[block, 0:2].reshape(2 * rows, width))
        query = (query_unit * query_gain).astype(BF16)
        query_docs = doc_ref[:, (block + blocks) * rows:(block + blocks + 1) * rows]
        peak = jnp.full((8, 2 * rows), masked_score, F32)
        for first in range(0, tiles, CHUNK):
            lead = (block + first) * rows
            raw = contract_last(key_rows[lead:lead + CHUNK * rows, :], query)
            for tile in range(first, first + CHUNK):
                span = slice((block + tile) * rows, (block + tile + 1) * rows)
                allowed = key_docs[span, :] == query_docs
                if tile == 0:
                    allowed = allowed & (key_index > query_index)
                if tile == tiles - 1:
                    allowed = allowed & (key_index <= query_index)
                scores = raw[(tile - first) * rows:(tile - first + 1) * rows]
                scores = jnp.concatenate(
                    [
                        jnp.where(allowed, scores[:, :rows], masked_score),
                        jnp.where(allowed, scores[:, rows:], masked_score),
                    ],
                    axis=1,
                )
                score_buf[slot, tile * rows:(tile + 1) * rows, :] = scores
                peak = jnp.maximum(peak, fold_rows(scores, jnp.max))
        peak = jnp.max(peak, axis=0, keepdims=True) * exponent_scale
        total = jnp.zeros((8, 2 * rows), F32)
        for tile in range(tiles):
            local = slice(tile * rows, (tile + 1) * rows)
            powers = jnp.exp2(score_buf[slot, local, :] * exponent_scale - peak)
            power_buf[slot, local, :] = powers.astype(BF16)
            total = total + fold_rows(powers, jnp.sum)
        return query_unit, query_inverse, query, 1.0 / jnp.sum(total, axis=0, keepdims=True)

    def gradients_of(block, query_unit, query_inverse, query, inverse_total):
        slot = block % 2
        reach = slice(block * rows, block * rows + window)
        out_grad = qd_ref[block, 2:4].reshape(2 * rows, width)
        out_cols = matmul(value_cols[:, reach], power_buf[slot]) * inverse_total
        out_grad_cols = jnp.concatenate(
            [out_grad[:rows].T, out_grad[rows:].T], axis=1
        ).astype(F32) * inverse_total
        row_dots = jnp.sum(
            out_grad_cols * out_cols.astype(BF16).astype(F32), axis=0, keepdims=True
        )
        scaled_cols = out_grad_cols.astype(BF16)
        scaled_rows = jnp.concatenate([scaled_cols[:, :rows].T, scaled_cols[:, rows:].T], axis=0)
        for first in range(0, tiles, CHUNK):
            local = slice(first * rows, (first + CHUNK) * rows)
            span = slice((block + first) * rows, (block + first + CHUNK) * rows)
            prob_grad = matmul(value_rows[span, :], scaled_cols)
            grad_buf[slot, local, :] = (
                power_buf[slot, local, :].astype(F32) * (prob_grad - row_dots)
            ).astype(BF16)
        dv_acc[reach, :] += matmul(power_buf[slot], scaled_rows)
        dk_acc[reach, :] += matmul(grad_buf[slot], query)
        query_cols = matmul(key_cols[:, reach], grad_buf[slot])
        normed_grad = (
            jnp.concatenate([query_cols[:, :rows].T, query_cols[:, rows:].T], axis=0) * score_scale
        )
        gain_acc[0:8, :] += fold_rows(normed_grad * query_unit, jnp.sum)
        query_grad = normalize_back(normed_grad, query_unit, query_inverse, query_gain)
        qgrad_ref[block, 0:2 * rows, :] = query_grad.astype(BF16)

    ready = powers_of(0)
    for block in range(blocks):
        upcoming = powers_of(block + 1) if block + 1 < blocks else None
        gradients_of(block, *ready)
        ready = upcoming

    for block in range(2 * blocks):
        source = prev_ref if block < blocks else own_ref
        span = slice(block * rows, (block + 1) * rows)
        unit, _ = unit_and_inverse(source[block % blocks, 0])
        key_part = dk_acc[span, :] * score_scale
        gain_acc[8:16, :] += fold_rows(key_part * unit, jnp.sum)
        if block < blocks:
            back_buf[block, 0] = key_part.astype(BF16)
            back_buf[block, 1] = dv_acc[span, :].astype(BF16)
            if block == blocks - 1:
                back_copy.start()
        else:
            dk_own_ref[block - blocks] = key_part
            dv_own_ref[block - blocks] = dv_acc[span, :]
    back_copy.wait()
    tail = []
    for first in (0, 8):
        tail += three_pieces(jnp.sum(gain_acc[first:first + 8, :], axis=0, keepdims=True))
    tail = jnp.concatenate(
        [piece.astype(F32) for piece in tail] + [jnp.zeros((10, width), F32)], axis=0
    ).astype(BF16)
    for block in range(blocks):
        qgrad_ref[block, 2 * rows:, :] = tail


def attend(queries, own, prev, docs, gains):
    blocks, _, rows, width = own.shape
    window = (blocks + 1) * rows
    tile_flops = 2 * window * 2 * rows * width
    return call(
        attend_body,
        [
            jax.ShapeDtypeStruct((blocks, 2 * rows + TAIL_ROWS, width), BF16),
            jax.ShapeDtypeStruct((blocks, rows, width), F32),
            jax.ShapeDtypeStruct((blocks, rows, width), F32),
            pltpu.HBM((blocks, 2, rows, width), BF16),
        ],
        [
            pltpu.VMEM((2 * blocks * rows, width), BF16),
            pltpu.VMEM((2 * blocks * rows, width), BF16),
            pltpu.VMEM((width, 2 * blocks * rows), BF16),
            pltpu.VMEM((width, 2 * blocks * rows), BF16),
            pltpu.VMEM((2 * blocks * rows, rows), jnp.int32),
            pltpu.VMEM((2, window, 2 * rows), F32),
            pltpu.VMEM((2, window, 2 * rows), BF16),
            pltpu.VMEM((2, window, 2 * rows), BF16),
            pltpu.VMEM((2 * blocks * rows, width), F32),
            pltpu.VMEM((2 * blocks * rows, width), F32),
            pltpu.VMEM((16, width), F32),
            pltpu.VMEM((blocks, 2, rows, width), BF16),
            pltpu.SemaphoreType.DMA,
        ],
        6 * blocks * tile_flops,
        32 * own.size,
        blocks * window * 2 * rows,
        queries, own, prev, docs, gains,
        vmem_bytes=20 << 20,
    )


def finish_keys_body(own_ref, dk_ref, dv_ref, back_ref, gains_ref, out_ref):
    key_gain = gains_ref[1:2, :]
    for block in range(own_ref.shape[0]):
        unit, inverse = unit_and_inverse(own_ref[block, 0])
        key_total = dk_ref[block] + back_ref[block, 0].astype(F32)
        value_total = dv_ref[block] + back_ref[block, 1].astype(F32)
        out_ref[block, 0] = normalize_back(key_total, unit, inverse, key_gain).astype(BF16)
        out_ref[block, 1] = value_total.astype(BF16)


def finish_keys(own, dk_own, dv_own, back, gains):
    return call(
        finish_keys_body,
        jax.ShapeDtypeStruct(own.shape, BF16),
        [], 10 * own.size, 8 * own.size, 0,
        own, dk_own, dv_own, back, gains,
    )


def shifted_terms(value, axis):
    count = lax.axis_size(axis)
    return [
        lax.ppermute(value, axis, [(i, (i + step) % count) for i in range(count)])
        for step in range(1, count)
    ]


def add_terms(value, terms):
    for term in terms:
        value = value + term
    return value


def shifted_sum(value, axis):
    return add_terms(value, shifted_terms(value, axis))


def per_device(ring_axes, query_raw, key_raw, value_matrix, query_gain, key_gain, doc_ids, output_gradient):
    ring_size = lax.axis_size("z")
    rings = lax.axis_size(ring_axes)
    rows = query_raw.shape[0]
    span = ring_size * rows
    forward = [(ring, ring + 1) for ring in range(rings - 1)]
    backward = [(ring + 1, ring) for ring in range(rings - 1)]

    def exchange(value):
        return lax.all_to_all(value, "z", 0, 0, tiled=True)

    doc_padded = jnp.concatenate([jnp.full((span,), -1, jnp.int32), doc_ids])
    docs = lax.dynamic_slice_in_dim(
        doc_padded, lax.axis_index(ring_axes) * span, 2 * span, 0
    ).reshape(1, 2 * span)
    (sent_keys,) = pack(ring_size, (key_raw, value_matrix))
    own = exchange(sent_keys)
    prev = lax.ppermute(own, ring_axes, forward)
    sent_queries, gains = pack(
        ring_size, (query_raw, output_gradient), jnp.stack([query_gain, key_gain])
    )
    queries = exchange(sent_queries)
    query_back, dk_own, dv_own, back = attend(queries, own, prev, docs, gains)
    got_back = lax.ppermute(back, ring_axes, backward)
    got_queries = exchange(query_back)
    query_grad = unpack_queries(got_queries, rows)
    gain_sum = shifted_sum(unpack_gains(got_queries), "kv")
    got_back, gain_sum = lax.optimization_barrier((got_back, gain_sum))
    got_keys = exchange(finish_keys(own, dk_own, dv_own, got_back, gains))
    gain_sum = shifted_sum(gain_sum, "y")
    key_grad, value_grad = unpack_keys(got_keys)
    terms = shifted_terms(gain_sum, "x")
    key_grad, terms = lax.optimization_barrier((key_grad, terms))
    gain_sum = add_terms(gain_sum, terms) / doc_ids.shape[0]
    return query_grad, key_grad, value_grad, gain_sum[0], gain_sum[1]


def solution(mesh):
    ring_size = LOOKBACK_SPAN // 128
    grid = Mesh(mesh.devices.reshape(4, 4, ring_size, 2), ("x", "y", "z", "kv"))
    split = P(("x", "y", "z"), "kv", None)
    return jax.shard_map(
        functools.partial(per_device, ("x", "y")),
        mesh=grid,
        in_specs=(split, split, split, P(), P(), P(), split),
        out_specs=(split, split, split, P(), P()),
        check_vma=False,
    )
```

time: 160 us -> 122 us (0.76)
  blocking collectives: 44.1 us -> 0 us
  waiting for transfers between devices: 50.2 us -> 62 us
  Pallas kernels: 27.3 us -> 19.9 us
  starting transfers between devices: 30.9 us -> 37 us
  local copies, waits for them, and re-layouts: 5.75 us -> 1.19 us
    psum x4 -> x0, blocking collectives: 44.1 us -> none  [per_device(): gain_sum = lax.psum(gain_sum, axis)]
    all_to_all x4, waiting for transfers between devices: 24.6 us -> 42.5 us  [exchange(): return lax.all_to_all(value, 'z', 0, 0, tiled=True)]
    pallas_call x6 -> x5, Pallas kernels: 27.3 us -> 15 us  [call(): pl.pallas_call(body, out_shape=out_shape, in_specs=[VMEM] * len(args), ou...]
    ppermute x1, waiting for transfers between devices: 11.3 us -> 0.01 us  [per_device(): got_back = lax.ppermute(back, ring_axes, backward)]
    ppermute x0 -> x7, starting transfers between devices: none -> 9.41 us  [shifted_terms(): lax.ppermute(value, axis, [(i, (i + step) % count) for i in range(count)])]
    ppermute x0 -> x7, waiting for transfers between devices: none -> 5.25 us  [shifted_terms(): lax.ppermute(value, axis, [(i, (i + step) % count) for i in range(count)])]
    pallas_call x0 -> x2, Pallas kernels: none -> 4.81 us  [pack(): pl.pallas_call(functools.partial(pack_body, per_owner, len(extras)), out_...]
    unnamed x22 -> x6, local copies, waits for them, and re-layouts: 5.21 us -> 0.66 us
  transfers between devices with their start and end apart: 6 -> 13, of which waited for: 5 -> 8; matrix products, arithmetic and copies ran while one was open for 0% -> 0% of each run, Pallas kernels for 4% -> 4%
where the time goes in v2:
time: 122 us; the launch traced here: 121 us
  waiting for transfers between devices  62 us (51%)
  starting transfers between devices  37 us (30%)
  Pallas kernels  19.9 us (16%)
    all_to_all x4, waiting for transfers between devices, exchange(): return lax.all_to_all(value, 'z', 0, 0, tiled=True)  42.5 us
    all_to_all x4, starting transfers between devices, exchange(): return lax.all_to_all(value, 'z', 0, 0, tiled=True)  19.2 us
    pallas_call x5, Pallas kernels, call(): pl.pallas_call(body, out_shape=out_shape, in_specs=[VMEM] * len(args), ou...  15 us
    ppermute x1, waiting for transfers between devices, per_device(): prev = lax.ppermute(own, ring_axes, forward)  14.3 us
    ppermute x7, starting transfers between devices, shifted_terms(): lax.ppermute(value, axis, [(i, (i + step) % count) for i in range(count)])  9.41 us
    ppermute x7, waiting for transfers between devices, shifted_terms(): lax.ppermute(value, axis, [(i, (i + step) % count) for i in range(count)])  5.25 us
    ppermute x1, starting transfers between devices, per_device(): got_back = lax.ppermute(back, ring_axes, backward)  4.89 us
    pallas_call x2, Pallas kernels, pack(): pl.pallas_call(functools.partial(pack_body, per_owner, len(extras)), out_...  4.81 us
  transfers between devices with their start and end apart: 13, of which 8 were waited for; matrix products, arithmetic and copies ran while one was open for 0% of the time, Pallas kernels for 4%

profile of v2, /device:TPU:2, one launch (start us, length us, event | category | flops | bytes accessed | tf_op | source)
XLA Modules:
  0.0 120.9 jit_solution(9067883637028094256)
XLA Ops:
  0.6 2.0 %shard_map.111 = bf16[8,2,128,128]{3,2,1,0:T(8,128)(2,1)} custom-call(bf16[128,8,128]{2,1,0:T(8,128)(2,1)} %refs_0_.3, bf16[128,8,128]{2,1,0:T(8,128)(2,1)} %refs_1_.3), custom_call_target="tpu_custom_call" | custom-call | flops 262144 | bytes 1048576 | tf_op jit(solution)/shard_map/pallas_call | solution.py:66
  2.6 8.5 %all-to-all-start.1 = ((bf16[8,2,128,128]{3,2,1,0:T(8,128)(2,1)}), bf16[8,2,128,128]{3,2,1,0:T(8,128)(2,1)S(1)}, u32[]{:S(2)}, u32[]{:S(2)}) async-start(bf16[8,2,128,128]{3,2,1,0:T(8,128)(2,1)} %shard_map.111), calls=%async_computation.1 | async-start | bytes 1048576 | tf_op jit(solution)/shard_map/all_to_all | solution.py:380
  11.1 0.0 copy-start.1
  11.1 0.0 copy-start.2
  11.1 0.6 copy-done.1
  11.8 0.0 copy-done.2
  11.8 2.8 %shard_map.110 = (bf16[8,4,128,128]{3,2,1,0:T(8,128)(2,1)}, f32[2,128]{1,0:T(2,128)S(1)}) custom-call(bf16[128,16,128]{2,1,0:T(8,128)(2,1)} %refs_0_.2, bf16[128,16,128]{2,1,0:T(8,128)(2,1)} %refs_1_.2, f32[2,128]{1,0:T(2,128)S(1)} %pad_maximum_fusion.refs_2_), custom_call_target="tpu_custom_call" | custom-call | flops 524288 | bytes 2097152 | tf_op jit(solution)/shard_map/pallas_call | solution.py:66
  14.6 14.0 %all-to-all-done.1.own_ref = bf16[8,2,128,128]{3,2,1,0:T(8,128)(2,1)S(1)} async-done(((bf16[8,2,128,128]{3,2,1,0:T(8,128)(2,1)}), bf16[8,2,128,128]{3,2,1,0:T(8,128)(2,1)S(1)}, u32[]{:S(2)}, u32[]{:S(2)}) %all-to-all-start.1) | async-done | bytes 524320 | tf_op jit(solution)/shard_map/all_to_all | solution.py:380
  28.6 0.0 copy-start
  28.6 3.7 %all-to-all-start = ((bf16[8,4,128,128]{3,2,1,0:T(8,128)(2,1)}), bf16[8,4,128,128]{3,2,1,0:T(8,128)(2,1)S(1)}, u32[]{:S(2)}, u32[]{:S(2)}) async-start(bf16[8,4,128,128]{3,2,1,0:T(8,128)(2,1)} %get-tuple-element.19), calls=%async_computation | async-start | bytes 2097152 | tf_op jit(solution)/shard_map/all_to_all | solution.py:380
  32.3 3.5 %collective-permute-start = (bf16[8,2,128,128]{3,2,1,0:T(8,128)(2,1)S(1)}, bf16[8,2,128,128]{3,2,1,0:T(8,128)(2,1)S(1)}, u32[]{:S(2)}, u32[]{:S(2)}) collective-permute-start(bf16[8,2,128,128]{3,2,1,0:T(8,128)(2,1)S(1)} %all-to-all-done.1.own_ref), channel_id=1, source_target_pairs={{0,16},{16,32},{32,48},{48,64},{64,80},{80,96},{96,112},{112,128},... | collective-permute-start | bytes 1572872 | tf_op jit(solution)/shard_map/ppermute | solution.py:388
  35.8 0.0 copy-done
  35.8 14.3 %collective-permute-done.prev_ref = bf16[8,2,128,128]{3,2,1,0:T(8,128)(2,1)S(1)} collective-permute-done((bf16[8,2,128,128]{3,2,1,0:T(8,128)(2,1)S(1)}, bf16[8,2,128,128]{3,2,1,0:T(8,128)(2,1)S(1)}, u32[]{:S(2)}, u32[]{:S(2)}) %collective-permute-start) | collective-permute-done | bytes 524320 | tf_op jit(solution)/shard_map/ppermute | solution.py:388
  50.2 11.3 %all-to-all-done.qd_ref = bf16[8,4,128,128]{3,2,1,0:T(8,128)(2,1)S(1)} async-done(((bf16[8,4,128,128]{3,2,1,0:T(8,128)(2,1)}), bf16[8,4,128,128]{3,2,1,0:T(8,128)(2,1)S(1)}, u32[]{:S(2)}, u32[]{:S(2)}) %all-to-all-start) | async-done | bytes 1048608 | tf_op jit(solution)/shard_map/all_to_all | solution.py:380
  61.5 11.2 %shard_map.112 = (bf16[8,272,128]{2,1,0:T(8,128)(2,1)}, f32[8,128,128]{2,1,0:T(8,128)S(1)}, f32[8,128,128]{2,1,0:T(8,128)S(1)}, bf16[8,2,128,128]{3,2,1,0:T(8,128)(2,1)}) custom-call(bf16[8,4,128,128]{3,2,1,0:T(8,128)(2,1)S(1)} %all-to-all-done.qd_ref, bf16[8,2,128,128]{3,2,1,0:T(8,128)(2,1)S(1)} %all-to-all-done.1.own_ref, ...), custom_call_target="tpu_custom_call" | custom-call | flops 3623878656 | bytes 8388608 | tf_op jit(solution)/shard_map/pallas_call | solution.py:23
  72.7 3.5 %all-to-all-start.2 = ((bf16[8,272,128]{2,1,0:T(8,128)(2,1)}), bf16[8,272,128]{2,1,0:T(8,128)(2,1)S(1)}, u32[]{:S(2)}, u32[]{:S(2)}) async-start(bf16[8,272,128]{2,1,0:T(8,128)(2,1)} %get-tuple-element.21), calls=%async_computation.2 | async-start | bytes 1114112 | tf_op jit(solution)/shard_map/all_to_all | solution.py:380
  76.2 4.9 %collective-permute-start.1 = (bf16[8,2,128,128]{3,2,1,0:T(8,128)(2,1)}, bf16[8,2,128,128]{3,2,1,0:T(8,128)(2,1)S(1)}, u32[]{:S(2)}, u32[]{:S(2)}) collective-permute-start(bf16[8,2,128,128]{3,2,1,0:T(8,128)(2,1)} %get-tuple-element.24), channel_id=1, source_target_pairs={{16,0},{32,16},{48,32},{64,48},{80,64},{96,80},{112,96},{128,112},... | collective-permute-start | bytes 1572872 | tf_op jit(solution)/shard_map/ppermute | solution.py:394
  81.1 13.7 %all-to-all-done.2.in_ref = bf16[8,272,128]{2,1,0:T(8,128)(2,1)S(1)} async-done(((bf16[8,272,128]{2,1,0:T(8,128)(2,1)}), bf16[8,272,128]{2,1,0:T(8,128)(2,1)S(1)}, u32[]{:S(2)}, u32[]{:S(2)}) %all-to-all-start.2) | async-done | bytes 557088 | tf_op jit(solution)/shard_map/all_to_all | solution.py:380
  94.9 0.3 collective-permute-start.2
  95.2 1.1 collective-permute-done.2
  96.3 0.0 collective-permute-done.1.back_ref
  96.3 1.4 %shard_map.115 = bf16[8,2,128,128]{3,2,1,0:T(8,128)(2,1)} custom-call(bf16[8,2,128,128]{3,2,1,0:T(8,128)(2,1)S(1)} %all-to-all-done.1.own_ref, f32[8,128,128]{2,1,0:T(8,128)S(1)} %get-tuple-element.22.dk_ref, f32[8,128,128]{2,1,0:T(8,128)S(1)} %get-tuple-element.23.dv_ref, bf16[8,2,128,128]{3,2,1,0:T(8,128)(2,1)S(1)} %collective-permute-done.1.back_ref, ...), custom_call_target="tpu_custom_call" | custom-call | flops 2621440 | bytes 2097152 | tf_op jit(solution)/shard_map/pallas_call | solution.py:23
  97.7 3.5 %all-to-all-start.3 = ((bf16[8,2,128,128]{3,2,1,0:T(8,128)(2,1)}), bf16[8,2,128,128]{3,2,1,0:T(8,128)(2,1)S(1)}, u32[]{:S(2)}, u32[]{:S(2)}) async-start(bf16[8,2,128,128]{3,2,1,0:T(8,128)(2,1)} %shard_map.115), calls=%async_computation.3 | async-start | bytes 1048576 | tf_op jit(solution)/shard_map/all_to_all | solution.py:380
  101.2 4.4 %collective-permute-start.5 = (f32[2,128]{1,0:T(2,128)S(1)}, f32[2,128]{1,0:T(2,128)S(1)}, u32[]{:S(2)}, u32[]{:S(2)}) collective-permute-start(f32[2,128]{1,0:T(2,128)S(1)} %add.31), channel_id=1, source_target_pairs={{0,48},{16,0},{32,16},{48,32},{1,49},{17,1},{33,17},{49,33},{2,50}... | collective-permute-start | bytes 3080 | tf_op jit(solution)/shard_map/ppermute | solution.py:356
  105.5 0.0 collective-permute-start.4
  105.5 0.9 collective-permute-start.3
  106.5 0.3 collective-permute-done.5
  106.8 3.8 %collective-permute-done.4 = f32[2,128]{1,0:T(2,128)S(1)} collective-permute-done((f32[2,128]{1,0:T(2,128)S(1)}, f32[2,128]{1,0:T(2,128)S(1)}, u32[]{:S(2)}, u32[]{:S(2)}) %collective-permute-start.4) | collective-permute-done | bytes 1056 | tf_op jit(solution)/shard_map/ppermute | solution.py:356
  110.6 0.0 collective-permute-done.3
  110.6 0.6 collective-permute-start.8
  111.2 2.4 %collective-permute-start.7 = (f32[2,128]{1,0:T(2,128)S(1)}, f32[2,128]{1,0:T(2,128)S(1)}, u32[]{:S(2)}, u32[]{:S(2)}) collective-permute-start(f32[2,128]{1,0:T(2,128)S(1)} %add_add_fusion), channel_id=1, source_target_pairs={{0,128},{64,192},{128,0},{192,64},{1,129},{65,193},{129,1},{193,65... | collective-permute-start | bytes 3080 | tf_op jit(solution)/shard_map/ppermute | solution.py:356
  113.6 0.8 collective-permute-start.6
  114.4 1.4 %shard_map.113 = bf16[128,16,128]{2,1,0:T(8,128)(2,1)} custom-call(bf16[8,272,128]{2,1,0:T(8,128)(2,1)S(1)} %all-to-all-done.2.in_ref), custom_call_target="tpu_custom_call" | custom-call | flops 278528 | bytes 1114112 | tf_op jit(solution)/shard_map/pallas_call | solution.py:23
  115.8 3.5 %all-to-all-done.3.in_ref = bf16[8,2,128,128]{3,2,1,0:T(8,128)(2,1)S(1)} async-done(((bf16[8,2,128,128]{3,2,1,0:T(8,128)(2,1)}), bf16[8,2,128,128]{3,2,1,0:T(8,128)(2,1)S(1)}, u32[]{:S(2)}, u32[]{:S(2)}) %all-to-all-start.3) | async-done | bytes 524320 | tf_op jit(solution)/shard_map/all_to_all | solution.py:380
  119.2 1.1 shard_map.116
  120.3 0.0 collective-permute-done.8
  120.3 0.0 collective-permute-done.7
  120.3 0.0 collective-permute-done.6
  120.3 0.5 slice_bitcast_fusion
  (6 shorter events, 0.1 us)
Async XLA Ops:
  2.6 26.0 %all-to-all-start.1 = ((bf16[8,2,128,128]{3,2,1,0:T(8,128)(2,1)}), bf16[8,2,128,128]{3,2,1,0:T(8,128)(2,1)S(1)}, u32[]{:S(2)}, u32[]{:S(2)}) async-start(bf16[8,2,128,128]{3,2,1,0:T(8,128)(2,1)} %shard_map.111), calls=%async_computation.1 | async-start | bytes 1048576 | tf_op jit(solution)/shard_map/all_to_all | solution.py:380
  11.1 0.7 copy-start.1
  11.1 0.7 copy-start.2
  28.6 7.2 %copy-start = (s32[16384]{0:T(1024)S(1)}, s32[16384]{0:T(1024)}, u32[]{:S(2)}) copy-start(s32[16384]{0:T(1024)} %param.12) | copy-start | bytes 196612
  28.6 32.8 %all-to-all-start = ((bf16[8,4,128,128]{3,2,1,0:T(8,128)(2,1)}), bf16[8,4,128,128]{3,2,1,0:T(8,128)(2,1)S(1)}, u32[]{:S(2)}, u32[]{:S(2)}) async-start(bf16[8,4,128,128]{3,2,1,0:T(8,128)(2,1)} %get-tuple-element.19), calls=%async_computation | async-start | bytes 2097152 | tf_op jit(solution)/shard_map/all_to_all | solution.py:380
  32.3 17.8 %collective-permute-start = (bf16[8,2,128,128]{3,2,1,0:T(8,128)(2,1)S(1)}, bf16[8,2,128,128]{3,2,1,0:T(8,128)(2,1)S(1)}, u32[]{:S(2)}, u32[]{:S(2)}) collective-permute-start(bf16[8,2,128,128]{3,2,1,0:T(8,128)(2,1)S(1)} %all-to-all-done.1.own_ref), channel_id=1, source_target_pairs={{0,16},{16,32},{32,48},{48,64},{64,80},{80,96},{96,112},{112,128},... | collective-permute-start | bytes 1572872 | tf_op jit(solution)/shard_map/ppermute | solution.py:388
  72.7 22.2 %all-to-all-start.2 = ((bf16[8,272,128]{2,1,0:T(8,128)(2,1)}), bf16[8,272,128]{2,1,0:T(8,128)(2,1)S(1)}, u32[]{:S(2)}, u32[]{:S(2)}) async-start(bf16[8,272,128]{2,1,0:T(8,128)(2,1)} %get-tuple-element.21), calls=%async_computation.2 | async-start | bytes 1114112 | tf_op jit(solution)/shard_map/all_to_all | solution.py:380
  76.2 20.1 %collective-permute-start.1 = (bf16[8,2,128,128]{3,2,1,0:T(8,128)(2,1)}, bf16[8,2,128,128]{3,2,1,0:T(8,128)(2,1)S(1)}, u32[]{:S(2)}, u32[]{:S(2)}) collective-permute-start(bf16[8,2,128,128]{3,2,1,0:T(8,128)(2,1)} %get-tuple-element.24), channel_id=1, source_target_pairs={{16,0},{32,16},{48,32},{64,48},{80,64},{96,80},{112,96},{128,112},... | collective-permute-start | bytes 1572872 | tf_op jit(solution)/shard_map/ppermute | solution.py:394
  94.9 1.4 %collective-permute-start.2 = (f32[2,128]{1,0:T(2,128)S(1)}, f32[2,128]{1,0:T(2,128)S(1)}, u32[]{:S(2)}, u32[]{:S(2)}) collective-permute-start(f32[2,128]{1,0:T(2,128)S(1)} %shard_map.114), channel_id=1, source_target_pairs={{0,1},{1,0},{2,3},{3,2},{4,5},{5,4},{6,7},{7,6},{8,9},{9,8},{10,11... | collective-permute-start | bytes 3080 | tf_op jit(solution)/shard_map/ppermute | solution.py:356
  97.7 21.6 %all-to-all-start.3 = ((bf16[8,2,128,128]{3,2,1,0:T(8,128)(2,1)}), bf16[8,2,128,128]{3,2,1,0:T(8,128)(2,1)S(1)}, u32[]{:S(2)}, u32[]{:S(2)}) async-start(bf16[8,2,128,128]{3,2,1,0:T(8,128)(2,1)} %shard_map.115), calls=%async_computation.3 | async-start | bytes 1048576 | tf_op jit(solution)/shard_map/all_to_all | solution.py:380
  101.2 5.7 %collective-permute-start.5 = (f32[2,128]{1,0:T(2,128)S(1)}, f32[2,128]{1,0:T(2,128)S(1)}, u32[]{:S(2)}, u32[]{:S(2)}) collective-permute-start(f32[2,128]{1,0:T(2,128)S(1)} %add.31), channel_id=1, source_target_pairs={{0,48},{16,0},{32,16},{48,32},{1,49},{17,1},{33,17},{49,33},{2,50}... | collective-permute-start | bytes 3080 | tf_op jit(solution)/shard_map/ppermute | solution.py:356
  105.5 5.1 %collective-permute-start.4 = (f32[2,128]{1,0:T(2,128)S(1)}, f32[2,128]{1,0:T(2,128)S(1)}, u32[]{:S(2)}, u32[]{:S(2)}) collective-permute-start(f32[2,128]{1,0:T(2,128)S(1)} %add.31), channel_id=1, source_target_pairs={{0,32},{16,48},{32,0},{48,16},{1,33},{17,49},{33,1},{49,17},{2,34}... | collective-permute-start | bytes 3080 | tf_op jit(solution)/shard_map/ppermute | solution.py:356
  105.5 5.1 %collective-permute-start.3 = (f32[2,128]{1,0:T(2,128)S(1)}, f32[2,128]{1,0:T(2,128)S(1)}, u32[]{:S(2)}, u32[]{:S(2)}) collective-permute-start(f32[2,128]{1,0:T(2,128)S(1)} %add.31), channel_id=1, source_target_pairs={{0,16},{16,32},{32,48},{48,0},{1,17},{17,33},{33,49},{49,1},{2,18}... | collective-permute-start | bytes 3080 | tf_op jit(solution)/shard_map/ppermute | solution.py:356
  110.6 9.7 %collective-permute-start.8 = (f32[2,128]{1,0:T(2,128)S(1)}, f32[2,128]{1,0:T(2,128)S(1)}, u32[]{:S(2)}, u32[]{:S(2)}) collective-permute-start(f32[2,128]{1,0:T(2,128)S(1)} %add_add_fusion), channel_id=1, source_target_pairs={{0,192},{64,0},{128,64},{192,128},{1,193},{65,1},{129,65},{193,129... | collective-permute-start | bytes 3080 | tf_op jit(solution)/shard_map/ppermute | solution.py:356
  111.2 9.1 %collective-permute-start.7 = (f32[2,128]{1,0:T(2,128)S(1)}, f32[2,128]{1,0:T(2,128)S(1)}, u32[]{:S(2)}, u32[]{:S(2)}) collective-permute-start(f32[2,128]{1,0:T(2,128)S(1)} %add_add_fusion), channel_id=1, source_target_pairs={{0,128},{64,192},{128,0},{192,64},{1,129},{65,193},{129,1},{193,65... | collective-permute-start | bytes 3080 | tf_op jit(solution)/shard_map/ppermute | solution.py:356
  113.6 6.7 %collective-permute-start.6 = (f32[2,128]{1,0:T(2,128)S(1)}, f32[2,128]{1,0:T(2,128)S(1)}, u32[]{:S(2)}, u32[]{:S(2)}) collective-permute-start(f32[2,128]{1,0:T(2,128)S(1)} %add_add_fusion), channel_id=1, source_target_pairs={{0,64},{64,128},{128,192},{192,0},{1,65},{65,129},{129,193},{193,1... | collective-permute-start | bytes 3080 | tf_op jit(solution)/shard_map/ppermute | solution.py:356

commit v3 on v2

--- a/solution.py
+++ b/solution.py
@@ -15,6 +15,7 @@
 BF16 = jnp.bfloat16
 TAIL_ROWS = 16
 VMEM_BYTES = 8 << 20
+SMEM = pl.BlockSpec(memory_space=pltpu.SMEM)
 HBM = pl.BlockSpec(memory_space=pltpu.HBM)
 VMEM = pl.BlockSpec(memory_space=pltpu.VMEM)
 
@@ -77,6 +78,66 @@
         compiler_params=pltpu.CompilerParams(vmem_limit_bytes=VMEM_BYTES),
         cost_estimate=pl.CostEstimate(flops=size, bytes_accessed=4 * size, transcendentals=0),
     )(*[pltpu.with_memory_space_constraint(source, pltpu.HBM) for source in sources], *extras)
+
+
+def pack_apart_body(place_ref, key_ref, value_ref, *refs):
+    outs, staged, wide, sems = refs[:-4], refs[-4:-2], refs[-2], refs[-1]
+    copies = [
+        pltpu.make_async_copy(source, stage, sems.at[index])
+        for index, (source, stage) in enumerate(zip((key_ref, value_ref), staged))
+    ]
+    for copy in copies:
+        copy.start()
+    owners = len(outs)
+    for slot, (copy, stage) in enumerate(zip(copies, staged)):
+        copy.wait()
+        tokens, total, width = stage.shape
+        wide[...] = stage[...].astype(F32).reshape(tokens * total, width)
+        for step, out_ref in enumerate(outs):
+            head = (place_ref[0] + step) % owners
+            out_ref[slot] = wide[pl.ds(head, tokens, stride=total), :].astype(BF16)
+
+
+def pack_apart(place, keys, values):
+    tokens, heads, width = keys.shape
+    return pl.pallas_call(
+        pack_apart_body,
+        out_shape=[jax.ShapeDtypeStruct((2, tokens, width), BF16)] * heads,
+        in_specs=[SMEM, HBM, HBM],
+        out_specs=[VMEM] * heads,
+        scratch_shapes=[pltpu.VMEM(keys.shape, BF16)] * 2 + [
+            pltpu.VMEM((tokens * heads, width), F32),
+            pltpu.SemaphoreType.DMA((2,)),
+        ],
+        compiler_params=pltpu.CompilerParams(vmem_limit_bytes=VMEM_BYTES),
+        cost_estimate=pl.CostEstimate(
+            flops=2 * keys.size, bytes_accessed=8 * keys.size, transcendentals=0
+        ),
+    )(
+        place,
+        pltpu.with_memory_space_constraint(keys, pltpu.HBM),
+        pltpu.with_memory_space_constraint(values, pltpu.HBM),
+    )
+
+
+def gather_pieces_body(place_ref, *refs):
+    pieces, out_ref = refs[:-1], refs[-1]
+    owners = len(pieces)
+    for step, piece in enumerate(pieces):
+        out_ref[(place_ref[0] + owners - step) % owners] = piece[...]
+
+
+def gather_pieces(place, pieces):
+    shape = (len(pieces),) + pieces[0].shape
+    size = len(pieces) * pieces[0].size
+    return pl.pallas_call(
+        gather_pieces_body,
+        out_shape=jax.ShapeDtypeStruct(shape, BF16),
+        in_specs=[SMEM] + [VMEM] * len(pieces),
+        out_specs=VMEM,
+        compiler_params=pltpu.CompilerParams(vmem_limit_bytes=VMEM_BYTES),
+        cost_estimate=pl.CostEstimate(flops=size, bytes_accessed=4 * size, transcendentals=0),
+    )(place, *pieces)
 
 
 def unpack_queries_body(in_ref, out_ref, wide):
@@ -243,10 +304,10 @@
         out_grad_cols = jnp.concatenate(
             [out_grad[:rows].T, out_grad[rows:].T], axis=1
         ).astype(F32) * inverse_total
+        scaled_cols = out_grad_cols.astype(BF16)
         row_dots = jnp.sum(
-            out_grad_cols * out_cols.astype(BF16).astype(F32), axis=0, keepdims=True
+            scaled_cols.astype(F32) * out_cols.astype(BF16).astype(F32), axis=0, keepdims=True
         )
-        scaled_cols = out_grad_cols.astype(BF16)
         scaled_rows = jnp.concatenate([scaled_cols[:, :rows].T, scaled_cols[:, rows:].T], axis=0)
         for first in range(0, tiles, CHUNK):
             local = slice(first * rows, (first + CHUNK) * rows)
@@ -379,16 +440,26 @@
     def exchange(value):
         return lax.all_to_all(value, "z", 0, 0, tiled=True)
 
+    def exchange_apart(pieces):
+        return [
+            lax.ppermute(piece, "z", [(i, (i + step) % ring_size) for i in range(ring_size)])
+            if step else piece
+            for step, piece in enumerate(pieces)
+        ]
+
     doc_padded = jnp.concatenate([jnp.full((span,), -1, jnp.int32), doc_ids])
     docs = lax.dynamic_slice_in_dim(
         doc_padded, lax.axis_index(ring_axes) * span, 2 * span, 0
     ).reshape(1, 2 * span)
-    (sent_keys,) = pack(ring_size, (key_raw, value_matrix))
-    own = exchange(sent_keys)
-    prev = lax.ppermute(own, ring_axes, forward)
+    place = lax.axis_index("z").astype(jnp.int32).reshape(1)
+    pieces = pack_apart(place, key_raw, value_matrix)
+    pieces = exchange_apart(pieces)
     sent_queries, gains = pack(
         ring_size, (query_raw, output_gradient), jnp.stack([query_gain, key_gain])
     )
+    pieces, sent_queries = lax.optimization_barrier((pieces, sent_queries))
+    own = gather_pieces(place, pieces)
+    prev = lax.ppermute(own, ring_axes, forward)
     queries = exchange(sent_queries)
     query_back, dk_own, dv_own, back = attend(queries, own, prev, docs, gains)
     got_back = lax.ppermute(back, ring_axes, backward)

time: 122 us -> 120 us (0.984)
  waiting for transfers between devices: 62 us -> 49 us
  starting transfers between devices: 37 us -> 47.9 us
    ppermute x0 -> x7, starting transfers between devices: none -> 18.5 us  [exchange_apart(): lax.ppermute(piece, 'z', [(i, (i + step) % ring_size) for i in range(ring...]
    all_to_all x4 -> x3, waiting for transfers between devices: 42.5 us -> 28.4 us  [exchange(): return lax.all_to_all(value, 'z', 0, 0, tiled=True)]
    all_to_all x4 -> x3, starting transfers between devices: 19.2 us -> 11.4 us  [exchange(): return lax.all_to_all(value, 'z', 0, 0, tiled=True)]
    ppermute x0 -> x7, waiting for transfers between devices: none -> 2.19 us  [exchange_apart(): lax.ppermute(piece, 'z', [(i, (i + step) % ring_size) for i in range(ring...]
    pallas_call x2 -> x1, Pallas kernels: 4.81 us -> 2.82 us  [pack(): pl.pallas_call(functools.partial(pack_body, per_owner, len(extras)), out_...]
    pallas_call x0 -> x2, Pallas kernels: none -> 1.36 us  [the longest x1 1.32 us: pack_apart(): pl.pallas_call(pack_apart_body, out_shape=[jax.ShapeDtypeStruct((2, token...]
  transfers between devices with their start and end apart: 13 -> 19, of which waited for: 8 -> 9; matrix products, arithmetic and copies ran while one was open for 0% -> 0% of each run, Pallas kernels for 4% -> 4%
where the time goes in v3:
time: 120 us; the launch traced here: 118 us
  waiting for transfers between devices  49 us (41%)
  starting transfers between devices  47.9 us (40%)
  Pallas kernels  19.2 us (16%)
  local copies, waits for them, and re-layouts  1.2 us (1%)
    all_to_all x3, waiting for transfers between devices, exchange(): return lax.all_to_all(value, 'z', 0, 0, tiled=True)  28.4 us
    ppermute x7, starting transfers between devices, exchange_apart(): lax.ppermute(piece, 'z', [(i, (i + step) % ring_size) for i in range(ring...  18.5 us
    pallas_call x5, Pallas kernels, call(): pl.pallas_call(body, out_shape=out_shape, in_specs=[VMEM] * len(args), ou...  15 us
    ppermute x1, waiting for transfers between devices, per_device(): prev = lax.ppermute(own, ring_axes, forward)  13.4 us
    all_to_all x3, starting transfers between devices, exchange(): return lax.all_to_all(value, 'z', 0, 0, tiled=True)  11.4 us
    ppermute x7, starting transfers between devices, shifted_terms(): lax.ppermute(value, axis, [(i, (i + step) % count) for i in range(count)])  9.43 us
    ppermute x7, waiting for transfers between devices, shifted_terms(): lax.ppermute(value, axis, [(i, (i + step) % count) for i in range(count)])  5.03 us
    ppermute x1, starting transfers between devices, per_device(): got_back = lax.ppermute(back, ring_axes, backward)  4.89 us
  transfers between devices with their start and end apart: 19, of which 9 were waited for; matrix products, arithmetic and copies ran while one was open for 0% of the time, Pallas kernels for 4%

profile of v3, /device:TPU:2, one launch (start us, length us, event | category | flops | bytes accessed | tf_op | source)
XLA Modules:
  0.0 118.1 jit_solution(7530597602549546043)
XLA Ops:
  0.6 1.3 %shard_map.110 = (bf16[2,128,128]{2,1,0:T(8,128)(2,1)S(1)}, bf16[2,128,128]{2,1,0:T(8,128)(2,1)S(1)}, bf16[2,128,128]{2,1,0:T(8,128)(2,1)S(1)}, bf16[2,128,128]{...) custom-call(s32[1]{0:T(128)} %bitcast.place_ref, ...), custom_call_target="tpu_custom_call" | custom-call | flops 262144 | bytes 1048576 | tf_op jit(solution)/shard_map/pallas_call | solution.py:103
  2.0 2.0 %collective-permute-start = (bf16[2,128,128]{2,1,0:T(8,128)(2,1)S(1)}, bf16[2,128,128]{2,1,0:T(8,128)(2,1)S(1)}, u32[]{:S(2)}, u32[]{:S(2)}) collective-permute-start(bf16[2,128,128]{2,1,0:T(8,128)(2,1)S(1)} %get-tuple-element.37), channel_id=1, source_target_pairs={{0,2},{2,4},{4,6},{6,8},{8,10},{10,12},{12,14},{14,0},{1,3},{3,5},... | collective-permute-start | bytes 196616 | tf_op jit(solution)/shard_map/ppermute | solution.py:445
  4.0 3.3 %collective-permute-start.1 = (bf16[2,128,128]{2,1,0:T(8,128)(2,1)S(1)}, bf16[2,128,128]{2,1,0:T(8,128)(2,1)S(1)}, u32[]{:S(2)}, u32[]{:S(2)}) collective-permute-start(bf16[2,128,128]{2,1,0:T(8,128)(2,1)S(1)} %get-tuple-element.38), channel_id=1, source_target_pairs={{0,4},{2,6},{4,8},{6,10},{8,12},{10,14},{12,0},{14,2},{1,5},{3,7},... | collective-permute-start | bytes 196616 | tf_op jit(solution)/shard_map/ppermute | solution.py:445
  7.2 4.0 %collective-permute-start.2 = (bf16[2,128,128]{2,1,0:T(8,128)(2,1)S(1)}, bf16[2,128,128]{2,1,0:T(8,128)(2,1)S(1)}, u32[]{:S(2)}, u32[]{:S(2)}) collective-permute-start(bf16[2,128,128]{2,1,0:T(8,128)(2,1)S(1)} %get-tuple-element.39), channel_id=1, source_target_pairs={{0,6},{2,8},{4,10},{6,12},{8,14},{10,0},{12,2},{14,4},{1,7},{3,9},... | collective-permute-start | bytes 196616 | tf_op jit(solution)/shard_map/ppermute | solution.py:445
  11.3 0.5 collective-permute-start.3
  11.8 4.9 %collective-permute-start.4 = (bf16[2,128,128]{2,1,0:T(8,128)(2,1)S(1)}, bf16[2,128,128]{2,1,0:T(8,128)(2,1)S(1)}, u32[]{:S(2)}, u32[]{:S(2)}) collective-permute-start(bf16[2,128,128]{2,1,0:T(8,128)(2,1)S(1)} %get-tuple-element.41), channel_id=1, source_target_pairs={{0,10},{2,12},{4,14},{6,0},{8,2},{10,4},{12,6},{14,8},{1,11},{3,13... | collective-permute-start | bytes 196616 | tf_op jit(solution)/shard_map/ppermute | solution.py:445
  16.8 0.0 collective-permute-done.refs_1_
  16.8 2.7 %collective-permute-start.5 = (bf16[2,128,128]{2,1,0:T(8,128)(2,1)S(1)}, bf16[2,128,128]{2,1,0:T(8,128)(2,1)S(1)}, u32[]{:S(2)}, u32[]{:S(2)}) collective-permute-start(bf16[2,128,128]{2,1,0:T(8,128)(2,1)S(1)} %get-tuple-element.42), channel_id=1, source_target_pairs={{0,12},{2,14},{4,0},{6,2},{8,4},{10,6},{12,8},{14,10},{1,13},{3,15... | collective-permute-start | bytes 196616 | tf_op jit(solution)/shard_map/ppermute | solution.py:445
  19.4 0.0 collective-permute-done.1.refs_2_
  19.4 1.0 collective-permute-start.6
  20.4 0.0 copy-start.1
  20.4 0.0 copy-start.2
  20.4 0.7 copy-done.1
  21.1 0.0 copy-done.2
  21.1 2.8 %shard_map.111 = (bf16[8,4,128,128]{3,2,1,0:T(8,128)(2,1)}, f32[2,128]{1,0:T(2,128)S(1)}) custom-call(bf16[128,16,128]{2,1,0:T(8,128)(2,1)} %refs_0_.1, bf16[128,16,128]{2,1,0:T(8,128)(2,1)} %refs_1_.1, f32[2,128]{1,0:T(2,128)S(1)} %pad_maximum_fusion.refs_2_), custom_call_target="tpu_custom_call" | custom-call | flops 524288 | bytes 2097152 | tf_op jit(solution)/shard_map/pallas_call | solution.py:67
  23.9 0.0 collective-permute-done.2.refs_3_
  23.9 0.0 collective-permute-done.3.refs_4_
  24.0 1.8 %collective-permute-done.4.refs_5_ = bf16[2,128,128]{2,1,0:T(8,128)(2,1)S(1)} collective-permute-done((bf16[2,128,128]{2,1,0:T(8,128)(2,1)S(1)}, bf16[2,128,128]{2,1,0:T(8,128)(2,1)S(1)}, u32[]{:S(2)}, u32[]{:S(2)}) %collective-permute-start.4) | collective-permute-done | bytes 65568 | tf_op jit(solution)/shard_map/ppermute | solution.py:445
  25.8 0.0 collective-permute-done.5.refs_6_
  25.8 0.4 collective-permute-done.6.refs_7_
  26.1 4.3 %all-to-all-start = ((bf16[8,4,128,128]{3,2,1,0:T(8,128)(2,1)}), bf16[8,4,128,128]{3,2,1,0:T(8,128)(2,1)S(1)}, u32[]{:S(2)}, u32[]{:S(2)}) async-start(bf16[8,4,128,128]{3,2,1,0:T(8,128)(2,1)} %get-tuple-element.45), calls=%async_computation | async-start | bytes 2097152 | tf_op jit(solution)/shard_map/all_to_all | solution.py:441
  30.5 0.0 copy-start
  30.5 3.7 %collective-permute-start.7 = (bf16[8,2,128,128]{3,2,1,0:T(8,128)(2,1)S(1)}, bf16[8,2,128,128]{3,2,1,0:T(8,128)(2,1)S(1)}, u32[]{:S(2)}, u32[]{:S(2)}) collective-permute-start(bf16[8,2,128,128]{3,2,1,0:T(8,128)(2,1)S(1)} %shard_map.112.own_ref), channel_id=1, source_target_pairs={{0,16},{16,32},{32,48},{48,64},{64,80},{80,96},{96,112},{112,128},... | collective-permute-start | bytes 1572872 | tf_op jit(solution)/shard_map/ppermute | solution.py:462
  34.2 0.0 copy-done
  34.2 13.4 %collective-permute-done.7.prev_ref = bf16[8,2,128,128]{3,2,1,0:T(8,128)(2,1)S(1)} collective-permute-done((bf16[8,2,128,128]{3,2,1,0:T(8,128)(2,1)S(1)}, bf16[8,2,128,128]{3,2,1,0:T(8,128)(2,1)S(1)}, u32[]{:S(2)}, u32[]{:S(2)}) %collective-permute-start.7) | collective-permute-done | bytes 524320 | tf_op jit(solution)/shard_map/ppermute | solution.py:462
  47.6 11.3 %all-to-all-done.qd_ref = bf16[8,4,128,128]{3,2,1,0:T(8,128)(2,1)S(1)} async-done(((bf16[8,4,128,128]{3,2,1,0:T(8,128)(2,1)}), bf16[8,4,128,128]{3,2,1,0:T(8,128)(2,1)S(1)}, u32[]{:S(2)}, u32[]{:S(2)}) %all-to-all-start) | async-done | bytes 1048608 | tf_op jit(solution)/shard_map/all_to_all | solution.py:441
  58.9 11.2 %shard_map.113 = (bf16[8,272,128]{2,1,0:T(8,128)(2,1)}, f32[8,128,128]{2,1,0:T(8,128)S(1)}, f32[8,128,128]{2,1,0:T(8,128)S(1)}, bf16[8,2,128,128]{3,2,1,0:T(8,128)(2,1)}) custom-call(bf16[8,4,128,128]{3,2,1,0:T(8,128)(2,1)S(1)} %all-to-all-done.qd_ref, bf16[8,2,128,128]{3,2,1,0:T(8,128)(2,1)S(1)} %shard_map.112.own_ref, ...), custom_call_target="tpu_custom_call" | custom-call | flops 3623878656 | bytes 8388608 | tf_op jit(solution)/shard_map/pallas_call | solution.py:24
  70.1 3.5 %all-to-all-start.1 = ((bf16[8,272,128]{2,1,0:T(8,128)(2,1)}), bf16[8,272,128]{2,1,0:T(8,128)(2,1)S(1)}, u32[]{:S(2)}, u32[]{:S(2)}) async-start(bf16[8,272,128]{2,1,0:T(8,128)(2,1)} %get-tuple-element.55), calls=%async_computation.1 | async-start | bytes 1114112 | tf_op jit(solution)/shard_map/all_to_all | solution.py:441
  73.6 4.9 %collective-permute-start.8 = (bf16[8,2,128,128]{3,2,1,0:T(8,128)(2,1)}, bf16[8,2,128,128]{3,2,1,0:T(8,128)(2,1)S(1)}, u32[]{:S(2)}, u32[]{:S(2)}) collective-permute-start(bf16[8,2,128,128]{3,2,1,0:T(8,128)(2,1)} %get-tuple-element.58), channel_id=1, source_target_pairs={{16,0},{32,16},{48,32},{64,48},{80,64},{96,80},{112,96},{128,112},... | collective-permute-start | bytes 1572872 | tf_op jit(solution)/shard_map/ppermute | solution.py:465
  78.5 13.7 %all-to-all-done.1.in_ref = bf16[8,272,128]{2,1,0:T(8,128)(2,1)S(1)} async-done(((bf16[8,272,128]{2,1,0:T(8,128)(2,1)}), bf16[8,272,128]{2,1,0:T(8,128)(2,1)S(1)}, u32[]{:S(2)}, u32[]{:S(2)}) %all-to-all-start.1) | async-done | bytes 557088 | tf_op jit(solution)/shard_map/all_to_all | solution.py:441
  92.3 0.1 collective-permute-start.9
  92.4 1.1 collective-permute-done.9
  93.5 0.0 collective-permute-done.8.back_ref
  93.5 1.4 %shard_map.116 = bf16[8,2,128,128]{3,2,1,0:T(8,128)(2,1)} custom-call(bf16[8,2,128,128]{3,2,1,0:T(8,128)(2,1)S(1)} %shard_map.112.own_ref, f32[8,128,128]{2,1,0:T(8,128)S(1)} %get-tuple-element.56.dk_ref, f32[8,128,128]{2,1,0:T(8,128)S(1)} %get-tuple-element.57.dv_ref, bf16[8,2,128,128]{3,2,1,0:T(8,128)(2,1)S(1)} %collective-permute-done.8.back_ref, ...), custom_call_target="tpu_custom_call" | custom-call | flops 2621440 | bytes 2097152 | tf_op jit(solution)/shard_map/pallas_call | solution.py:24
  94.9 3.5 %all-to-all-start.2 = ((bf16[8,2,128,128]{3,2,1,0:T(8,128)(2,1)}), bf16[8,2,128,128]{3,2,1,0:T(8,128)(2,1)S(1)}, u32[]{:S(2)}, u32[]{:S(2)}) async-start(bf16[8,2,128,128]{3,2,1,0:T(8,128)(2,1)} %shard_map.116), calls=%async_computation.2 | async-start | bytes 1048576 | tf_op jit(solution)/shard_map/all_to_all | solution.py:441
  98.4 4.5 %collective-permute-start.12 = (f32[2,128]{1,0:T(2,128)S(1)}, f32[2,128]{1,0:T(2,128)S(1)}, u32[]{:S(2)}, u32[]{:S(2)}) collective-permute-start(f32[2,128]{1,0:T(2,128)S(1)} %add.31), channel_id=1, source_target_pairs={{0,48},{16,0},{32,16},{48,32},{1,49},{17,1},{33,17},{49,33},{2,50}... | collective-permute-start | bytes 3080 | tf_op jit(solution)/shard_map/ppermute | solution.py:417
  102.9 0.0 collective-permute-start.11
  102.9 1.2 collective-permute-start.10
  104.1 0.1 collective-permute-done.12
  104.2 3.8 %collective-permute-done.11 = f32[2,128]{1,0:T(2,128)S(1)} collective-permute-done((f32[2,128]{1,0:T(2,128)S(1)}, f32[2,128]{1,0:T(2,128)S(1)}, u32[]{:S(2)}, u32[]{:S(2)}) %collective-permute-start.11) | collective-permute-done | bytes 1056 | tf_op jit(solution)/shard_map/ppermute | solution.py:417
  108.0 0.0 collective-permute-done.10
  108.0 0.6 collective-permute-start.15
  108.6 2.4 %collective-permute-start.14 = (f32[2,128]{1,0:T(2,128)S(1)}, f32[2,128]{1,0:T(2,128)S(1)}, u32[]{:S(2)}, u32[]{:S(2)}) collective-permute-start(f32[2,128]{1,0:T(2,128)S(1)} %add_add_fusion), channel_id=1, source_target_pairs={{0,128},{64,192},{128,0},{192,64},{1,129},{65,193},{129,1},{193,65... | collective-permute-start | bytes 3080 | tf_op jit(solution)/shard_map/ppermute | solution.py:417
  111.0 0.6 collective-permute-start.13
  111.6 1.4 %shard_map.114 = bf16[128,16,128]{2,1,0:T(8,128)(2,1)} custom-call(bf16[8,272,128]{2,1,0:T(8,128)(2,1)S(1)} %all-to-all-done.1.in_ref), custom_call_target="tpu_custom_call" | custom-call | flops 278528 | bytes 1114112 | tf_op jit(solution)/shard_map/pallas_call | solution.py:24
  113.0 3.4 %all-to-all-done.2.in_ref = bf16[8,2,128,128]{3,2,1,0:T(8,128)(2,1)S(1)} async-done(((bf16[8,2,128,128]{3,2,1,0:T(8,128)(2,1)}), bf16[8,2,128,128]{3,2,1,0:T(8,128)(2,1)S(1)}, u32[]{:S(2)}, u32[]{:S(2)}) %all-to-all-start.2) | async-done | bytes 524320 | tf_op jit(solution)/shard_map/all_to_all | solution.py:441
  116.4 1.1 shard_map.117
  117.5 0.0 collective-permute-done.15
  117.5 0.0 collective-permute-done.14
  117.5 0.0 collective-permute-done.13
  117.5 0.5 slice_bitcast_fusion
  (7 shorter events, 0.1 us)
Async XLA Ops:
  2.0 14.8 %collective-permute-start = (bf16[2,128,128]{2,1,0:T(8,128)(2,1)S(1)}, bf16[2,128,128]{2,1,0:T(8,128)(2,1)S(1)}, u32[]{:S(2)}, u32[]{:S(2)}) collective-permute-start(bf16[2,128,128]{2,1,0:T(8,128)(2,1)S(1)} %get-tuple-element.37), channel_id=1, source_target_pairs={{0,2},{2,4},{4,6},{6,8},{8,10},{10,12},{12,14},{14,0},{1,3},{3,5},... | collective-permute-start | bytes 196616 | tf_op jit(solution)/shard_map/ppermute | solution.py:445
  4.0 15.5 %collective-permute-start.1 = (bf16[2,128,128]{2,1,0:T(8,128)(2,1)S(1)}, bf16[2,128,128]{2,1,0:T(8,128)(2,1)S(1)}, u32[]{:S(2)}, u32[]{:S(2)}) collective-permute-start(bf16[2,128,128]{2,1,0:T(8,128)(2,1)S(1)} %get-tuple-element.38), channel_id=1, source_target_pairs={{0,4},{2,6},{4,8},{6,10},{8,12},{10,14},{12,0},{14,2},{1,5},{3,7},... | collective-permute-start | bytes 196616 | tf_op jit(solution)/shard_map/ppermute | solution.py:445
  7.2 16.7 %collective-permute-start.2 = (bf16[2,128,128]{2,1,0:T(8,128)(2,1)S(1)}, bf16[2,128,128]{2,1,0:T(8,128)(2,1)S(1)}, u32[]{:S(2)}, u32[]{:S(2)}) collective-permute-start(bf16[2,128,128]{2,1,0:T(8,128)(2,1)S(1)} %get-tuple-element.39), channel_id=1, source_target_pairs={{0,6},{2,8},{4,10},{6,12},{8,14},{10,0},{12,2},{14,4},{1,7},{3,9},... | collective-permute-start | bytes 196616 | tf_op jit(solution)/shard_map/ppermute | solution.py:445
  11.3 12.7 %collective-permute-start.3 = (bf16[2,128,128]{2,1,0:T(8,128)(2,1)S(1)}, bf16[2,128,128]{2,1,0:T(8,128)(2,1)S(1)}, u32[]{:S(2)}, u32[]{:S(2)}) collective-permute-start(bf16[2,128,128]{2,1,0:T(8,128)(2,1)S(1)} %get-tuple-element.40), channel_id=1, source_target_pairs={{0,8},{2,10},{4,12},{6,14},{8,0},{10,2},{12,4},{14,6},{1,9},{3,11}... | collective-permute-start | bytes 196616 | tf_op jit(solution)/shard_map/ppermute | solution.py:445
  11.8 13.9 %collective-permute-start.4 = (bf16[2,128,128]{2,1,0:T(8,128)(2,1)S(1)}, bf16[2,128,128]{2,1,0:T(8,128)(2,1)S(1)}, u32[]{:S(2)}, u32[]{:S(2)}) collective-permute-start(bf16[2,128,128]{2,1,0:T(8,128)(2,1)S(1)} %get-tuple-element.41), channel_id=1, source_target_pairs={{0,10},{2,12},{4,14},{6,0},{8,2},{10,4},{12,6},{14,8},{1,11},{3,13... | collective-permute-start | bytes 196616 | tf_op jit(solution)/shard_map/ppermute | solution.py:445
  16.8 9.0 %collective-permute-start.5 = (bf16[2,128,128]{2,1,0:T(8,128)(2,1)S(1)}, bf16[2,128,128]{2,1,0:T(8,128)(2,1)S(1)}, u32[]{:S(2)}, u32[]{:S(2)}) collective-permute-start(bf16[2,128,128]{2,1,0:T(8,128)(2,1)S(1)} %get-tuple-element.42), channel_id=1, source_target_pairs={{0,12},{2,14},{4,0},{6,2},{8,4},{10,6},{12,8},{14,10},{1,13},{3,15... | collective-permute-start | bytes 196616 | tf_op jit(solution)/shard_map/ppermute | solution.py:445
  19.4 6.7 %collective-permute-start.6 = (bf16[2,128,128]{2,1,0:T(8,128)(2,1)S(1)}, bf16[2,128,128]{2,1,0:T(8,128)(2,1)S(1)}, u32[]{:S(2)}, u32[]{:S(2)}) collective-permute-start(bf16[2,128,128]{2,1,0:T(8,128)(2,1)S(1)} %get-tuple-element.43), channel_id=1, source_target_pairs={{0,14},{2,0},{4,2},{6,4},{8,6},{10,8},{12,10},{14,12},{1,15},{3,1}... | collective-permute-start | bytes 196616 | tf_op jit(solution)/shard_map/ppermute | solution.py:445
  20.4 0.7 copy-start.1
  20.4 0.7 copy-start.2
  26.1 32.7 %all-to-all-start = ((bf16[8,4,128,128]{3,2,1,0:T(8,128)(2,1)}), bf16[8,4,128,128]{3,2,1,0:T(8,128)(2,1)S(1)}, u32[]{:S(2)}, u32[]{:S(2)}) async-start(bf16[8,4,128,128]{3,2,1,0:T(8,128)(2,1)} %get-tuple-element.45), calls=%async_computation | async-start | bytes 2097152 | tf_op jit(solution)/shard_map/all_to_all | solution.py:441
  30.5 3.7 %copy-start = (s32[16384]{0:T(1024)S(1)}, s32[16384]{0:T(1024)}, u32[]{:S(2)}) copy-start(s32[16384]{0:T(1024)} %param.12) | copy-start | bytes 196612
  30.5 17.1 %collective-permute-start.7 = (bf16[8,2,128,128]{3,2,1,0:T(8,128)(2,1)S(1)}, bf16[8,2,128,128]{3,2,1,0:T(8,128)(2,1)S(1)}, u32[]{:S(2)}, u32[]{:S(2)}) collective-permute-start(bf16[8,2,128,128]{3,2,1,0:T(8,128)(2,1)S(1)} %shard_map.112.own_ref), channel_id=1, source_target_pairs={{0,16},{16,32},{32,48},{48,64},{64,80},{80,96},{96,112},{112,128},... | collective-permute-start | bytes 1572872 | tf_op jit(solution)/shard_map/ppermute | solution.py:462
  70.1 22.2 %all-to-all-start.1 = ((bf16[8,272,128]{2,1,0:T(8,128)(2,1)}), bf16[8,272,128]{2,1,0:T(8,128)(2,1)S(1)}, u32[]{:S(2)}, u32[]{:S(2)}) async-start(bf16[8,272,128]{2,1,0:T(8,128)(2,1)} %get-tuple-element.55), calls=%async_computation.1 | async-start | bytes 1114112 | tf_op jit(solution)/shard_map/all_to_all | solution.py:441
  73.6 19.9 %collective-permute-start.8 = (bf16[8,2,128,128]{3,2,1,0:T(8,128)(2,1)}, bf16[8,2,128,128]{3,2,1,0:T(8,128)(2,1)S(1)}, u32[]{:S(2)}, u32[]{:S(2)}) collective-permute-start(bf16[8,2,128,128]{3,2,1,0:T(8,128)(2,1)} %get-tuple-element.58), channel_id=1, source_target_pairs={{16,0},{32,16},{48,32},{64,48},{80,64},{96,80},{112,96},{128,112},... | collective-permute-start | bytes 1572872 | tf_op jit(solution)/shard_map/ppermute | solution.py:465
  92.3 1.2 %collective-permute-start.9 = (f32[2,128]{1,0:T(2,128)S(1)}, f32[2,128]{1,0:T(2,128)S(1)}, u32[]{:S(2)}, u32[]{:S(2)}) collective-permute-start(f32[2,128]{1,0:T(2,128)S(1)} %shard_map.115), channel_id=1, source_target_pairs={{0,1},{1,0},{2,3},{3,2},{4,5},{5,4},{6,7},{7,6},{8,9},{9,8},{10,11... | collective-permute-start | bytes 3080 | tf_op jit(solution)/shard_map/ppermute | solution.py:417
  94.9 21.6 %all-to-all-start.2 = ((bf16[8,2,128,128]{3,2,1,0:T(8,128)(2,1)}), bf16[8,2,128,128]{3,2,1,0:T(8,128)(2,1)S(1)}, u32[]{:S(2)}, u32[]{:S(2)}) async-start(bf16[8,2,128,128]{3,2,1,0:T(8,128)(2,1)} %shard_map.116), calls=%async_computation.2 | async-start | bytes 1048576 | tf_op jit(solution)/shard_map/all_to_all | solution.py:441
  98.4 5.8 %collective-permute-start.12 = (f32[2,128]{1,0:T(2,128)S(1)}, f32[2,128]{1,0:T(2,128)S(1)}, u32[]{:S(2)}, u32[]{:S(2)}) collective-permute-start(f32[2,128]{1,0:T(2,128)S(1)} %add.31), channel_id=1, source_target_pairs={{0,48},{16,0},{32,16},{48,32},{1,49},{17,1},{33,17},{49,33},{2,50}... | collective-permute-start | bytes 3080 | tf_op jit(solution)/shard_map/ppermute | solution.py:417
  102.9 5.1 %collective-permute-start.11 = (f32[2,128]{1,0:T(2,128)S(1)}, f32[2,128]{1,0:T(2,128)S(1)}, u32[]{:S(2)}, u32[]{:S(2)}) collective-permute-start(f32[2,128]{1,0:T(2,128)S(1)} %add.31), channel_id=1, source_target_pairs={{0,32},{16,48},{32,0},{48,16},{1,33},{17,49},{33,1},{49,17},{2,34}... | collective-permute-start | bytes 3080 | tf_op jit(solution)/shard_map/ppermute | solution.py:417
  102.9 5.1 %collective-permute-start.10 = (f32[2,128]{1,0:T(2,128)S(1)}, f32[2,128]{1,0:T(2,128)S(1)}, u32[]{:S(2)}, u32[]{:S(2)}) collective-permute-start(f32[2,128]{1,0:T(2,128)S(1)} %add.31), channel_id=1, source_target_pairs={{0,16},{16,32},{32,48},{48,0},{1,17},{17,33},{33,49},{49,1},{2,18}... | collective-permute-start | bytes 3080 | tf_op jit(solution)/shard_map/ppermute | solution.py:417
  108.0 9.5 %collective-permute-start.15 = (f32[2,128]{1,0:T(2,128)S(1)}, f32[2,128]{1,0:T(2,128)S(1)}, u32[]{:S(2)}, u32[]{:S(2)}) collective-permute-start(f32[2,128]{1,0:T(2,128)S(1)} %add_add_fusion), channel_id=1, source_target_pairs={{0,192},{64,0},{128,64},{192,128},{1,193},{65,1},{129,65},{193,129... | collective-permute-start | bytes 3080 | tf_op jit(solution)/shard_map/ppermute | solution.py:417
  108.6 8.9 %collective-permute-start.14 = (f32[2,128]{1,0:T(2,128)S(1)}, f32[2,128]{1,0:T(2,128)S(1)}, u32[]{:S(2)}, u32[]{:S(2)}) collective-permute-start(f32[2,128]{1,0:T(2,128)S(1)} %add_add_fusion), channel_id=1, source_target_pairs={{0,128},{64,192},{128,0},{192,64},{1,129},{65,193},{129,1},{193,65... | collective-permute-start | bytes 3080 | tf_op jit(solution)/shard_map/ppermute | solution.py:417
  111.0 6.5 %collective-permute-start.13 = (f32[2,128]{1,0:T(2,128)S(1)}, f32[2,128]{1,0:T(2,128)S(1)}, u32[]{:S(2)}, u32[]{:S(2)}) collective-permute-start(f32[2,128]{1,0:T(2,128)S(1)} %add_add_fusion), channel_id=1, source_target_pairs={{0,64},{64,128},{128,192},{192,0},{1,65},{65,129},{129,193},{193,1... | collective-permute-start | bytes 3080 | tf_op jit(solution)/shard_map/ppermute | solution.py:417

commit v4 on v3

--- a/solution.py
+++ b/solution.py
@@ -14,6 +14,7 @@
 F32 = jnp.float32
 BF16 = jnp.bfloat16
 TAIL_ROWS = 16
+STEP_ORDER = (1, 7, 2, 6, 3, 5, 4)
 VMEM_BYTES = 8 << 20
 SMEM = pl.BlockSpec(memory_space=pltpu.SMEM)
 HBM = pl.BlockSpec(memory_space=pltpu.HBM)
@@ -123,7 +124,7 @@
 def gather_pieces_body(place_ref, *refs):
     pieces, out_ref = refs[:-1], refs[-1]
     owners = len(pieces)
-    for step, piece in enumerate(pieces):
+    for step, piece in zip((0,) + STEP_ORDER, pieces):
         out_ref[(place_ref[0] + owners - step) % owners] = piece[...]
 
 
@@ -252,8 +253,6 @@
         key_cols[:, span] = normed.T
         value_cols[:, span] = values.T
         key_docs[span, :] = jnp.broadcast_to(doc_ref[:, span], (rows, rows)).T
-    dk_acc[...] = jnp.zeros_like(dk_acc)
-    dv_acc[...] = jnp.zeros_like(dv_acc)
     gain_acc[...] = jnp.zeros_like(gain_acc)
 
     back_copy = pltpu.make_async_copy(back_buf, back_ref, back_sem)
@@ -261,7 +260,20 @@
     query_index = lax.broadcasted_iota(jnp.int32, (rows, rows), 1)
     CHUNK = 1
 
-    def powers_of(block):
+    def accumulate(total, block, terms):
+        first, last = block * rows, block * rows + window
+        seen = last - rows if block else first
+        if block:
+            total[first:seen, :] += terms[:seen - first]
+        total[seen:last, :] = terms[seen - first:]
+
+    def finish_part(source, index, place):
+        unit, _ = unit_and_inverse(source[index, 0])
+        part = dk_acc[place * rows:(place + 1) * rows, :] * score_scale
+        gain_acc[8:16, :] += fold_rows(part * unit, jnp.sum)
+        return part
+
+    def powers_of(block, ready):
         slot = block % 2
         query_unit, query_inverse = unit_and_inverse(qd_ref[block, 0:2].reshape(2 * rows, width))
         query = (query_unit * query_gain).astype(BF16)
@@ -287,6 +299,7 @@
                 )
                 score_buf[slot, tile * rows:(tile + 1) * rows, :] = scores
                 peak = jnp.maximum(peak, fold_rows(scores, jnp.max))
+            yield
         peak = jnp.max(peak, axis=0, keepdims=True) * exponent_scale
         total = jnp.zeros((8, 2 * rows), F32)
         for tile in range(tiles):
@@ -294,7 +307,10 @@
             powers = jnp.exp2(score_buf[slot, local, :] * exponent_scale - peak)
             power_buf[slot, local, :] = powers.astype(BF16)
             total = total + fold_rows(powers, jnp.sum)
-        return query_unit, query_inverse, query, 1.0 / jnp.sum(total, axis=0, keepdims=True)
+            yield
+        ready[block] = (
+            query_unit, query_inverse, query, 1.0 / jnp.sum(total, axis=0, keepdims=True)
+        )
 
     def gradients_of(block, query_unit, query_inverse, query, inverse_total):
         slot = block % 2
@@ -305,6 +321,7 @@
             [out_grad[:rows].T, out_grad[rows:].T], axis=1
         ).astype(F32) * inverse_total
         scaled_cols = out_grad_cols.astype(BF16)
+        yield
         row_dots = jnp.sum(
             scaled_cols.astype(F32) * out_cols.astype(BF16).astype(F32), axis=0, keepdims=True
         )
@@ -316,9 +333,17 @@
             grad_buf[slot, local, :] = (
                 power_buf[slot, local, :].astype(F32) * (prob_grad - row_dots)
             ).astype(BF16)
-        dv_acc[reach, :] += matmul(power_buf[slot], scaled_rows)
-        dk_acc[reach, :] += matmul(grad_buf[slot], query)
+            yield
+        accumulate(dv_acc, block, matmul(power_buf[slot], scaled_rows))
+        yield
+        accumulate(dk_acc, block, matmul(grad_buf[slot], query))
+        yield
+        key_part = finish_part(prev_ref, block, block)
+        back_buf[block, 0] = key_part.astype(BF16)
+        back_buf[block, 1] = dv_acc[block * rows:(block + 1) * rows, :].astype(BF16)
+        yield
         query_cols = matmul(key_cols[:, reach], grad_buf[slot])
+        yield
         normed_grad = (
             jnp.concatenate([query_cols[:, :rows].T, query_cols[:, rows:].T], axis=0) * score_scale
         )
@@ -326,27 +351,20 @@
         query_grad = normalize_back(normed_grad, query_unit, query_inverse, query_gain)
         qgrad_ref[block, 0:2 * rows, :] = query_grad.astype(BF16)
 
-    ready = powers_of(0)
+    ready = {}
+    for _ in powers_of(0, ready):
+        pass
     for block in range(blocks):
-        upcoming = powers_of(block + 1) if block + 1 < blocks else None
-        gradients_of(block, *ready)
-        ready = upcoming
-
-    for block in range(2 * blocks):
-        source = prev_ref if block < blocks else own_ref
-        span = slice(block * rows, (block + 1) * rows)
-        unit, _ = unit_and_inverse(source[block % blocks, 0])
-        key_part = dk_acc[span, :] * score_scale
-        gain_acc[8:16, :] += fold_rows(key_part * unit, jnp.sum)
-        if block < blocks:
-            back_buf[block, 0] = key_part.astype(BF16)
-            back_buf[block, 1] = dv_acc[span, :].astype(BF16)
-            if block == blocks - 1:
-                back_copy.start()
-        else:
-            dk_own_ref[block - blocks] = key_part
-            dv_own_ref[block - blocks] = dv_acc[span, :]
-    back_copy.wait()
+        streams = [gradients_of(block, *ready[block])]
+        if block + 1 < blocks:
+            streams.append(powers_of(block + 1, ready))
+        while streams:
+            streams = [stream for stream in streams if next(stream, stream) is not stream]
+
+    back_copy.start()
+    for block in range(blocks):
+        dk_own_ref[block] = finish_part(own_ref, block, block + blocks)
+        dv_own_ref[block] = dv_acc[(block + blocks) * rows:(block + blocks + 1) * rows, :]
     tail = []
     for first in (0, 8):
         tail += three_pieces(jnp.sum(gain_acc[first:first + 8, :], axis=0, keepdims=True))
@@ -355,6 +373,7 @@
     ).astype(BF16)
     for block in range(blocks):
         qgrad_ref[block, 2 * rows:, :] = tail
+    back_copy.wait()
 
 
 def attend(queries, own, prev, docs, gains):
@@ -441,11 +460,12 @@
         return lax.all_to_all(value, "z", 0, 0, tiled=True)
 
     def exchange_apart(pieces):
-        return [
-            lax.ppermute(piece, "z", [(i, (i + step) % ring_size) for i in range(ring_size)])
-            if step else piece
-            for step, piece in enumerate(pieces)
-        ]
+        got = list(pieces)
+        for step in STEP_ORDER:
+            got[step] = lax.ppermute(
+                pieces[step], "z", [(i, (i + step) % ring_size) for i in range(ring_size)]
+            )
+        return got
 
     doc_padded = jnp.concatenate([jnp.full((span,), -1, jnp.int32), doc_ids])
     docs = lax.dynamic_slice_in_dim(
@@ -457,6 +477,7 @@
     sent_queries, gains = pack(
         ring_size, (query_raw, output_gradient), jnp.stack([query_gain, key_gain])
     )
+    pieces = [pieces[step] for step in (0,) + STEP_ORDER]
     pieces, sent_queries = lax.optimization_barrier((pieces, sent_queries))
     own = gather_pieces(place, pieces)
     prev = lax.ppermute(own, ring_axes, forward)

time: 120 us -> 114 us (0.950)
  waiting for transfers between devices: 49 us -> 41.4 us
  starting transfers between devices: 47.9 us -> 50.6 us
    all_to_all x3, waiting for transfers between devices: 28.4 us -> 25.1 us  [exchange(): return lax.all_to_all(value, 'z', 0, 0, tiled=True)]
    ppermute x1, waiting for transfers between devices: 13.4 us -> 10.9 us  [per_device(): prev = lax.ppermute(own, ring_axes, forward)]
    ppermute x7, waiting for transfers between devices: 2.19 us -> 0.17 us  [exchange_apart(): lax.ppermute(pieces[step], 'z', [(i, (i + step) % ring_size) for i in ran...]
    all_to_all x3, starting transfers between devices: 11.4 us -> 13.3 us  [exchange(): return lax.all_to_all(value, 'z', 0, 0, tiled=True)]
    ppermute x7, starting transfers between devices: 18.5 us -> 19.7 us  [exchange_apart(): lax.ppermute(pieces[step], 'z', [(i, (i + step) % ring_size) for i in ran...]
  transfers between devices with their start and end apart: 19 -> 19, of which waited for: 9 -> 8; matrix products, arithmetic and copies ran while one was open for 0% -> 0% of each run, Pallas kernels for 4% -> 5%
where the time goes in v4:
time: 114 us; the launch traced here: 112 us
  starting transfers between devices  50.6 us (44%)
  waiting for transfers between devices  41.4 us (36%)
  Pallas kernels  18.3 us (16%)
  local copies, waits for them, and re-layouts  1.2 us (1%)
    all_to_all x3, waiting for transfers between devices, exchange(): return lax.all_to_all(value, 'z', 0, 0, tiled=True)  25.1 us
    ppermute x7, starting transfers between devices, exchange_apart(): lax.ppermute(pieces[step], 'z', [(i, (i + step) % ring_size) for i in ran...  19.7 us
    pallas_call x5, Pallas kernels, call(): pl.pallas_call(body, out_shape=out_shape, in_specs=[VMEM] * len(args), ou...  14.1 us
    all_to_all x3, starting transfers between devices, exchange(): return lax.all_to_all(value, 'z', 0, 0, tiled=True)  13.3 us
    ppermute x1, waiting for transfers between devices, per_device(): prev = lax.ppermute(own, ring_axes, forward)  10.9 us
    ppermute x7, starting transfers between devices, shifted_terms(): lax.ppermute(value, axis, [(i, (i + step) % count) for i in range(count)])  9.16 us
    ppermute x7, waiting for transfers between devices, shifted_terms(): lax.ppermute(value, axis, [(i, (i + step) % count) for i in range(count)])  5.25 us
    ppermute x1, starting transfers between devices, per_device(): got_back = lax.ppermute(back, ring_axes, backward)  4.89 us
  transfers between devices with their start and end apart: 19, of which 8 were waited for; matrix products, arithmetic and copies ran while one was open for 0% of the time, Pallas kernels for 5%

profile of v4, /device:TPU:2, one launch (start us, length us, event | category | flops | bytes accessed | tf_op | source)
XLA Modules:
  0.0 112.3 jit_solution(788029085403286275)
XLA Ops:
  0.6 1.3 %shard_map.110 = (bf16[2,128,128]{2,1,0:T(8,128)(2,1)S(1)}, bf16[2,128,128]{2,1,0:T(8,128)(2,1)S(1)}, bf16[2,128,128]{2,1,0:T(8,128)(2,1)S(1)}, bf16[2,128,128]{...) custom-call(s32[1]{0:T(128)} %bitcast.place_ref, ...), custom_call_target="tpu_custom_call" | custom-call | flops 262144 | bytes 1048576 | tf_op jit(solution)/shard_map/pallas_call | solution.py:104
  2.0 2.0 %collective-permute-start = (bf16[2,128,128]{2,1,0:T(8,128)(2,1)S(1)}, bf16[2,128,128]{2,1,0:T(8,128)(2,1)S(1)}, u32[]{:S(2)}, u32[]{:S(2)}) collective-permute-start(bf16[2,128,128]{2,1,0:T(8,128)(2,1)S(1)} %get-tuple-element.37), channel_id=1, source_target_pairs={{0,2},{2,4},{4,6},{6,8},{8,10},{10,12},{12,14},{14,0},{1,3},{3,5},... | collective-permute-start | bytes 196616 | tf_op jit(solution)/shard_map/ppermute | solution.py:465
  4.0 4.0 %collective-permute-start.1 = (bf16[2,128,128]{2,1,0:T(8,128)(2,1)S(1)}, bf16[2,128,128]{2,1,0:T(8,128)(2,1)S(1)}, u32[]{:S(2)}, u32[]{:S(2)}) collective-permute-start(bf16[2,128,128]{2,1,0:T(8,128)(2,1)S(1)} %get-tuple-element.38), channel_id=1, source_target_pairs={{0,14},{2,0},{4,2},{6,4},{8,6},{10,8},{12,10},{14,12},{1,15},{3,1}... | collective-permute-start | bytes 196616 | tf_op jit(solution)/shard_map/ppermute | solution.py:465
  8.0 0.0 collective-permute-start.2
  8.0 4.1 %collective-permute-start.3 = (bf16[2,128,128]{2,1,0:T(8,128)(2,1)S(1)}, bf16[2,128,128]{2,1,0:T(8,128)(2,1)S(1)}, u32[]{:S(2)}, u32[]{:S(2)}) collective-permute-start(bf16[2,128,128]{2,1,0:T(8,128)(2,1)S(1)} %get-tuple-element.40), channel_id=1, source_target_pairs={{0,12},{2,14},{4,0},{6,2},{8,4},{10,6},{12,8},{14,10},{1,13},{3,15... | collective-permute-start | bytes 196616 | tf_op jit(solution)/shard_map/ppermute | solution.py:465
  12.1 0.6 collective-permute-start.4
  12.7 0.0 collective-permute-done.refs_1_
  12.7 4.4 %collective-permute-start.5 = (bf16[2,128,128]{2,1,0:T(8,128)(2,1)S(1)}, bf16[2,128,128]{2,1,0:T(8,128)(2,1)S(1)}, u32[]{:S(2)}, u32[]{:S(2)}) collective-permute-start(bf16[2,128,128]{2,1,0:T(8,128)(2,1)S(1)} %get-tuple-element.42), channel_id=1, source_target_pairs={{0,10},{2,12},{4,14},{6,0},{8,2},{10,4},{12,6},{14,8},{1,11},{3,13... | collective-permute-start | bytes 196616 | tf_op jit(solution)/shard_map/ppermute | solution.py:465
  17.2 0.0 collective-permute-done.1.refs_2_
  17.2 4.5 %collective-permute-start.6 = (bf16[2,128,128]{2,1,0:T(8,128)(2,1)S(1)}, bf16[2,128,128]{2,1,0:T(8,128)(2,1)S(1)}, u32[]{:S(2)}, u32[]{:S(2)}) collective-permute-start(bf16[2,128,128]{2,1,0:T(8,128)(2,1)S(1)} %get-tuple-element.43), channel_id=1, source_target_pairs={{0,8},{2,10},{4,12},{6,14},{8,0},{10,2},{12,4},{14,6},{1,9},{3,11}... | collective-permute-start | bytes 196616 | tf_op jit(solution)/shard_map/ppermute | solution.py:465
  21.6 0.0 copy-start.1
  21.6 0.0 copy-start.2
  21.6 0.7 copy-done.1
  22.3 0.0 copy-done.2
  22.3 2.8 %shard_map.111 = (bf16[8,4,128,128]{3,2,1,0:T(8,128)(2,1)}, f32[2,128]{1,0:T(2,128)S(1)}) custom-call(bf16[128,16,128]{2,1,0:T(8,128)(2,1)} %refs_0_.1, bf16[128,16,128]{2,1,0:T(8,128)(2,1)} %refs_1_.1, f32[2,128]{1,0:T(2,128)S(1)} %pad_maximum_fusion.refs_2_), custom_call_target="tpu_custom_call" | custom-call | flops 524288 | bytes 2097152 | tf_op jit(solution)/shard_map/pallas_call | solution.py:68
  25.1 0.0 collective-permute-done.2.refs_3_
  25.2 0.0 collective-permute-done.3.refs_4_
  25.2 0.0 collective-permute-done.4.refs_5_
  25.2 0.0 collective-permute-done.5.refs_6_
  25.2 0.2 collective-permute-done.6.refs_7_
  25.3 6.1 %all-to-all-start = ((bf16[8,4,128,128]{3,2,1,0:T(8,128)(2,1)}), bf16[8,4,128,128]{3,2,1,0:T(8,128)(2,1)S(1)}, u32[]{:S(2)}, u32[]{:S(2)}) async-start(bf16[8,4,128,128]{3,2,1,0:T(8,128)(2,1)} %get-tuple-element.45), calls=%async_computation | async-start | bytes 2097152 | tf_op jit(solution)/shard_map/all_to_all | solution.py:460
  31.5 0.0 copy-start
  31.6 3.7 %collective-permute-start.7 = (bf16[8,2,128,128]{3,2,1,0:T(8,128)(2,1)S(1)}, bf16[8,2,128,128]{3,2,1,0:T(8,128)(2,1)S(1)}, u32[]{:S(2)}, u32[]{:S(2)}) collective-permute-start(bf16[8,2,128,128]{3,2,1,0:T(8,128)(2,1)S(1)} %shard_map.112.own_ref), channel_id=1, source_target_pairs={{0,16},{16,32},{32,48},{48,64},{64,80},{80,96},{96,112},{112,128},... | collective-permute-start | bytes 1572872 | tf_op jit(solution)/shard_map/ppermute | solution.py:483
  35.2 0.0 copy-done
  35.3 10.9 %collective-permute-done.7.prev_ref = bf16[8,2,128,128]{3,2,1,0:T(8,128)(2,1)S(1)} collective-permute-done((bf16[8,2,128,128]{3,2,1,0:T(8,128)(2,1)S(1)}, bf16[8,2,128,128]{3,2,1,0:T(8,128)(2,1)S(1)}, u32[]{:S(2)}, u32[]{:S(2)}) %collective-permute-start.7) | collective-permute-done | bytes 524320 | tf_op jit(solution)/shard_map/ppermute | solution.py:483
  46.1 11.3 %all-to-all-done.qd_ref = bf16[8,4,128,128]{3,2,1,0:T(8,128)(2,1)S(1)} async-done(((bf16[8,4,128,128]{3,2,1,0:T(8,128)(2,1)}), bf16[8,4,128,128]{3,2,1,0:T(8,128)(2,1)S(1)}, u32[]{:S(2)}, u32[]{:S(2)}) %all-to-all-start) | async-done | bytes 1048608 | tf_op jit(solution)/shard_map/all_to_all | solution.py:460
  57.5 10.3 %shard_map.113 = (bf16[8,272,128]{2,1,0:T(8,128)(2,1)}, f32[8,128,128]{2,1,0:T(8,128)S(1)}, f32[8,128,128]{2,1,0:T(8,128)S(1)}, bf16[8,2,128,128]{3,2,1,0:T(8,128)(2,1)}) custom-call(bf16[8,4,128,128]{3,2,1,0:T(8,128)(2,1)S(1)} %all-to-all-done.qd_ref, bf16[8,2,128,128]{3,2,1,0:T(8,128)(2,1)S(1)} %shard_map.112.own_ref, ...), custom_call_target="tpu_custom_call" | custom-call | flops 3623878656 | bytes 8388608 | tf_op jit(solution)/shard_map/pallas_call | solution.py:25
  67.8 3.5 %all-to-all-start.1 = ((bf16[8,272,128]{2,1,0:T(8,128)(2,1)}), bf16[8,272,128]{2,1,0:T(8,128)(2,1)S(1)}, u32[]{:S(2)}, u32[]{:S(2)}) async-start(bf16[8,272,128]{2,1,0:T(8,128)(2,1)} %get-tuple-element.55), calls=%async_computation.1 | async-start | bytes 1114112 | tf_op jit(solution)/shard_map/all_to_all | solution.py:460
  71.3 4.9 %collective-permute-start.8 = (bf16[8,2,128,128]{3,2,1,0:T(8,128)(2,1)}, bf16[8,2,128,128]{3,2,1,0:T(8,128)(2,1)S(1)}, u32[]{:S(2)}, u32[]{:S(2)}) collective-permute-start(bf16[8,2,128,128]{3,2,1,0:T(8,128)(2,1)} %get-tuple-element.58), channel_id=1, source_target_pairs={{16,0},{32,16},{48,32},{64,48},{80,64},{96,80},{112,96},{128,112},... | collective-permute-start | bytes 1572872 | tf_op jit(solution)/shard_map/ppermute | solution.py:486
  76.2 10.4 %all-to-all-done.1.in_ref = bf16[8,272,128]{2,1,0:T(8,128)(2,1)S(1)} async-done(((bf16[8,272,128]{2,1,0:T(8,128)(2,1)}), bf16[8,272,128]{2,1,0:T(8,128)(2,1)S(1)}, u32[]{:S(2)}, u32[]{:S(2)}) %all-to-all-start.1) | async-done | bytes 557088 | tf_op jit(solution)/shard_map/all_to_all | solution.py:460
  86.6 0.1 collective-permute-start.9
  86.7 1.1 %collective-permute-done.9 = f32[2,128]{1,0:T(2,128)S(1)} collective-permute-done((f32[2,128]{1,0:T(2,128)S(1)}, f32[2,128]{1,0:T(2,128)S(1)}, u32[]{:S(2)}, u32[]{:S(2)}) %collective-permute-start.9) | collective-permute-done | bytes 1056 | tf_op jit(solution)/shard_map/ppermute | solution.py:436
  87.8 0.0 collective-permute-done.8.back_ref
  87.8 1.4 %shard_map.116 = bf16[8,2,128,128]{3,2,1,0:T(8,128)(2,1)} custom-call(bf16[8,2,128,128]{3,2,1,0:T(8,128)(2,1)S(1)} %shard_map.112.own_ref, f32[8,128,128]{2,1,0:T(8,128)S(1)} %get-tuple-element.56.dk_ref, f32[8,128,128]{2,1,0:T(8,128)S(1)} %get-tuple-element.57.dv_ref, bf16[8,2,128,128]{3,2,1,0:T(8,128)(2,1)S(1)} %collective-permute-done.8.back_ref, ...), custom_call_target="tpu_custom_call" | custom-call | flops 2621440 | bytes 2097152 | tf_op jit(solution)/shard_map/pallas_call | solution.py:25
  89.2 3.6 %all-to-all-start.2 = ((bf16[8,2,128,128]{3,2,1,0:T(8,128)(2,1)}), bf16[8,2,128,128]{3,2,1,0:T(8,128)(2,1)S(1)}, u32[]{:S(2)}, u32[]{:S(2)}) async-start(bf16[8,2,128,128]{3,2,1,0:T(8,128)(2,1)} %shard_map.116), calls=%async_computation.2 | async-start | bytes 1048576 | tf_op jit(solution)/shard_map/all_to_all | solution.py:460
  92.8 4.5 %collective-permute-start.12 = (f32[2,128]{1,0:T(2,128)S(1)}, f32[2,128]{1,0:T(2,128)S(1)}, u32[]{:S(2)}, u32[]{:S(2)}) collective-permute-start(f32[2,128]{1,0:T(2,128)S(1)} %add.31), channel_id=1, source_target_pairs={{0,48},{16,0},{32,16},{48,32},{1,49},{17,1},{33,17},{49,33},{2,50}... | collective-permute-start | bytes 3080 | tf_op jit(solution)/shard_map/ppermute | solution.py:436
  97.3 0.0 collective-permute-start.11
  97.3 1.0 collective-permute-start.10
  98.2 0.3 collective-permute-done.12
  98.6 3.8 %collective-permute-done.11 = f32[2,128]{1,0:T(2,128)S(1)} collective-permute-done((f32[2,128]{1,0:T(2,128)S(1)}, f32[2,128]{1,0:T(2,128)S(1)}, u32[]{:S(2)}, u32[]{:S(2)}) %collective-permute-start.11) | collective-permute-done | bytes 1056 | tf_op jit(solution)/shard_map/ppermute | solution.py:436
  102.4 0.0 collective-permute-done.10
  102.4 0.6 collective-permute-start.15
  103.0 2.4 %collective-permute-start.14 = (f32[2,128]{1,0:T(2,128)S(1)}, f32[2,128]{1,0:T(2,128)S(1)}, u32[]{:S(2)}, u32[]{:S(2)}) collective-permute-start(f32[2,128]{1,0:T(2,128)S(1)} %add_add_fusion), channel_id=1, source_target_pairs={{0,128},{64,192},{128,0},{192,64},{1,129},{65,193},{129,1},{193,65... | collective-permute-start | bytes 3080 | tf_op jit(solution)/shard_map/ppermute | solution.py:436
  105.4 0.6 collective-permute-start.13
  106.0 1.4 %shard_map.114 = bf16[128,16,128]{2,1,0:T(8,128)(2,1)} custom-call(bf16[8,272,128]{2,1,0:T(8,128)(2,1)S(1)} %all-to-all-done.1.in_ref), custom_call_target="tpu_custom_call" | custom-call | flops 278528 | bytes 1114112 | tf_op jit(solution)/shard_map/pallas_call | solution.py:25
  107.3 3.4 %all-to-all-done.2.in_ref = bf16[8,2,128,128]{3,2,1,0:T(8,128)(2,1)S(1)} async-done(((bf16[8,2,128,128]{3,2,1,0:T(8,128)(2,1)}), bf16[8,2,128,128]{3,2,1,0:T(8,128)(2,1)S(1)}, u32[]{:S(2)}, u32[]{:S(2)}) %all-to-all-start.2) | async-done | bytes 524320 | tf_op jit(solution)/shard_map/all_to_all | solution.py:460
  110.7 1.1 shard_map.117
  111.8 0.0 collective-permute-done.15
  111.8 0.0 collective-permute-done.14
  111.8 0.0 collective-permute-done.13
  111.8 0.5 slice_bitcast_fusion
  (7 shorter events, 0.1 us)
Async XLA Ops:
  2.0 10.8 %collective-permute-start = (bf16[2,128,128]{2,1,0:T(8,128)(2,1)S(1)}, bf16[2,128,128]{2,1,0:T(8,128)(2,1)S(1)}, u32[]{:S(2)}, u32[]{:S(2)}) collective-permute-start(bf16[2,128,128]{2,1,0:T(8,128)(2,1)S(1)} %get-tuple-element.37), channel_id=1, source_target_pairs={{0,2},{2,4},{4,6},{6,8},{8,10},{10,12},{12,14},{14,0},{1,3},{3,5},... | collective-permute-start | bytes 196616 | tf_op jit(solution)/shard_map/ppermute | solution.py:465
  4.0 13.2 %collective-permute-start.1 = (bf16[2,128,128]{2,1,0:T(8,128)(2,1)S(1)}, bf16[2,128,128]{2,1,0:T(8,128)(2,1)S(1)}, u32[]{:S(2)}, u32[]{:S(2)}) collective-permute-start(bf16[2,128,128]{2,1,0:T(8,128)(2,1)S(1)} %get-tuple-element.38), channel_id=1, source_target_pairs={{0,14},{2,0},{4,2},{6,4},{8,6},{10,8},{12,10},{14,12},{1,15},{3,1}... | collective-permute-start | bytes 196616 | tf_op jit(solution)/shard_map/ppermute | solution.py:465
  8.0 17.2 %collective-permute-start.2 = (bf16[2,128,128]{2,1,0:T(8,128)(2,1)S(1)}, bf16[2,128,128]{2,1,0:T(8,128)(2,1)S(1)}, u32[]{:S(2)}, u32[]{:S(2)}) collective-permute-start(bf16[2,128,128]{2,1,0:T(8,128)(2,1)S(1)} %get-tuple-element.39), channel_id=1, source_target_pairs={{0,4},{2,6},{4,8},{6,10},{8,12},{10,14},{12,0},{14,2},{1,5},{3,7},... | collective-permute-start | bytes 196616 | tf_op jit(solution)/shard_map/ppermute | solution.py:465
  8.0 17.2 %collective-permute-start.3 = (bf16[2,128,128]{2,1,0:T(8,128)(2,1)S(1)}, bf16[2,128,128]{2,1,0:T(8,128)(2,1)S(1)}, u32[]{:S(2)}, u32[]{:S(2)}) collective-permute-start(bf16[2,128,128]{2,1,0:T(8,128)(2,1)S(1)} %get-tuple-element.40), channel_id=1, source_target_pairs={{0,12},{2,14},{4,0},{6,2},{8,4},{10,6},{12,8},{14,10},{1,13},{3,15... | collective-permute-start | bytes 196616 | tf_op jit(solution)/shard_map/ppermute | solution.py:465
  12.1 13.1 %collective-permute-start.4 = (bf16[2,128,128]{2,1,0:T(8,128)(2,1)S(1)}, bf16[2,128,128]{2,1,0:T(8,128)(2,1)S(1)}, u32[]{:S(2)}, u32[]{:S(2)}) collective-permute-start(bf16[2,128,128]{2,1,0:T(8,128)(2,1)S(1)} %get-tuple-element.41), channel_id=1, source_target_pairs={{0,6},{2,8},{4,10},{6,12},{8,14},{10,0},{12,2},{14,4},{1,7},{3,9},... | collective-permute-start | bytes 196616 | tf_op jit(solution)/shard_map/ppermute | solution.py:465
  12.7 12.5 %collective-permute-start.5 = (bf16[2,128,128]{2,1,0:T(8,128)(2,1)S(1)}, bf16[2,128,128]{2,1,0:T(8,128)(2,1)S(1)}, u32[]{:S(2)}, u32[]{:S(2)}) collective-permute-start(bf16[2,128,128]{2,1,0:T(8,128)(2,1)S(1)} %get-tuple-element.42), channel_id=1, source_target_pairs={{0,10},{2,12},{4,14},{6,0},{8,2},{10,4},{12,6},{14,8},{1,11},{3,13... | collective-permute-start | bytes 196616 | tf_op jit(solution)/shard_map/ppermute | solution.py:465
  17.2 8.2 %collective-permute-start.6 = (bf16[2,128,128]{2,1,0:T(8,128)(2,1)S(1)}, bf16[2,128,128]{2,1,0:T(8,128)(2,1)S(1)}, u32[]{:S(2)}, u32[]{:S(2)}) collective-permute-start(bf16[2,128,128]{2,1,0:T(8,128)(2,1)S(1)} %get-tuple-element.43), channel_id=1, source_target_pairs={{0,8},{2,10},{4,12},{6,14},{8,0},{10,2},{12,4},{14,6},{1,9},{3,11}... | collective-permute-start | bytes 196616 | tf_op jit(solution)/shard_map/ppermute | solution.py:465
  21.6 0.7 copy-start.1
  21.6 0.7 copy-start.2
  25.3 32.1 %all-to-all-start = ((bf16[8,4,128,128]{3,2,1,0:T(8,128)(2,1)}), bf16[8,4,128,128]{3,2,1,0:T(8,128)(2,1)S(1)}, u32[]{:S(2)}, u32[]{:S(2)}) async-start(bf16[8,4,128,128]{3,2,1,0:T(8,128)(2,1)} %get-tuple-element.45), calls=%async_computation | async-start | bytes 2097152 | tf_op jit(solution)/shard_map/all_to_all | solution.py:460
  31.5 3.7 %copy-start = (s32[16384]{0:T(1024)S(1)}, s32[16384]{0:T(1024)}, u32[]{:S(2)}) copy-start(s32[16384]{0:T(1024)} %param.12) | copy-start | bytes 196612
  31.6 14.6 %collective-permute-start.7 = (bf16[8,2,128,128]{3,2,1,0:T(8,128)(2,1)S(1)}, bf16[8,2,128,128]{3,2,1,0:T(8,128)(2,1)S(1)}, u32[]{:S(2)}, u32[]{:S(2)}) collective-permute-start(bf16[8,2,128,128]{3,2,1,0:T(8,128)(2,1)S(1)} %shard_map.112.own_ref), channel_id=1, source_target_pairs={{0,16},{16,32},{32,48},{48,64},{64,80},{80,96},{96,112},{112,128},... | collective-permute-start | bytes 1572872 | tf_op jit(solution)/shard_map/ppermute | solution.py:483
  67.8 18.8 %all-to-all-start.1 = ((bf16[8,272,128]{2,1,0:T(8,128)(2,1)}), bf16[8,272,128]{2,1,0:T(8,128)(2,1)S(1)}, u32[]{:S(2)}, u32[]{:S(2)}) async-start(bf16[8,272,128]{2,1,0:T(8,128)(2,1)} %get-tuple-element.55), calls=%async_computation.1 | async-start | bytes 1114112 | tf_op jit(solution)/shard_map/all_to_all | solution.py:460
  71.3 16.5 %collective-permute-start.8 = (bf16[8,2,128,128]{3,2,1,0:T(8,128)(2,1)}, bf16[8,2,128,128]{3,2,1,0:T(8,128)(2,1)S(1)}, u32[]{:S(2)}, u32[]{:S(2)}) collective-permute-start(bf16[8,2,128,128]{3,2,1,0:T(8,128)(2,1)} %get-tuple-element.58), channel_id=1, source_target_pairs={{16,0},{32,16},{48,32},{64,48},{80,64},{96,80},{112,96},{128,112},... | collective-permute-start | bytes 1572872 | tf_op jit(solution)/shard_map/ppermute | solution.py:486
  86.6 1.2 %collective-permute-start.9 = (f32[2,128]{1,0:T(2,128)S(1)}, f32[2,128]{1,0:T(2,128)S(1)}, u32[]{:S(2)}, u32[]{:S(2)}) collective-permute-start(f32[2,128]{1,0:T(2,128)S(1)} %shard_map.115), channel_id=1, source_target_pairs={{0,1},{1,0},{2,3},{3,2},{4,5},{5,4},{6,7},{7,6},{8,9},{9,8},{10,11... | collective-permute-start | bytes 3080 | tf_op jit(solution)/shard_map/ppermute | solution.py:436
  89.2 21.5 %all-to-all-start.2 = ((bf16[8,2,128,128]{3,2,1,0:T(8,128)(2,1)}), bf16[8,2,128,128]{3,2,1,0:T(8,128)(2,1)S(1)}, u32[]{:S(2)}, u32[]{:S(2)}) async-start(bf16[8,2,128,128]{3,2,1,0:T(8,128)(2,1)} %shard_map.116), calls=%async_computation.2 | async-start | bytes 1048576 | tf_op jit(solution)/shard_map/all_to_all | solution.py:460
  92.8 5.8 %collective-permute-start.12 = (f32[2,128]{1,0:T(2,128)S(1)}, f32[2,128]{1,0:T(2,128)S(1)}, u32[]{:S(2)}, u32[]{:S(2)}) collective-permute-start(f32[2,128]{1,0:T(2,128)S(1)} %add.31), channel_id=1, source_target_pairs={{0,48},{16,0},{32,16},{48,32},{1,49},{17,1},{33,17},{49,33},{2,50}... | collective-permute-start | bytes 3080 | tf_op jit(solution)/shard_map/ppermute | solution.py:436
  97.3 5.1 %collective-permute-start.11 = (f32[2,128]{1,0:T(2,128)S(1)}, f32[2,128]{1,0:T(2,128)S(1)}, u32[]{:S(2)}, u32[]{:S(2)}) collective-permute-start(f32[2,128]{1,0:T(2,128)S(1)} %add.31), channel_id=1, source_target_pairs={{0,32},{16,48},{32,0},{48,16},{1,33},{17,49},{33,1},{49,17},{2,34}... | collective-permute-start | bytes 3080 | tf_op jit(solution)/shard_map/ppermute | solution.py:436
  97.3 5.1 %collective-permute-start.10 = (f32[2,128]{1,0:T(2,128)S(1)}, f32[2,128]{1,0:T(2,128)S(1)}, u32[]{:S(2)}, u32[]{:S(2)}) collective-permute-start(f32[2,128]{1,0:T(2,128)S(1)} %add.31), channel_id=1, source_target_pairs={{0,16},{16,32},{32,48},{48,0},{1,17},{17,33},{33,49},{49,1},{2,18}... | collective-permute-start | bytes 3080 | tf_op jit(solution)/shard_map/ppermute | solution.py:436
  102.4 9.4 %collective-permute-start.15 = (f32[2,128]{1,0:T(2,128)S(1)}, f32[2,128]{1,0:T(2,128)S(1)}, u32[]{:S(2)}, u32[]{:S(2)}) collective-permute-start(f32[2,128]{1,0:T(2,128)S(1)} %add_add_fusion), channel_id=1, source_target_pairs={{0,192},{64,0},{128,64},{192,128},{1,193},{65,1},{129,65},{193,129... | collective-permute-start | bytes 3080 | tf_op jit(solution)/shard_map/ppermute | solution.py:436
  103.0 8.8 %collective-permute-start.14 = (f32[2,128]{1,0:T(2,128)S(1)}, f32[2,128]{1,0:T(2,128)S(1)}, u32[]{:S(2)}, u32[]{:S(2)}) collective-permute-start(f32[2,128]{1,0:T(2,128)S(1)} %add_add_fusion), channel_id=1, source_target_pairs={{0,128},{64,192},{128,0},{192,64},{1,129},{65,193},{129,1},{193,65... | collective-permute-start | bytes 3080 | tf_op jit(solution)/shard_map/ppermute | solution.py:436
  105.4 6.4 %collective-permute-start.13 = (f32[2,128]{1,0:T(2,128)S(1)}, f32[2,128]{1,0:T(2,128)S(1)}, u32[]{:S(2)}, u32[]{:S(2)}) collective-permute-start(f32[2,128]{1,0:T(2,128)S(1)} %add_add_fusion), channel_id=1, source_target_pairs={{0,64},{64,128},{128,192},{192,0},{1,65},{65,129},{129,193},{193,1... | collective-permute-start | bytes 3080 | tf_op jit(solution)/shard_map/ppermute | solution.py:436

commit v5 on v4

--- a/solution.py
+++ b/solution.py
@@ -14,7 +14,7 @@
 F32 = jnp.float32
 BF16 = jnp.bfloat16
 TAIL_ROWS = 16
-STEP_ORDER = (1, 7, 2, 6, 3, 5, 4)
+STEP_ORDER = (1, 7, 2, 6, 4, 3, 5)
 VMEM_BYTES = 8 << 20
 SMEM = pl.BlockSpec(memory_space=pltpu.SMEM)
 HBM = pl.BlockSpec(memory_space=pltpu.HBM)

time: 114 us -> 118 us (1.035)
  waiting for transfers between devices: 41.4 us -> 46.6 us
    all_to_all x3, waiting for transfers between devices: 25.1 us -> 28.4 us  [exchange(): return lax.all_to_all(value, 'z', 0, 0, tiled=True)]
    ppermute x1, waiting for transfers between devices: 10.9 us -> 12.8 us  [per_device(): prev = lax.ppermute(own, ring_axes, forward)]
where the time goes in v5:
time: 118 us; the launch traced here: 117 us
  starting transfers between devices  50.1 us (42%)
  waiting for transfers between devices  46.6 us (39%)
  Pallas kernels  18.3 us (16%)
  local copies, waits for them, and re-layouts  1.2 us (1%)
    all_to_all x3, waiting for transfers between devices, exchange(): return lax.all_to_all(value, 'z', 0, 0, tiled=True)  28.4 us
    ppermute x7, starting transfers between devices, exchange_apart(): lax.ppermute(pieces[step], 'z', [(i, (i + step) % ring_size) for i in ran...  19.7 us
    pallas_call x5, Pallas kernels, call(): pl.pallas_call(body, out_shape=out_shape, in_specs=[VMEM] * len(args), ou...  14.1 us
    ppermute x1, waiting for transfers between devices, per_device(): prev = lax.ppermute(own, ring_axes, forward)  12.8 us
    all_to_all x3, starting transfers between devices, exchange(): return lax.all_to_all(value, 'z', 0, 0, tiled=True)  12.7 us
    ppermute x7, starting transfers between devices, shifted_terms(): lax.ppermute(value, axis, [(i, (i + step) % count) for i in range(count)])  9.21 us
    ppermute x7, waiting for transfers between devices, shifted_terms(): lax.ppermute(value, axis, [(i, (i + step) % count) for i in range(count)])  5.25 us
    ppermute x1, starting transfers between devices, per_device(): got_back = lax.ppermute(back, ring_axes, backward)  4.9 us
  transfers between devices with their start and end apart: 19, of which 8 were waited for; matrix products, arithmetic and copies ran while one was open for 0% of the time, Pallas kernels for 5%

profile of v5, /device:TPU:2, one launch (start us, length us, event | category | flops | bytes accessed | tf_op | source)
XLA Modules:
  0.0 117.0 jit_solution(9656937098039964738)
XLA Ops:
  0.6 1.3 %shard_map.110 = (bf16[2,128,128]{2,1,0:T(8,128)(2,1)S(1)}, bf16[2,128,128]{2,1,0:T(8,128)(2,1)S(1)}, bf16[2,128,128]{2,1,0:T(8,128)(2,1)S(1)}, bf16[2,128,128]{...) custom-call(s32[1]{0:T(128)} %bitcast.place_ref, ...), custom_call_target="tpu_custom_call" | custom-call | flops 262144 | bytes 1048576 | tf_op jit(solution)/shard_map/pallas_call | solution.py:104
  2.0 2.0 %collective-permute-start = (bf16[2,128,128]{2,1,0:T(8,128)(2,1)S(1)}, bf16[2,128,128]{2,1,0:T(8,128)(2,1)S(1)}, u32[]{:S(2)}, u32[]{:S(2)}) collective-permute-start(bf16[2,128,128]{2,1,0:T(8,128)(2,1)S(1)} %get-tuple-element.37), channel_id=1, source_target_pairs={{0,2},{2,4},{4,6},{6,8},{8,10},{10,12},{12,14},{14,0},{1,3},{3,5},... | collective-permute-start | bytes 196616 | tf_op jit(solution)/shard_map/ppermute | solution.py:465
  4.0 4.0 %collective-permute-start.1 = (bf16[2,128,128]{2,1,0:T(8,128)(2,1)S(1)}, bf16[2,128,128]{2,1,0:T(8,128)(2,1)S(1)}, u32[]{:S(2)}, u32[]{:S(2)}) collective-permute-start(bf16[2,128,128]{2,1,0:T(8,128)(2,1)S(1)} %get-tuple-element.38), channel_id=1, source_target_pairs={{0,14},{2,0},{4,2},{6,4},{8,6},{10,8},{12,10},{14,12},{1,15},{3,1}... | collective-permute-start | bytes 196616 | tf_op jit(solution)/shard_map/ppermute | solution.py:465
  8.0 0.0 collective-permute-start.2
  8.0 4.1 %collective-permute-start.3 = (bf16[2,128,128]{2,1,0:T(8,128)(2,1)S(1)}, bf16[2,128,128]{2,1,0:T(8,128)(2,1)S(1)}, u32[]{:S(2)}, u32[]{:S(2)}) collective-permute-start(bf16[2,128,128]{2,1,0:T(8,128)(2,1)S(1)} %get-tuple-element.40), channel_id=1, source_target_pairs={{0,12},{2,14},{4,0},{6,2},{8,4},{10,6},{12,8},{14,10},{1,13},{3,15... | collective-permute-start | bytes 196616 | tf_op jit(solution)/shard_map/ppermute | solution.py:465
  12.1 4.5 %collective-permute-start.4 = (bf16[2,128,128]{2,1,0:T(8,128)(2,1)S(1)}, bf16[2,128,128]{2,1,0:T(8,128)(2,1)S(1)}, u32[]{:S(2)}, u32[]{:S(2)}) collective-permute-start(bf16[2,128,128]{2,1,0:T(8,128)(2,1)S(1)} %get-tuple-element.41), channel_id=1, source_target_pairs={{0,8},{2,10},{4,12},{6,14},{8,0},{10,2},{12,4},{14,6},{1,9},{3,11}... | collective-permute-start | bytes 196616 | tf_op jit(solution)/shard_map/ppermute | solution.py:465
  16.6 0.0 collective-permute-done.refs_1_
  16.6 0.0 collective-permute-start.5
  16.6 0.0 collective-permute-done.1.refs_2_
  16.6 5.0 %collective-permute-start.6 = (bf16[2,128,128]{2,1,0:T(8,128)(2,1)S(1)}, bf16[2,128,128]{2,1,0:T(8,128)(2,1)S(1)}, u32[]{:S(2)}, u32[]{:S(2)}) collective-permute-start(bf16[2,128,128]{2,1,0:T(8,128)(2,1)S(1)} %get-tuple-element.43), channel_id=1, source_target_pairs={{0,10},{2,12},{4,14},{6,0},{8,2},{10,4},{12,6},{14,8},{1,11},{3,13... | collective-permute-start | bytes 196616 | tf_op jit(solution)/shard_map/ppermute | solution.py:465
  21.6 0.0 copy-start.1
  21.6 0.0 copy-start.2
  21.6 0.7 copy-done.1
  22.3 0.0 copy-done.2
  22.3 2.8 %shard_map.111 = (bf16[8,4,128,128]{3,2,1,0:T(8,128)(2,1)}, f32[2,128]{1,0:T(2,128)S(1)}) custom-call(bf16[128,16,128]{2,1,0:T(8,128)(2,1)} %refs_0_.1, bf16[128,16,128]{2,1,0:T(8,128)(2,1)} %refs_1_.1, f32[2,128]{1,0:T(2,128)S(1)} %pad_maximum_fusion.refs_2_), custom_call_target="tpu_custom_call" | custom-call | flops 524288 | bytes 2097152 | tf_op jit(solution)/shard_map/pallas_call | solution.py:68
  25.1 0.0 collective-permute-done.2.refs_3_
  25.2 0.0 collective-permute-done.3.refs_4_
  25.2 0.0 collective-permute-done.4.refs_5_
  25.2 0.2 collective-permute-done.5.refs_6_
  25.3 0.0 collective-permute-done.6.refs_7_
  25.3 5.6 %all-to-all-start = ((bf16[8,4,128,128]{3,2,1,0:T(8,128)(2,1)}), bf16[8,4,128,128]{3,2,1,0:T(8,128)(2,1)S(1)}, u32[]{:S(2)}, u32[]{:S(2)}) async-start(bf16[8,4,128,128]{3,2,1,0:T(8,128)(2,1)} %get-tuple-element.45), calls=%async_computation | async-start | bytes 2097152 | tf_op jit(solution)/shard_map/all_to_all | solution.py:460
  30.9 0.0 copy-start
  31.0 3.7 %collective-permute-start.7 = (bf16[8,2,128,128]{3,2,1,0:T(8,128)(2,1)S(1)}, bf16[8,2,128,128]{3,2,1,0:T(8,128)(2,1)S(1)}, u32[]{:S(2)}, u32[]{:S(2)}) collective-permute-start(bf16[8,2,128,128]{3,2,1,0:T(8,128)(2,1)S(1)} %shard_map.112.own_ref), channel_id=1, source_target_pairs={{0,16},{16,32},{32,48},{48,64},{64,80},{80,96},{96,112},{112,128},... | collective-permute-start | bytes 1572872 | tf_op jit(solution)/shard_map/ppermute | solution.py:483
  34.7 0.0 copy-done
  34.7 12.8 %collective-permute-done.7.prev_ref = bf16[8,2,128,128]{3,2,1,0:T(8,128)(2,1)S(1)} collective-permute-done((bf16[8,2,128,128]{3,2,1,0:T(8,128)(2,1)S(1)}, bf16[8,2,128,128]{3,2,1,0:T(8,128)(2,1)S(1)}, u32[]{:S(2)}, u32[]{:S(2)}) %collective-permute-start.7) | collective-permute-done | bytes 524320 | tf_op jit(solution)/shard_map/ppermute | solution.py:483
  47.5 11.3 %all-to-all-done.qd_ref = bf16[8,4,128,128]{3,2,1,0:T(8,128)(2,1)S(1)} async-done(((bf16[8,4,128,128]{3,2,1,0:T(8,128)(2,1)}), bf16[8,4,128,128]{3,2,1,0:T(8,128)(2,1)S(1)}, u32[]{:S(2)}, u32[]{:S(2)}) %all-to-all-start) | async-done | bytes 1048608 | tf_op jit(solution)/shard_map/all_to_all | solution.py:460
  58.7 10.3 %shard_map.113 = (bf16[8,272,128]{2,1,0:T(8,128)(2,1)}, f32[8,128,128]{2,1,0:T(8,128)S(1)}, f32[8,128,128]{2,1,0:T(8,128)S(1)}, bf16[8,2,128,128]{3,2,1,0:T(8,128)(2,1)}) custom-call(bf16[8,4,128,128]{3,2,1,0:T(8,128)(2,1)S(1)} %all-to-all-done.qd_ref, bf16[8,2,128,128]{3,2,1,0:T(8,128)(2,1)S(1)} %shard_map.112.own_ref, ...), custom_call_target="tpu_custom_call" | custom-call | flops 3623878656 | bytes 8388608 | tf_op jit(solution)/shard_map/pallas_call | solution.py:25
  69.0 3.5 %all-to-all-start.1 = ((bf16[8,272,128]{2,1,0:T(8,128)(2,1)}), bf16[8,272,128]{2,1,0:T(8,128)(2,1)S(1)}, u32[]{:S(2)}, u32[]{:S(2)}) async-start(bf16[8,272,128]{2,1,0:T(8,128)(2,1)} %get-tuple-element.55), calls=%async_computation.1 | async-start | bytes 1114112 | tf_op jit(solution)/shard_map/all_to_all | solution.py:460
  72.6 4.9 %collective-permute-start.8 = (bf16[8,2,128,128]{3,2,1,0:T(8,128)(2,1)}, bf16[8,2,128,128]{3,2,1,0:T(8,128)(2,1)S(1)}, u32[]{:S(2)}, u32[]{:S(2)}) collective-permute-start(bf16[8,2,128,128]{3,2,1,0:T(8,128)(2,1)} %get-tuple-element.58), channel_id=1, source_target_pairs={{16,0},{32,16},{48,32},{64,48},{80,64},{96,80},{112,96},{128,112},... | collective-permute-start | bytes 1572872 | tf_op jit(solution)/shard_map/ppermute | solution.py:486
  77.5 13.7 %all-to-all-done.1.in_ref = bf16[8,272,128]{2,1,0:T(8,128)(2,1)S(1)} async-done(((bf16[8,272,128]{2,1,0:T(8,128)(2,1)}), bf16[8,272,128]{2,1,0:T(8,128)(2,1)S(1)}, u32[]{:S(2)}, u32[]{:S(2)}) %all-to-all-start.1) | async-done | bytes 557088 | tf_op jit(solution)/shard_map/all_to_all | solution.py:460
  91.2 0.1 collective-permute-start.9
  91.3 1.1 collective-permute-done.9
  92.5 0.0 collective-permute-done.8.back_ref
  92.5 1.4 %shard_map.116 = bf16[8,2,128,128]{3,2,1,0:T(8,128)(2,1)} custom-call(bf16[8,2,128,128]{3,2,1,0:T(8,128)(2,1)S(1)} %shard_map.112.own_ref, f32[8,128,128]{2,1,0:T(8,128)S(1)} %get-tuple-element.56.dk_ref, f32[8,128,128]{2,1,0:T(8,128)S(1)} %get-tuple-element.57.dv_ref, bf16[8,2,128,128]{3,2,1,0:T(8,128)(2,1)S(1)} %collective-permute-done.8.back_ref, ...), custom_call_target="tpu_custom_call" | custom-call | flops 2621440 | bytes 2097152 | tf_op jit(solution)/shard_map/pallas_call | solution.py:25
  93.8 3.5 %all-to-all-start.2 = ((bf16[8,2,128,128]{3,2,1,0:T(8,128)(2,1)}), bf16[8,2,128,128]{3,2,1,0:T(8,128)(2,1)S(1)}, u32[]{:S(2)}, u32[]{:S(2)}) async-start(bf16[8,2,128,128]{3,2,1,0:T(8,128)(2,1)} %shard_map.116), calls=%async_computation.2 | async-start | bytes 1048576 | tf_op jit(solution)/shard_map/all_to_all | solution.py:460
  97.4 4.5 %collective-permute-start.12 = (f32[2,128]{1,0:T(2,128)S(1)}, f32[2,128]{1,0:T(2,128)S(1)}, u32[]{:S(2)}, u32[]{:S(2)}) collective-permute-start(f32[2,128]{1,0:T(2,128)S(1)} %add.31), channel_id=1, source_target_pairs={{0,48},{16,0},{32,16},{48,32},{1,49},{17,1},{33,17},{49,33},{2,50}... | collective-permute-start | bytes 3080 | tf_op jit(solution)/shard_map/ppermute | solution.py:436
  101.9 0.0 collective-permute-start.11
  101.9 1.0 collective-permute-start.10
  102.8 0.3 collective-permute-done.12
  103.2 3.8 %collective-permute-done.11 = f32[2,128]{1,0:T(2,128)S(1)} collective-permute-done((f32[2,128]{1,0:T(2,128)S(1)}, f32[2,128]{1,0:T(2,128)S(1)}, u32[]{:S(2)}, u32[]{:S(2)}) %collective-permute-start.11) | collective-permute-done | bytes 1056 | tf_op jit(solution)/shard_map/ppermute | solution.py:436
  107.0 0.0 collective-permute-done.10
  107.0 0.6 collective-permute-start.15
  107.6 2.4 %collective-permute-start.14 = (f32[2,128]{1,0:T(2,128)S(1)}, f32[2,128]{1,0:T(2,128)S(1)}, u32[]{:S(2)}, u32[]{:S(2)}) collective-permute-start(f32[2,128]{1,0:T(2,128)S(1)} %add_add_fusion), channel_id=1, source_target_pairs={{0,128},{64,192},{128,0},{192,64},{1,129},{65,193},{129,1},{193,65... | collective-permute-start | bytes 3080 | tf_op jit(solution)/shard_map/ppermute | solution.py:436
  110.0 0.6 collective-permute-start.13
  110.6 1.4 %shard_map.114 = bf16[128,16,128]{2,1,0:T(8,128)(2,1)} custom-call(bf16[8,272,128]{2,1,0:T(8,128)(2,1)S(1)} %all-to-all-done.1.in_ref), custom_call_target="tpu_custom_call" | custom-call | flops 278528 | bytes 1114112 | tf_op jit(solution)/shard_map/pallas_call | solution.py:25
  112.0 3.4 %all-to-all-done.2.in_ref = bf16[8,2,128,128]{3,2,1,0:T(8,128)(2,1)S(1)} async-done(((bf16[8,2,128,128]{3,2,1,0:T(8,128)(2,1)}), bf16[8,2,128,128]{3,2,1,0:T(8,128)(2,1)S(1)}, u32[]{:S(2)}, u32[]{:S(2)}) %all-to-all-start.2) | async-done | bytes 524320 | tf_op jit(solution)/shard_map/all_to_all | solution.py:460
  115.4 1.1 shard_map.117
  116.5 0.0 collective-permute-done.15
  116.5 0.0 collective-permute-done.14
  116.5 0.0 collective-permute-done.13
  116.5 0.5 slice_bitcast_fusion
  (7 shorter events, 0.1 us)
Async XLA Ops:
  2.0 14.6 %collective-permute-start = (bf16[2,128,128]{2,1,0:T(8,128)(2,1)S(1)}, bf16[2,128,128]{2,1,0:T(8,128)(2,1)S(1)}, u32[]{:S(2)}, u32[]{:S(2)}) collective-permute-start(bf16[2,128,128]{2,1,0:T(8,128)(2,1)S(1)} %get-tuple-element.37), channel_id=1, source_target_pairs={{0,2},{2,4},{4,6},{6,8},{8,10},{10,12},{12,14},{14,0},{1,3},{3,5},... | collective-permute-start | bytes 196616 | tf_op jit(solution)/shard_map/ppermute | solution.py:465
  4.0 12.7 %collective-permute-start.1 = (bf16[2,128,128]{2,1,0:T(8,128)(2,1)S(1)}, bf16[2,128,128]{2,1,0:T(8,128)(2,1)S(1)}, u32[]{:S(2)}, u32[]{:S(2)}) collective-permute-start(bf16[2,128,128]{2,1,0:T(8,128)(2,1)S(1)} %get-tuple-element.38), channel_id=1, source_target_pairs={{0,14},{2,0},{4,2},{6,4},{8,6},{10,8},{12,10},{14,12},{1,15},{3,1}... | collective-permute-start | bytes 196616 | tf_op jit(solution)/shard_map/ppermute | solution.py:465
  8.0 17.2 %collective-permute-start.2 = (bf16[2,128,128]{2,1,0:T(8,128)(2,1)S(1)}, bf16[2,128,128]{2,1,0:T(8,128)(2,1)S(1)}, u32[]{:S(2)}, u32[]{:S(2)}) collective-permute-start(bf16[2,128,128]{2,1,0:T(8,128)(2,1)S(1)} %get-tuple-element.39), channel_id=1, source_target_pairs={{0,4},{2,6},{4,8},{6,10},{8,12},{10,14},{12,0},{14,2},{1,5},{3,7},... | collective-permute-start | bytes 196616 | tf_op jit(solution)/shard_map/ppermute | solution.py:465
  8.0 17.2 %collective-permute-start.3 = (bf16[2,128,128]{2,1,0:T(8,128)(2,1)S(1)}, bf16[2,128,128]{2,1,0:T(8,128)(2,1)S(1)}, u32[]{:S(2)}, u32[]{:S(2)}) collective-permute-start(bf16[2,128,128]{2,1,0:T(8,128)(2,1)S(1)} %get-tuple-element.40), channel_id=1, source_target_pairs={{0,12},{2,14},{4,0},{6,2},{8,4},{10,6},{12,8},{14,10},{1,13},{3,15... | collective-permute-start | bytes 196616 | tf_op jit(solution)/shard_map/ppermute | solution.py:465
  12.1 13.1 %collective-permute-start.4 = (bf16[2,128,128]{2,1,0:T(8,128)(2,1)S(1)}, bf16[2,128,128]{2,1,0:T(8,128)(2,1)S(1)}, u32[]{:S(2)}, u32[]{:S(2)}) collective-permute-start(bf16[2,128,128]{2,1,0:T(8,128)(2,1)S(1)} %get-tuple-element.41), channel_id=1, source_target_pairs={{0,8},{2,10},{4,12},{6,14},{8,0},{10,2},{12,4},{14,6},{1,9},{3,11}... | collective-permute-start | bytes 196616 | tf_op jit(solution)/shard_map/ppermute | solution.py:465
  16.6 8.7 %collective-permute-start.5 = (bf16[2,128,128]{2,1,0:T(8,128)(2,1)S(1)}, bf16[2,128,128]{2,1,0:T(8,128)(2,1)S(1)}, u32[]{:S(2)}, u32[]{:S(2)}) collective-permute-start(bf16[2,128,128]{2,1,0:T(8,128)(2,1)S(1)} %get-tuple-element.42), channel_id=1, source_target_pairs={{0,6},{2,8},{4,10},{6,12},{8,14},{10,0},{12,2},{14,4},{1,7},{3,9},... | collective-permute-start | bytes 196616 | tf_op jit(solution)/shard_map/ppermute | solution.py:465
  16.6 8.7 %collective-permute-start.6 = (bf16[2,128,128]{2,1,0:T(8,128)(2,1)S(1)}, bf16[2,128,128]{2,1,0:T(8,128)(2,1)S(1)}, u32[]{:S(2)}, u32[]{:S(2)}) collective-permute-start(bf16[2,128,128]{2,1,0:T(8,128)(2,1)S(1)} %get-tuple-element.43), channel_id=1, source_target_pairs={{0,10},{2,12},{4,14},{6,0},{8,2},{10,4},{12,6},{14,8},{1,11},{3,13... | collective-permute-start | bytes 196616 | tf_op jit(solution)/shard_map/ppermute | solution.py:465
  21.6 0.7 copy-start.1
  21.6 0.7 copy-start.2
  25.3 33.4 %all-to-all-start = ((bf16[8,4,128,128]{3,2,1,0:T(8,128)(2,1)}), bf16[8,4,128,128]{3,2,1,0:T(8,128)(2,1)S(1)}, u32[]{:S(2)}, u32[]{:S(2)}) async-start(bf16[8,4,128,128]{3,2,1,0:T(8,128)(2,1)} %get-tuple-element.45), calls=%async_computation | async-start | bytes 2097152 | tf_op jit(solution)/shard_map/all_to_all | solution.py:460
  30.9 3.7 %copy-start = (s32[16384]{0:T(1024)S(1)}, s32[16384]{0:T(1024)}, u32[]{:S(2)}) copy-start(s32[16384]{0:T(1024)} %param.12) | copy-start | bytes 196612
  31.0 16.5 %collective-permute-start.7 = (bf16[8,2,128,128]{3,2,1,0:T(8,128)(2,1)S(1)}, bf16[8,2,128,128]{3,2,1,0:T(8,128)(2,1)S(1)}, u32[]{:S(2)}, u32[]{:S(2)}) collective-permute-start(bf16[8,2,128,128]{3,2,1,0:T(8,128)(2,1)S(1)} %shard_map.112.own_ref), channel_id=1, source_target_pairs={{0,16},{16,32},{32,48},{48,64},{64,80},{80,96},{96,112},{112,128},... | collective-permute-start | bytes 1572872 | tf_op jit(solution)/shard_map/ppermute | solution.py:483
  69.0 22.2 %all-to-all-start.1 = ((bf16[8,272,128]{2,1,0:T(8,128)(2,1)}), bf16[8,272,128]{2,1,0:T(8,128)(2,1)S(1)}, u32[]{:S(2)}, u32[]{:S(2)}) async-start(bf16[8,272,128]{2,1,0:T(8,128)(2,1)} %get-tuple-element.55), calls=%async_computation.1 | async-start | bytes 1114112 | tf_op jit(solution)/shard_map/all_to_all | solution.py:460
  72.6 19.9 %collective-permute-start.8 = (bf16[8,2,128,128]{3,2,1,0:T(8,128)(2,1)}, bf16[8,2,128,128]{3,2,1,0:T(8,128)(2,1)S(1)}, u32[]{:S(2)}, u32[]{:S(2)}) collective-permute-start(bf16[8,2,128,128]{3,2,1,0:T(8,128)(2,1)} %get-tuple-element.58), channel_id=1, source_target_pairs={{16,0},{32,16},{48,32},{64,48},{80,64},{96,80},{112,96},{128,112},... | collective-permute-start | bytes 1572872 | tf_op jit(solution)/shard_map/ppermute | solution.py:486
  91.2 1.2 %collective-permute-start.9 = (f32[2,128]{1,0:T(2,128)S(1)}, f32[2,128]{1,0:T(2,128)S(1)}, u32[]{:S(2)}, u32[]{:S(2)}) collective-permute-start(f32[2,128]{1,0:T(2,128)S(1)} %shard_map.115), channel_id=1, source_target_pairs={{0,1},{1,0},{2,3},{3,2},{4,5},{5,4},{6,7},{7,6},{8,9},{9,8},{10,11... | collective-permute-start | bytes 3080 | tf_op jit(solution)/shard_map/ppermute | solution.py:436
  93.8 21.6 %all-to-all-start.2 = ((bf16[8,2,128,128]{3,2,1,0:T(8,128)(2,1)}), bf16[8,2,128,128]{3,2,1,0:T(8,128)(2,1)S(1)}, u32[]{:S(2)}, u32[]{:S(2)}) async-start(bf16[8,2,128,128]{3,2,1,0:T(8,128)(2,1)} %shard_map.116), calls=%async_computation.2 | async-start | bytes 1048576 | tf_op jit(solution)/shard_map/all_to_all | solution.py:460
  97.4 5.8 %collective-permute-start.12 = (f32[2,128]{1,0:T(2,128)S(1)}, f32[2,128]{1,0:T(2,128)S(1)}, u32[]{:S(2)}, u32[]{:S(2)}) collective-permute-start(f32[2,128]{1,0:T(2,128)S(1)} %add.31), channel_id=1, source_target_pairs={{0,48},{16,0},{32,16},{48,32},{1,49},{17,1},{33,17},{49,33},{2,50}... | collective-permute-start | bytes 3080 | tf_op jit(solution)/shard_map/ppermute | solution.py:436
  101.9 5.1 %collective-permute-start.11 = (f32[2,128]{1,0:T(2,128)S(1)}, f32[2,128]{1,0:T(2,128)S(1)}, u32[]{:S(2)}, u32[]{:S(2)}) collective-permute-start(f32[2,128]{1,0:T(2,128)S(1)} %add.31), channel_id=1, source_target_pairs={{0,32},{16,48},{32,0},{48,16},{1,33},{17,49},{33,1},{49,17},{2,34}... | collective-permute-start | bytes 3080 | tf_op jit(solution)/shard_map/ppermute | solution.py:436
  101.9 5.1 %collective-permute-start.10 = (f32[2,128]{1,0:T(2,128)S(1)}, f32[2,128]{1,0:T(2,128)S(1)}, u32[]{:S(2)}, u32[]{:S(2)}) collective-permute-start(f32[2,128]{1,0:T(2,128)S(1)} %add.31), channel_id=1, source_target_pairs={{0,16},{16,32},{32,48},{48,0},{1,17},{17,33},{33,49},{49,1},{2,18}... | collective-permute-start | bytes 3080 | tf_op jit(solution)/shard_map/ppermute | solution.py:436
  107.0 9.5 %collective-permute-start.15 = (f32[2,128]{1,0:T(2,128)S(1)}, f32[2,128]{1,0:T(2,128)S(1)}, u32[]{:S(2)}, u32[]{:S(2)}) collective-permute-start(f32[2,128]{1,0:T(2,128)S(1)} %add_add_fusion), channel_id=1, source_target_pairs={{0,192},{64,0},{128,64},{192,128},{1,193},{65,1},{129,65},{193,129... | collective-permute-start | bytes 3080 | tf_op jit(solution)/shard_map/ppermute | solution.py:436
  107.6 8.9 %collective-permute-start.14 = (f32[2,128]{1,0:T(2,128)S(1)}, f32[2,128]{1,0:T(2,128)S(1)}, u32[]{:S(2)}, u32[]{:S(2)}) collective-permute-start(f32[2,128]{1,0:T(2,128)S(1)} %add_add_fusion), channel_id=1, source_target_pairs={{0,128},{64,192},{128,0},{192,64},{1,129},{65,193},{129,1},{193,65... | collective-permute-start | bytes 3080 | tf_op jit(solution)/shard_map/ppermute | solution.py:436
  110.0 6.5 %collective-permute-start.13 = (f32[2,128]{1,0:T(2,128)S(1)}, f32[2,128]{1,0:T(2,128)S(1)}, u32[]{:S(2)}, u32[]{:S(2)}) collective-permute-start(f32[2,128]{1,0:T(2,128)S(1)} %add_add_fusion), channel_id=1, source_target_pairs={{0,64},{64,128},{128,192},{192,0},{1,65},{65,129},{129,193},{193,1... | collective-permute-start | bytes 3080 | tf_op jit(solution)/shard_map/ppermute | solution.py:436
